TPU v7x, 32 devices: a whole 2x2x4 slice. The times are simulated.
32 devices in a mesh: fsdp: 4 (over z), ctx: 4 (over y, x), tp: 2 (over core).
Axes of the slice: x: 2, y: 2, z: 4, core: 2. Of those that a mesh axis runs over, the one named last changes fastest.
Arguments:
- tokens: bfloat16 [4096, 1024], P(('fsdp', 'ctx')), may hold values from -6 to 6
- lengths: int32 [4, 4], P('fsdp'), may hold values from 1 to 959, as said below
- norm_gain: bfloat16 [1024], P('fsdp'), may hold values from 0.5 to 1.5
- qkv_weight: bfloat16 [3, 1024, 1024], P(None, 'fsdp', 'tp'), may hold values from -0.1875 to 0.1875
- beta_weight: bfloat16 [1024, 8], P('fsdp', 'tp'), may hold values from -0.1875 to 0.1875
- conv_weight: bfloat16 [3, 4, 8, 128], P(None, None, 'tp', 'fsdp'), may hold values from -3 to 3
- head_gain: bfloat16 [128], P('fsdp'), may hold values from 0.5 to 1.5
- out_weight: bfloat16 [1024, 1024], P('tp', 'fsdp'), may hold values from -0.1875 to 0.1875
- mlp_gain: bfloat16 [1024], P('fsdp'), may hold values from 0.5 to 1.5
- gate_up_weight: bfloat16 [2, 1024, 2816], P(None, 'fsdp', 'tp'), may hold values from -0.1875 to 0.1875
- down_weight: bfloat16 [2816, 1024], P('tp', 'fsdp'), may hold values from -0.15625 to 0.15625
- cotangent: bfloat16 [4096, 1024], P(('fsdp', 'ctx')), may hold values from -6 to 6
Outputs:
- layer_out: bfloat16 [4096, 1024], P(('fsdp', 'ctx'))
- input_grad: float32 [4096, 1024], P(('fsdp', 'ctx'))
- norm_gain_grad: float32 [1024], P('fsdp')
- qkv_grad: float32 [3, 1024, 1024], P(None, 'fsdp', 'tp')
- beta_grad: float32 [1024, 8], P('fsdp', 'tp')
- conv_grad: float32 [3, 4, 8, 128], P(None, None, 'tp', 'fsdp')
- head_gain_grad: float32 [128], P('fsdp')
- out_grad: float32 [1024, 1024], P('tp', 'fsdp')
- mlp_gain_grad: float32 [1024], P('fsdp')
- gate_up_grad: float32 [2, 1024, 2816], P(None, 'fsdp', 'tp')
- down_grad: float32 [2816, 1024], P('tp', 'fsdp')
- rms: float32 [5], replicated
Inputs may be any that keep to these rules, and one draw needn't show every extreme that they name: Row g lists the 4 sequence lengths of stream g in order; they sum to at most 1024, the remaining slots at the end are padding. The second sequence of each stream ends at slot 960, so it includes a slot of the first and of the last of its 4 blocks of 256 slots.
All inputs are finite; a program needn't handle non-finite values.
Results may differ from a plain program's by a relative error of at most 0.012.
The roundings to bfloat16 on the way count: a program that leaves them out, or rounds other values in their place, can miss the bound.
Values may be sent and summed in bfloat16 or wider, within the bound.
No kernel may reach another device: no remote copies, remote signals or barrier semaphores. Data moves between devices by JAX's collectives and lax.ppermute only.
A program may use at most 128 MiB of HBM per device.

v0:
```python
import functools

import jax
import jax.numpy as jnp
from jax import lax
from jax.experimental import pallas as pl
from jax.experimental.pallas import tpu as pltpu
from jax.sharding import PartitionSpec as P

HD = 128
CONV = 4
PAD = 8
EPS = 1e-06
F32 = jnp.float32
BF16 = jnp.bfloat16
NN = (((1,), (0,)), ((), ()))
NT = (((1,), (1,)), ((), ()))
TN = (((0,), (0,)), ((), ()))
SCALE = HD ** (-0.5)
COST = 3.0
US = {'delta_terms': 12, 'delta_outputs': 6.5, 'mlp': 12.2, 'mlp_grads': 6.5, 'middle_back': 9.6, 'delta_back': 22, 'input_back': 3.7, 'mixer_sum': 3.5, 'mixer_total': 2.3, 'gate_up_whole': 3.3, 'mixer_whole': 2.9}
GU_BLOCKS = 6
SMALL_ROWS = 24

ANY = pl.BlockSpec(memory_space=pl.ANY)
SMEM = pl.BlockSpec(memory_space=pltpu.SMEM)
VMEM = pl.BlockSpec(memory_space=pltpu.VMEM)


def parts_of(value, count):
    if value.dtype == BF16:
        return [value]
    pieces = []
    for left in range(count):
        piece = value.astype(BF16)
        pieces.append(piece)
        if left + 1 < count:
            value = value - piece.astype(F32)
    return pieces


def pdot(left, right, dims=NN):
    return lax.dot_general(left, right, dims, preferred_element_type=F32)


def mm_parts(lefts, rights, dims=NN):
    total = None
    for i, a in enumerate(lefts):
        for j, b in enumerate(rights):
            if i + j < max(len(lefts), len(rights)):
                term = pdot(a, b, dims)
                total = term if total is None else total + term
    return total


def mm(left, right, dims=NN, split=2):
    return mm_parts(parts_of(left, split), parts_of(right, split), dims)


def sigmoid(v):
    return 1.0 / (1.0 + jnp.exp(-v))


def iota(shape, axis):
    return lax.broadcasted_iota(jnp.int32, shape, axis)


def slots(meta, rows, axis, lengths):
    first = meta[0] * rows
    place = iota((rows, 1) if axis == 0 else (1, rows), axis) + first
    begins, end = jnp.zeros_like(place), 0
    for i in range(lengths):
        end = end + meta[2 + i]
        begins = jnp.where(end <= place, jnp.maximum(begins, end), begins)
    return begins - first, place < end


def unit_lower_inverses(lowers):
    n = lowers[0].shape[0]
    half = n // 2
    row, col = iota((half, half), 0), iota((half, half), 1)
    blocks = [low[at : at + half, at : at + half] for low in lowers for at in (0, half)]
    inverses = [jnp.where(row == col, 1.0, 0.0) - jnp.where(row // 2 == col // 2, b, 0.0) for b in blocks]
    split = [parts_of(b, 2) for b in blocks]
    zero = jnp.zeros((half, half), BF16)
    size = 2
    while size < half:
        inside = (row // (2 * size) == col // (2 * size)) & (row // size != col // size)
        pieces = [parts_of(inv, 2) for inv in inverses]
        steps = [mm_parts([jnp.where(inside, s, zero) for s in sp], pc) for sp, pc in zip(split, pieces, strict=True)]
        inverses = [inv - mm_parts(pc, parts_of(st, 2)) for inv, pc, st in zip(inverses, pieces, steps, strict=True)]
        size *= 2
    out = []
    for i, low in enumerate(lowers):
        top, bottom = inverses[2 * i], inverses[2 * i + 1]
        corner = -mm(bottom, mm(low[half:, :half], top))
        out.append((top, corner, bottom))
    return out


def conv_rows(pre, reach):
    return (pltpu.roll(pre, reach, 0) if reach else pre)[PAD:]


def conv_forward(pre, taps, age):
    total = jnp.zeros((pre.shape[0] - PAD, pre.shape[1]), F32)
    for k in range(CONV):
        reach = CONV - 1 - k
        total = total + jnp.where(age >= reach, conv_rows(pre, reach), 0.0) * taps[k : k + 1]
    return total


def pick(refs, j, *index):
    value = refs[-1][index]
    for k in range(len(refs) - 1, 0, -1):
        value = jnp.where(j == k, refs[k - 1][index], value)
    return value


def l2_ratio(values):
    return lax.rsqrt(jnp.sum(values * values, -1, keepdims=True) + EPS)


def rms_ratio(values):
    return lax.rsqrt(jnp.mean(values * values, -1, keepdims=True) + EPS)


def norm_back(values, gain, grad):
    ratio = rms_ratio(values)
    scaled = values * ratio
    weighted = grad * gain
    value_grad = ratio * (weighted - scaled * jnp.mean(weighted * scaled, -1, keepdims=True))
    return value_grad, jnp.sum(grad * scaled, 0, keepdims=True)


def terms_kernel(*refs, lengths, n_fsdp, n_blocks):
    (meta, x_ref, gain_ref, bw_ref, taps_ref, local_ref, own_ref), refs = refs[:7], refs[7:]
    pieces = [refs[j * n_blocks : (j + 1) * n_blocks] for j in range(4)]
    (w_ref, pre_ref, act_ref, tt_ref, y_ref, ms_ref, xt_ref, xh_ref, beta_ref, sem) = refs[4 * n_blocks :]
    heads = w_ref.shape[0]
    d_loc = local_ref.shape[1]
    rows = x_ref.shape[0] - PAD
    ctx, fsdp = meta[0], meta[1]

    def fill(source, head, i, shard):
        at = pl.multiple_of(shard * d_loc, d_loc)
        pltpu.make_async_copy(source, w_ref.at[head, i, pl.ds(at, d_loc), :], sem).start()

    for j, blocks in enumerate(pieces):
        head = ctx ^ j
        for i in range(3):
            if j:
                fill(local_ref.at[i, :, pl.ds(pl.multiple_of(head * HD, HD), HD)], head, i, fsdp)
            else:
                fill(own_ref.at[pl.ds(i * d_loc, d_loc), :], head, i, fsdp)
            r = 0
            for block in blocks:
                for k in range(block.shape[0]):
                    r += 1
                    fill(block.at[k, pl.ds(i * d_loc, d_loc), :], head, i, lax.rem(fsdp + n_fsdp - r, n_fsdp))

    x_wide = x_ref[...].astype(F32)
    normed = (x_wide * rms_ratio(x_wide) * gain_ref[...]).astype(BF16)
    xt_ref[...] = normed[PAD:].T
    xh_ref[...] = normed[:PAD].T
    beta = sigmoid(pdot(normed[PAD:], bw_ref[...]))
    beta_ref[...] = beta
    lb, _ = slots(meta, rows, 0, lengths)
    place = iota((rows, 1), 0)
    age = place - lb
    row, col = iota((rows, rows), 0), iota((rows, rows), 1)
    below = (col >= lb) & (col < row)
    lb_last = lb[rows - 1 :]
    last = jnp.where(place >= lb_last, 1.0, 0.0)
    keep = jnp.where(lb_last < 0, 1.0, 0.0)
    eye = jnp.where(iota((HD, HD), 0) == iota((HD, HD), 1), 1.0, 0.0)
    pltpu.make_async_copy(w_ref, w_ref, sem).wait()

    lowers, keys, scaled = [], [], []
    for h in range(heads):
        acts = []
        for i in range(3):
            pre = pdot(normed, w_ref[h, i]).astype(BF16)
            pre_ref[h, i] = pre
            total = conv_forward(pre.astype(F32), taps_ref[h, i], age)
            act = total * sigmoid(total)
            if i < 2:
                act = act * l2_ratio(act)
            acts.append(act.astype(BF16))
            act_ref[h, i] = acts[i]
        key, value = acts[1], acts[2]
        beta_h = beta[:, h : h + 1]
        lowers.append(jnp.where(below, beta_h * pdot(key, key, NT), 0.0))
        keys.append(key)
        scaled.append(beta_h * jnp.concatenate([key, value], -1).astype(F32))
    half = rows // 2
    for h, (top, corner, bottom) in enumerate(unit_lower_inverses(lowers)):
        tt_ref[h, :half, :half] = top.T
        tt_ref[h, :half, half:] = corner.T
        tt_ref[h, half:, :half] = jnp.zeros((half, half), F32)
        tt_ref[h, half:, half:] = bottom.T
        upper = mm(top, scaled[h][:half])
        lower = mm(jnp.concatenate([corner, bottom], -1), scaled[h])
        solved = jnp.concatenate([upper, lower])
        y_ref[h] = solved
        ms_ref[h, 0] = (keep * (eye - mm(solved[:, :HD], keys[h], TN))).astype(BF16)
        ms_ref[h, 1] = mm(last * solved[:, HD:], keys[h], TN).astype(BF16)


def output_kernel(*refs, lengths, sources, n_fsdp):
    (meta, y_ref, act_ref, gain_ref, local_ref, own_ref, o0, o1, o2, o3), refs = refs[:10], refs[10:]
    arrived, (ow_ref, mixed_ref, r_ref, s_ref, n_ref, attn_ref, sem) = refs[:sources], refs[sources:]
    heads, rows = y_ref.shape[:2]
    ctx = meta[0]
    fsdp = meta[1]
    d_loc = own_ref.shape[0]

    def fill(source, head, shard):
        at = pl.multiple_of(shard * d_loc, d_loc)
        pltpu.make_async_copy(source, ow_ref.at[head, pl.ds(at, d_loc), :], sem).start()

    for j, piece in enumerate((o0, o1, o2, o3)):
        head = ctx ^ j
        fill(local_ref.at[:, pl.ds(pl.multiple_of(head * HD, HD), HD)] if j else own_ref, head, fsdp)
        for r in range(1, n_fsdp):
            fill(piece.at[r - 1], head, lax.rem(fsdp + n_fsdp - r, n_fsdp))
    lb, _ = slots(meta, rows, 0, lengths)
    row, col = iota((rows, rows), 0), iota((rows, rows), 1)
    upto = (col >= lb) & (col <= row)
    carried = jnp.where(lb < 0, 1.0, 0.0)
    normed = []
    for h in range(heads):
        state = jnp.zeros((HD, HD), F32)
        for c in range(sources):
            after = pick(arrived, ctx ^ c, h, 1).astype(F32)
            if c:
                after = after + mm(state, pick(arrived, ctx ^ c, h, 0))
            state = jnp.where(c < ctx, after, state)
        query, key = act_ref[h, 0], act_ref[h, 1]
        w_part, u_part = y_ref[h, :, :HD], y_ref[h, :, HD:]
        scores = jnp.where(upto, pdot(query, key, NT) * SCALE, 0.0)
        fresh = u_part - carried * mm(w_part, state, NT)
        mixed = carried * (SCALE * mm(query, state, NT)) + mm(scores, fresh)
        mixed_ref[h] = mixed
        r_ref[h] = fresh
        s_ref[h] = state
        out = (mixed * rms_ratio(mixed) * gain_ref[...]).astype(BF16)
        n_ref[:, h * HD : (h + 1) * HD] = out
        normed.append(out)
    pltpu.make_async_copy(ow_ref, ow_ref, sem).wait()
    total = pdot(normed[0], ow_ref[0], NT)
    for h in range(1, heads):
        total = total + pdot(normed[h], ow_ref[h], NT)
    attn_ref[...] = total


def mlp_kernel(*refs, lengths, n_fsdp):
    (meta, x_ref, attn_ref, other_ref, gain_ref, cot_ref, local_ref, own_ref, f1, f2, a3, b3, down_ref,
     mid_ref, nt_ref, at_ref, g_ref, gf_ref, part_ref, st_ref, w, gu, sem) = refs
    rows, width = x_ref.shape
    units = down_ref.shape[0]
    d_loc = local_ref.shape[0]
    step = GU_BLOCKS * HD
    half = step // 2
    quarters = w.shape[0]
    ctx, fsdp = meta[0], meta[1]

    def fill(source, quarter, shard, at, size):
        start = pl.multiple_of(shard * d_loc, d_loc)
        pltpu.make_async_copy(source, w.at[quarter, pl.ds(start, d_loc), pl.ds(at, size)], sem).start()

    for f in range(n_fsdp):
        fill(own_ref.at[f], ctx, f, 0, step)
    for j in range(1, 4):
        quarter = ctx ^ j
        fill(local_ref.at[:, pl.ds(pl.multiple_of(quarter * step, HD), step)], quarter, fsdp, 0, step)
        for r in range(1, n_fsdp):
            shard = lax.rem(fsdp + n_fsdp - r, n_fsdp)
            if j < 3:
                fill((f1, f2)[j - 1].at[r - 1], quarter, shard, 0, step)
            else:
                fill(a3.at[r - 1], quarter, shard, 0, half)
                fill(b3.at[r - 1], quarter, shard, half, half)

    _, inside = slots(meta, rows, 0, lengths)
    valid = jnp.where(inside, 1.0, 0.0)
    x_wide = x_ref[...].astype(F32)
    attn = (attn_ref[...] + other_ref[...]) * valid
    middle = x_wide + attn
    mid_ref[...] = middle
    for i, v in enumerate((x_wide, attn, middle)):
        st_ref[i : i + 1] = jnp.sum(valid * v * v, 0, keepdims=True)
    normed = (middle * rms_ratio(middle) * gain_ref[...]).astype(BF16)
    nt_ref[...] = normed.T
    g_ffn = (cot_ref[...].astype(F32) * valid).astype(BF16)
    gf_ref[...] = g_ffn
    g_act = pdot(g_ffn, down_ref[...], NT)
    pltpu.make_async_copy(w, w, sem).wait()
    for q in range(quarters):
        gu[:, q * step : (q + 1) * step] = pdot(normed, w[q])
    gate, up = gu[:, :units], gu[:, units : 2 * units]
    sig = sigmoid(gate)
    act = (gate * sig * up).astype(BF16)
    at_ref[...] = act.T
    g_up = g_act * gate * sig
    g_gate = g_act * up * sig * (1.0 + gate * (1.0 - sig))
    gu[:, :units] = g_gate
    gu[:, units : 2 * units] = g_up
    part = None
    for q in range(quarters):
        real = min(step, 2 * units - q * step)
        grad = gu[:, q * step : q * step + real].astype(BF16)
        if real < step:
            grad = jnp.concatenate([grad, jnp.zeros((rows, step - real), BF16)], -1)
        g_ref[ctx ^ q] = grad
        term = pdot(grad, w[q], NT)
        part = term if part is None else part + term
    part_ref[:rows] = part
    part_ref[rows:] = pdot(act, down_ref[...])


def mlp_grads_kernel(nt_ref, g_ref, at_ref, gf_ref, x_ref, y_ref, late_x_ref, late_y_ref, own_ref, down_ref):
    half = g_ref.shape[2] // 2
    nt = nt_ref[...]

    def put(ref, j, side):
        ref[...] = pdot(nt, g_ref[j, :, side * half : (side + 1) * half]).astype(BF16)

    put(x_ref.at[0], 3, 0)
    put(y_ref.at[0], 3, 1)
    put(x_ref.at[1], 1, 0)
    put(y_ref.at[1], 2, 1)
    put(late_x_ref, 1, 1)
    put(late_y_ref, 2, 0)
    put(own_ref.at[0], 0, 0)
    put(own_ref.at[1], 0, 1)
    down_ref[...] = pdot(at_ref[...], gf_ref[...]).astype(BF16)


def middle_kernel(
    meta, part_ref, other_ref, mid_ref, cot_ref, gain_ref, hgain_ref, ow_ref, n_ref, mixed_ref, act_ref, y_ref,
    out_ref, gm_ref, og_ref, do_ref, dr_ref, ds_ref, sm_ref, *, lengths
):
    heads, rows = mixed_ref.shape[:2]
    ctx = meta[0]
    lb, inside = slots(meta, rows, 0, lengths)
    lb_row, _ = slots(meta, rows, 1, lengths)
    valid = jnp.where(inside, 1.0, 0.0)
    row, col = iota((rows, rows), 0), iota((rows, rows), 1)
    upto = (row >= lb_row) & (row <= col)
    carried = jnp.where(lb < 0, 1.0, 0.0)
    middle = mid_ref[...]
    value_grad, gain_grad = norm_back(middle, gain_ref[...], part_ref[:rows] + other_ref[:rows])
    g_middle = cot_ref[...].astype(F32) + value_grad
    gm_ref[...] = g_middle
    g_attn = (g_middle * valid).astype(BF16)
    turned_grad = g_attn.T
    total = jnp.zeros((1, HD), F32)
    for h in range(heads):
        key = act_ref[h, 1]
        g_head = pdot(g_attn, ow_ref[h])
        d_mixed, part = norm_back(mixed_ref[h], hgain_ref[...], g_head)
        total = total + part
        turned = jnp.where(upto, pdot(key, act_ref[h, 0], NT) * SCALE, 0.0)
        d_fresh = mm(turned, d_mixed)
        do_ref[h] = d_mixed
        dr_ref[h] = d_fresh
        d_state = SCALE * mm(carried * d_mixed, act_ref[h, 0], TN) - mm(carried * d_fresh, y_ref[h, :, :HD], TN)
        ds_ref[h] = d_state.astype(BF16)
        og_ref[ctx ^ h] = pdot(turned_grad, n_ref[:, h * HD : (h + 1) * HD]).astype(BF16)
    ffn = (part_ref[rows:] + other_ref[rows:]) * valid
    result = middle + ffn
    out_ref[...] = result.astype(BF16)
    sm_ref[...] = jnp.zeros_like(sm_ref)
    sm_ref[0:1] = gain_grad
    sm_ref[1:2, :HD] = total
    sm_ref[2:3] = jnp.sum(valid * ffn * ffn, 0, keepdims=True)
    sm_ref[3:4] = jnp.sum(valid * result * result, 0, keepdims=True)
    sm_ref[4:5] = jnp.broadcast_to(jnp.sum(valid, 0, keepdims=True), gain_grad.shape) / gain_grad.shape[1]


def delta_back_kernel(*refs, lengths, sources):
    meta, grads, maps = refs[0], refs[1 : 1 + sources], refs[1 + sources : 1 + 2 * sources]
    (pre_ref, act_ref, tt_ref, y_ref, r_ref, s_ref, do_ref, dr_ref, beta_ref, taps_ref, w_ref, bw_ref, xt_ref, xh_ref, sm_ref, og_ref,
     keep_ref, x_ref, y2_ref, late_x_ref, late_y_ref, part_ref, bg_ref, cg_ref) = refs[1 + 2 * sources :]
    heads, rows = r_ref.shape[:2]
    width = w_ref.shape[2]
    ext = rows + PAD
    ctx = meta[0]
    lb, _ = slots(meta, rows, 0, lengths)
    lb_row, _ = slots(meta, rows, 1, lengths)
    place = iota((rows, 1), 0)
    age = place - lb
    row, col = iota((rows, rows), 0), iota((rows, rows), 1)
    last = jnp.where(place >= lb[rows - 1 :], 1.0, 0.0)
    carried = jnp.where(lb < 0, 1.0, 0.0)
    upto = (col >= lb) & (col <= row)
    below = (col >= lb) & (col < row)
    turned_upto = (row >= lb_row) & (row <= col)
    lane = iota((rows, HD), 1)
    logits = jnp.zeros((rows, HD), F32)
    top = jnp.zeros((PAD, HD), F32)
    xt, xh = xt_ref[...], xh_ref[...]
    part = jnp.zeros((rows, width), F32)
    ahead = jnp.zeros((PAD, width), F32)
    for h in range(heads):
        d_state = jnp.zeros((HD, HD), F32)
        for c in range(sources, 0, -1):
            before = pick(grads, ctx ^ c, h).astype(F32)
            if c < sources:
                before = before + mm(d_state, pick(maps, ctx ^ c, h, 0), NT)
            d_state = jnp.where(c > ctx, before, d_state)
        query, key, value = act_ref[h, 0], act_ref[h, 1], act_ref[h, 2]
        solved = y_ref[h]
        fresh, state, d_mixed = r_ref[h], s_ref[h], do_ref[h]
        beta = beta_ref[:, h : h + 1]
        d_fresh = dr_ref[h] + last * mm(key, d_state, NT)
        d_scores = jnp.where(upto, SCALE * mm(d_mixed, fresh, NT), 0.0)
        turned = jnp.where(turned_upto, SCALE * mm(fresh, d_mixed, NT), 0.0)
        d_query = mm(d_scores, key) + carried * (SCALE * mm(d_mixed, state))
        d_key = mm(turned, query) + mm(last * fresh, d_state)
        d_solved = jnp.concatenate([-carried * mm(d_fresh, state), d_fresh], -1)
        d_scaled = mm(tt_ref[h], d_solved)
        d_value = beta * d_scaled[:, HD:]
        d_key = d_key + beta * d_scaled[:, :HD]
        d_beta = jnp.sum(d_scaled[:, :HD] * key.astype(F32) + d_scaled[:, HD:] * value.astype(F32), -1, keepdims=True)
        d_lower = jnp.where(below, -mm(d_scaled, solved, NT), 0.0)
        d_beta = d_beta + jnp.sum(d_lower * pdot(key, key, NT), -1, keepdims=True)
        d_gram = beta * d_lower
        d_key = d_key + mm(d_gram, key) + mm(d_gram, key, TN)
        logits = jnp.where(lane == h, d_beta * beta * (1.0 - beta), logits)
        g_main, g_head = [], []
        for i, grad in enumerate((d_query, d_key, d_value)):
            taps = taps_ref[h, i]
            pre = pre_ref[h, i].astype(F32)
            total = conv_forward(pre, taps, age)
            sig = sigmoid(total)
            if i < 2:
                act = total * sig
                ratio = l2_ratio(act)
                unit = act * ratio
                grad = ratio * (grad - unit * jnp.sum(grad * unit, -1, keepdims=True))
            grad = grad * sig * (1.0 + total * (1.0 - sig))
            back = jnp.zeros((ext, HD), F32)
            for k in range(CONV):
                reach = CONV - 1 - k
                grad_k = jnp.where(age >= reach, grad, 0.0)
                cg_ref[h, i * CONV + k : i * CONV + k + 1, :] = jnp.sum(grad_k * conv_rows(pre, reach), 0, keepdims=True)
                padded = jnp.concatenate([top, grad_k])
                back = back + (pltpu.roll(padded, ext - reach, 0) if reach else padded) * taps[k : k + 1]
            g_main.append(back[PAD:].astype(BF16))
            g_head.append(back[:PAD].astype(BF16))
            part = part + pdot(g_main[i], w_ref[h, i], NT)
            ahead = ahead + pdot(g_head[i], w_ref[h, i], NT)
        piece = pdot(xt, jnp.concatenate(g_main, -1)) + pdot(xh, jnp.concatenate(g_head, -1))
        piece = piece.astype(BF16)
        places = (
            (keep_ref.at[0], keep_ref.at[1]),
            (x_ref.at[1], late_x_ref),
            (late_y_ref, y2_ref.at[1]),
            (x_ref.at[0], y2_ref.at[0]),
        )
        for j, (a, b) in enumerate(places):

            @pl.when(ctx ^ j == h)
            def _(a=a, b=b, j=j, piece=piece):
                a[...] = piece[:, : 2 * HD]
                b[:, :HD] = piece[:, 2 * HD :]
                b[:, HD:] = og_ref[j]

    logits = logits.astype(BF16)
    part_ref[:rows] = part + pdot(logits, bw_ref[...], NT)
    part_ref[rows:ext] = ahead
    part_ref[ext:] = jnp.zeros((PAD, width), F32)
    part_ref[ext : ext + 1, :HD] = sm_ref[1:2, :HD]
    bg_ref[...] = lax.dot_general(logits, xt, (((0,), (1,)), ((), ())), preferred_element_type=F32)[:PAD]


def last_kernel(x_ref, gain_ref, part_ref, other_ref, rim_ref, rim2_ref, gm_ref, sm_ref, st_ref, bg_ref, cg_ref, grad_ref, small_ref):
    rows, width = x_ref.shape
    heads = cg_ref.shape[0]
    total = part_ref[...] + other_ref[...]
    grad = jnp.concatenate([total[: rows - PAD], total[rows - PAD : rows] + (rim_ref[...] + rim2_ref[...])])
    value_grad, gain_grad = norm_back(x_ref[...].astype(F32), gain_ref[...], grad)
    grad_ref[...] = gm_ref[...] + value_grad
    small_ref[...] = jnp.zeros_like(small_ref)
    small_ref[0:1] = gain_grad
    small_ref[1:2] = sm_ref[0:1]
    small_ref[2 : 2 + heads] = bg_ref[:heads]
    small_ref[6:9] = st_ref[0:3]
    small_ref[9:11] = sm_ref[2:4]
    small_ref[11:12] = sm_ref[4:5]
    small_ref[12:13, :HD] = total[rows + PAD : rows + PAD + 1, :HD]
    per = width // HD
    for h in range(heads):
        for k in range(3 * CONV):
            at = h * 3 * CONV + k
            small_ref[13 + at // per : 14 + at // per, (at % per) * HD : (at % per + 1) * HD] = cg_ref[h, k : k + 1]


def gate_up_whole_kernel(meta, a0, b0, a1, b1, a2, b2, a3, b3, gu_ref):
    ctx = meta[0]
    units = gu_ref.shape[2]
    side = GU_BLOCKS // 2
    for q in range(4):
        for j, pair in enumerate(((a0, b0), (a1, b1), (a2, b2), (a3, b3))):

            @pl.when(ctx ^ j == q)
            def _(pair=pair, q=q):
                for k in range(GU_BLOCKS):
                    at = (q * GU_BLOCKS + k) * HD
                    if at < 2 * units:
                        block = pair[k // side][:, k % side * HD : (k % side + 1) * HD]
                        gu_ref[at // units, :, at % units : at % units + HD] = block.astype(F32)


def mixer_whole_kernel(meta, p0, p1, p2, p3, qkv_ref, out_ref):
    ctx = meta[0]
    for q in range(4):
        for j, ref in enumerate((p0, p1, p2, p3)):

            @pl.when(ctx ^ j == q)
            def _(ref=ref, q=q):
                for i in range(3):
                    qkv_ref[i, :, q * HD : (q + 1) * HD] = ref[:, i * HD : (i + 1) * HD].astype(F32)
                out_ref[q * HD : (q + 1) * HD, :] = ref[:, 3 * HD :].T.astype(F32)


def sds(*shape, dtype=F32):
    return jax.ShapeDtypeStruct(shape, dtype)


def call(body, name, out_shape, in_specs, args, scratch=(), gflops=1, mbytes=4):
    return pl.pallas_call(
        body,
        name=name,
        in_specs=in_specs,
        out_specs=jax.tree.map(lambda _: VMEM, out_shape),
        out_shape=out_shape,
        scratch_shapes=list(scratch),
        compiler_params=pltpu.CompilerParams(vmem_limit_bytes=56 * 1024 * 1024),
        cost_estimate=pl.CostEstimate(flops=int(COST * US[name] * 1_150_000_000), bytes_accessed=10**6, transcendentals=0),
    )(*args)


def shifted(value, axis, steps):
    count = lax.axis_size(axis)
    first, end = max(0, -steps), min(count, count - steps)
    return lax.ppermute(value, axis, [(s, s + steps) for s in range(first, end)])


def swapped(value, axis, mask):
    return lax.ppermute(value, axis, [(s, s ^ mask) for s in range(lax.axis_size(axis))])


def far_shards(value):
    count, here = lax.axis_size("fsdp"), lax.axis_index("fsdp")
    if count <= 4:
        turns = [[(s, (s + r) % count) for s in range(count)] for r in range(1, count)]
        return [lax.ppermute(value, "fsdp", turn)[None] for turn in turns]
    return [others(lax.all_gather(value, "fsdp", axis=0))]


def others(value):
    return jnp.concatenate([other(value, r) for r in range(1, lax.axis_size("fsdp"))])


def other(value, r):
    count, here = lax.axis_size("fsdp"), lax.axis_index("fsdp")
    return lax.dynamic_index_in_dim(value, (here + count - r) % count, 0)


def scatter_sum(halves):
    count, here = lax.axis_size("fsdp"), lax.axis_index("fsdp")
    if count > 4:
        return lax.psum_scatter(jnp.concatenate(halves, -1), "fsdp", scatter_dimension=0, tiled=True)
    value = jnp.concatenate(halves, -1)
    rows = value.shape[0] // count
    total = lax.dynamic_slice_in_dim(value, here * rows, rows, 0).astype(F32)
    for r in range(1, count):
        part = lax.dynamic_slice_in_dim(value, (here + r) % count * rows, rows, 0)
        total = total + lax.ppermute(part, "fsdp", [(s, (s + r) % count) for s in range(count)]).astype(F32)
    return total.astype(BF16)


def plane_gather(a, b):
    a1, b2 = swapped(a, "ctx", 1), swapped(b, "ctx", 2)
    b1, a2 = swapped(b, "ctx", 1), swapped(a, "ctx", 2)
    return [(a1, b1), (a2, b2), (swapped(a1, "ctx", 2), swapped(b2, "ctx", 1))]


def in_order(pieces):
    here = lax.axis_index("ctx")
    stacked = jnp.stack(pieces)
    return [lax.dynamic_index_in_dim(stacked, here ^ k, 0, False) for k in range(len(pieces))]


def plane_sum(pieces):
    return (pieces[0].astype(F32) + pieces[1].astype(F32)) + (pieces[2].astype(F32) + pieces[3].astype(F32))


def butterfly(value):
    for axis in ("ctx", "fsdp"):
        mask = 1
        while mask < lax.axis_size(axis):
            value = value + swapped(value, axis, mask)
            mask *= 2
    return value


def local(
    tokens, lengths, norm_gain, qkv_weight, beta_weight, conv_weight, head_gain, out_weight, mlp_gain, gate_up_weight, down_weight, cotangent
):
    rows, width = tokens.shape
    n_ctx, n_fsdp = lax.axis_size("ctx"), lax.axis_size("fsdp")
    ctx, fsdp = lax.axis_index("ctx"), lax.axis_index("fsdp")
    d_loc = qkv_weight.shape[1]
    heads = beta_weight.shape[1]
    units = down_weight.shape[0]
    hd_loc = head_gain.shape[0]
    n_len = lengths.shape[1]
    step = GU_BLOCKS * HD
    ext = rows + PAD
    meta = jnp.concatenate([jnp.stack([ctx, fsdp]).astype(jnp.int32), lengths[0]])

    small = jnp.concatenate([norm_gain, mlp_gain, head_gain, beta_weight.reshape(-1), conv_weight.reshape(-1)])
    small_rows = -(-small.shape[0] // (HD * 16)) * 16
    small = jnp.pad(small, (0, small_rows * HD - small.shape[0])).reshape(small_rows, HD)
    qkv_part = lax.dynamic_slice_in_dim(qkv_weight, ctx * HD, HD, 2).reshape(3 * d_loc, HD)
    out_part = lax.dynamic_slice_in_dim(out_weight, ctx * HD, HD, 0).T
    pack = jnp.concatenate([qkv_part, small])
    packs = lax.all_gather(pack, "fsdp", axis=0)
    pack_far = [others(packs)] if n_fsdp > 4 else [other(packs, r) for r in range(1, n_fsdp)]
    out_local = out_weight.T
    out_part, gate_up_weight, _ = lax.optimization_barrier((out_part, gate_up_weight, packs))
    out_far = far_shards(out_part)
    gu_local = jnp.concatenate(
        [gate_up_weight[0], gate_up_weight[1], jnp.zeros((d_loc, n_ctx * step - 2 * units), BF16)], -1
    )
    gu_own = lax.all_gather(lax.dynamic_slice_in_dim(gu_local, ctx * step, step, 1), "fsdp", axis=0)
    down_full = lax.all_gather(down_weight, "fsdp", axis=1, tiled=True)
    x_ext = jnp.concatenate([shifted(tokens[rows - PAD :], "ctx", 1), tokens])

    one = [swapped(p, "ctx", 1) for p in pack_far]
    two = [swapped(p, "ctx", 2) for p in pack_far]
    three = [swapped(two[k], "ctx", 1) if k % 2 else swapped(one[k], "ctx", 2) for k in range(len(pack_far))]
    out_far = jnp.concatenate(out_far)
    out_pieces = [out_far] + [swapped(out_far, "ctx", j) for j in range(1, n_ctx)]

    flat = packs[:, 3 * d_loc :].reshape(n_fsdp, -1)
    at = 0
    first_gain = flat[:, at : at + d_loc].reshape(1, width).astype(F32)
    at += d_loc
    second_gain = flat[:, at : at + d_loc].reshape(1, width).astype(F32)
    at += d_loc
    head_full = flat[:, at : at + hd_loc].reshape(1, HD).astype(F32)
    at += hd_loc
    beta_full = jnp.pad(flat[:, at : at + d_loc * heads].reshape(width, heads), ((0, 0), (0, HD - heads)))
    at += d_loc * heads
    conv_full = flat[:, at : at + 3 * CONV * heads * hd_loc].reshape(n_fsdp, 3, CONV, heads, hd_loc)
    conv_full = conv_full.transpose(3, 1, 2, 0, 4).reshape(heads, 3, CONV, HD).astype(F32)

    qkv_full, pre, acts, turned, solved, ends_map, normed_t, normed_far, beta = call(
        functools.partial(terms_kernel, lengths=n_len, n_fsdp=n_fsdp, n_blocks=len(pack_far)),
        "delta_terms",
        (
            sds(heads, 3, width, HD, dtype=BF16),
            sds(heads, 3, ext, HD, dtype=BF16),
            sds(heads, 3, rows, HD, dtype=BF16),
            sds(heads, rows, rows),
            sds(heads, rows, 2 * HD),
            sds(heads, 2, HD, HD, dtype=BF16),
            sds(width, rows, dtype=BF16),
            sds(width, PAD, dtype=BF16),
            sds(rows, HD),
        ),
        [SMEM] + [VMEM] * 4 + [ANY] * (2 + 4 * len(pack_far)),
        (meta, x_ext, first_gain, beta_full, conv_full, qkv_weight, pack, *pack_far, *one, *two, *three),
        [pltpu.SemaphoreType.DMA],
        gflops=15,
        mbytes=8,
    )
    arrived = [swapped(ends_map, "ctx", j) for j in range(1, n_ctx)]
    gu_far, _ = lax.optimization_barrier((others(gu_own), ends_map))
    gu_one, gu_two = swapped(gu_far, "ctx", 1), swapped(gu_far, "ctx", 2)
    gu_three = (swapped(gu_one[:, :, : step // 2], "ctx", 2), swapped(gu_two[:, :, step // 2 :], "ctx", 1))
    out_full, mixed, fresh, state, head_out, attn_part = call(
        functools.partial(output_kernel, lengths=n_len, sources=n_ctx - 1, n_fsdp=n_fsdp),
        "delta_outputs",
        (
            sds(heads, width, HD, dtype=BF16),
            sds(heads, rows, HD),
            sds(heads, rows, HD),
            sds(heads, HD, HD),
            sds(rows, heads * HD, dtype=BF16),
            sds(rows, width),
        ),
        [SMEM] + [VMEM] * 3 + [ANY] * (2 + n_ctx) + [VMEM] * len(arrived),
        (meta, solved, acts, head_full, out_local, out_part, *out_pieces, *arrived),
        [pltpu.SemaphoreType.DMA],
        gflops=6,
        mbytes=6,
    )
    attn_other = swapped(attn_part, "tp", 1)

    middle, normed_mid_t, act_t, g_gu, g_ffn, mlp_part, stats = call(
        functools.partial(mlp_kernel, lengths=n_len, n_fsdp=n_fsdp),
        "mlp",
        (
            sds(rows, width),
            sds(width, rows, dtype=BF16),
            sds(units, rows, dtype=BF16),
            sds(n_ctx, rows, step, dtype=BF16),
            sds(rows, width, dtype=BF16),
            sds(2 * rows, width),
            sds(8, width),
        ),
        [SMEM] + [VMEM] * 5 + [ANY] * 6 + [VMEM],
        (
            meta, tokens, attn_part, attn_other, second_gain, cotangent, gu_local, gu_own, gu_one, gu_two, *gu_three, down_full,
        ),
        [pltpu.VMEM((n_ctx, width, step), BF16), pltpu.VMEM((rows, n_ctx * step), F32), pltpu.SemaphoreType.DMA],
        gflops=10,
        mbytes=14,
    )
    mlp_other = swapped(mlp_part, "tp", 1)

    result, g_middle, out_grads, d_mixed, d_fresh, d_state, sums = call(
        functools.partial(middle_kernel, lengths=n_len),
        "middle_back",
        (
            sds(rows, width, dtype=BF16),
            sds(rows, width),
            sds(n_ctx, width, HD, dtype=BF16),
            sds(heads, rows, HD),
            sds(heads, rows, HD),
            sds(heads, HD, HD, dtype=BF16),
            sds(8, width),
        ),
        [SMEM] + [VMEM] * 11,
        (
            meta, mlp_part, mlp_other, middle, cotangent, second_gain, head_full, out_full, head_out, mixed, acts,
            solved,
        ),
        gflops=6,
        mbytes=12,
    )
    behind = [swapped(d_state, "ctx", j) for j in range(1, n_ctx)]

    normed_mid_t, g_gu, g_ffn, _ = lax.optimization_barrier((normed_mid_t, g_gu, g_ffn, d_state))
    quarter = sds(width, step // 2, dtype=BF16)
    double = sds(2, width, step // 2, dtype=BF16)
    gu_x, gu_y, gu_late_x, gu_late_y, gu_keep, down_grad = call(
        mlp_grads_kernel,
        "mlp_grads",
        (double, double, quarter, quarter, double, sds(units, width, dtype=BF16)),
        [VMEM] * 4,
        (normed_mid_t, g_gu, act_t, g_ffn),
        gflops=4,
        mbytes=12,
    )
    down_sh = lax.psum_scatter(down_grad, "fsdp", scatter_dimension=1, tiled=True)
    behind, gu_x, gu_y = lax.optimization_barrier((behind, gu_x, gu_y))
    from_x, from_y = swapped(gu_x, "ctx", 1), swapped(gu_y, "ctx", 2)

    half = sds(width, 2 * HD, dtype=BF16)
    double = sds(2, width, 2 * HD, dtype=BF16)
    back = call(
        functools.partial(delta_back_kernel, lengths=n_len, sources=n_ctx - 1),
        "delta_back",
        (double, double, double, half, half, sds(ext + PAD, width), sds(PAD, width), sds(heads, 16, HD)),
        [SMEM] + [VMEM] * (2 * n_ctx - 2 + 16),
        (
            meta, *behind, *arrived, pre, acts, turned, solved, fresh, state, d_mixed, d_fresh, beta, conv_full, qkv_full, beta_full,
            normed_t, normed_far, sums, out_grads,
        ),
        gflops=16,
        mbytes=16,
    )

    def add(left, right):
        return (left.astype(F32) + right.astype(F32)).astype(BF16)

    from_x, from_y, back = lax.optimization_barrier((from_x, from_y, back))
    mix_keep, mix_x, mix_y, mix_late_x, mix_late_y, in_part, beta_grad, conv_grad = back
    gu_late_y, gu_late_x = add(gu_late_y, from_x[0]), add(gu_late_x, from_y[0])
    rim = shifted(in_part[rows:ext], "ctx", -1)
    gu_late_y, gu_late_x, mix_x, mix_y = lax.optimization_barrier((gu_late_y, gu_late_x, mix_x, mix_y))
    gu_late_y, gu_late_x = swapped(gu_late_y, "ctx", 2), swapped(gu_late_x, "ctx", 1)
    mix_from_x, mix_from_y = swapped(mix_x, "ctx", 1), swapped(mix_y, "ctx", 2)
    in_other = swapped(in_part, "tp", 1)
    gu_sum = [
        (gu_keep[0].astype(F32) + from_x[1].astype(F32) + gu_late_y.astype(F32)).astype(BF16),
        (gu_keep[1].astype(F32) + from_y[1].astype(F32) + gu_late_x.astype(F32)).astype(BF16),
    ]
    gu_sh = lax.psum_scatter(jnp.concatenate(gu_sum, -1), "fsdp", scatter_dimension=0, tiled=True)

    mix_late_y, mix_late_x = add(mix_late_y, mix_from_x[0]), add(mix_late_x, mix_from_y[0])
    mix_late_y, mix_late_x, down_sh = lax.optimization_barrier((mix_late_y, mix_late_x, down_sh))
    mix_late_y, mix_late_x = swapped(mix_late_y, "ctx", 2), swapped(mix_late_x, "ctx", 1)
    side = units // 2
    down_a, down_b = down_sh[:side], down_sh[side:]
    down_a, down_b = add(down_a, swapped(down_a, "ctx", 1)), add(down_b, swapped(down_b, "ctx", 2))
    mix_sum = [
        (mix_keep[0].astype(F32) + mix_from_x[1].astype(F32) + mix_late_y.astype(F32)).astype(BF16),
        (mix_keep[1].astype(F32) + mix_from_y[1].astype(F32) + mix_late_x.astype(F32)).astype(BF16),
    ]
    rim_other = swapped(rim, "tp", 1)
    mix_sum, down_a, down_b, rim, rim_other = lax.optimization_barrier((mix_sum, down_a, down_b, rim, rim_other))
    mix_sh = scatter_sum(mix_sum)
    down_out = jnp.concatenate(
        [
            down_a.astype(F32) + swapped(down_a, "ctx", 2).astype(F32),
            down_b.astype(F32) + swapped(down_b, "ctx", 1).astype(F32),
        ]
    )

    input_grad, smalls = call(
        last_kernel,
        "input_back",
        (sds(rows, width), sds(SMALL_ROWS, width)),
        [VMEM] * 11,
        (tokens, first_gain, in_part, in_other, rim, rim_other, g_middle, sums, stats, beta_grad, conv_grad),
        gflops=1,
        mbytes=6,
    )
    smalls = butterfly(smalls)
    mine = lax.dynamic_slice_in_dim(smalls[:6], fsdp * d_loc, d_loc, 1)
    first_out, second_out, beta_out = mine[0], mine[1], mine[2 : 2 + heads].T
    head_out_grad = lax.dynamic_slice_in_dim(smalls[12], fsdp * hd_loc, hd_loc)
    conv_out = smalls[13 : 13 + heads * 3 * CONV * HD // width].reshape(heads, 3, CONV, HD)
    conv_out = lax.dynamic_slice_in_dim(conv_out, fsdp * hd_loc, hd_loc, 3).transpose(1, 2, 0, 3)
    stat = jnp.sum(smalls[6:12], -1)
    rms = jnp.sqrt(stat[:5] / (stat[5] * width))

    def pieces(part):
        return [part] + [swapped(part, "ctx", j) for j in range(1, n_ctx)]

    gu_pairs = plane_gather(gu_sh[:, : step // 2], gu_sh[:, step // 2 :])
    gu_out = call(
        gate_up_whole_kernel,
        "gate_up_whole",
        sds(2, d_loc, units),
        [SMEM] + [VMEM] * (2 * n_ctx),
        (meta, gu_sh[:, : step // 2], gu_sh[:, step // 2 :], *[p for pair in gu_pairs for p in pair]),
        gflops=1,
        mbytes=6,
    )
    qkv_out, out_out = call(
        mixer_whole_kernel,
        "mixer_whole",
        (sds(3, d_loc, heads * HD), sds(heads * HD, d_loc)),
        [SMEM] + [VMEM] * n_ctx,
        (meta, *pieces(mix_sh)),
        gflops=1,
        mbytes=4,
    )
    return (
        result,
        input_grad,
        first_out,
        qkv_out,
        beta_out,
        conv_out,
        head_out_grad,
        out_out,
        second_out,
        gu_out,
        down_out,
        rms,
    )


def solution(mesh):
    return jax.shard_map(
        local,
        mesh=mesh,
        in_specs=(
            P(("fsdp", "ctx"), None),
            P("fsdp", None),
            P("fsdp"),
            P(None, "fsdp", "tp"),
            P("fsdp", "tp"),
            P(None, None, "tp", "fsdp"),
            P("fsdp"),
            P("tp", "fsdp"),
            P("fsdp"),
            P(None, "fsdp", "tp"),
            P("tp", "fsdp"),
            P(("fsdp", "ctx"), None),
        ),
        out_specs=(
            P(("fsdp", "ctx"), None),
            P(("fsdp", "ctx"), None),
            P("fsdp"),
            P(None, "fsdp", "tp"),
            P("fsdp", "tp"),
            P(None, None, "tp", "fsdp"),
            P("fsdp"),
            P("tp", "fsdp"),
            P("fsdp"),
            P(None, "fsdp", "tp"),
            P("tp", "fsdp"),
            P(),
        ),
        check_vma=False,
    )
```

profile of v0, /device:TPU:0, one launch (start us, length us, event | category | flops | bytes accessed | tf_op | source)
XLA Modules:
  0.0 350.4 jit_solution(11437005783292165295)
XLA Ops:
  12.1 21.7 %all-gather = bf16[3200,128]{1,0:T(8,128)(2,1)S(1)} all-gather(bf16[800,128]{1,0:T(8,128)(2,1)S(1)} %pad_maximum_fusion.4.refs_6_), channel_id=2, replica_groups=mesh['fsdp'=4,'ctx'=4,'tp'=2] {'fsdp'}, dimensions={0}, use_global_device_ids=true | all-gather | bytes 1024000 | tf_op jit(solution)/shard_map/all_gather | solution.py:632
  43.0 2.4 collective-permute-start
  46.9 2.5 collective-permute-start.1
  54.8 6.0 %collective-permute-done.10 = bf16[256,128]{1,0:T(8,128)(2,1)S(1)} collective-permute-done((bf16[256,128]{1,0:T(8,128)(2,1)S(1)}, bf16[256,128]{1,0:T(8,128)(2,1)S(1)}, u32[]{:S(2)}, u32[]{:S(2)}) %collective-permute-start.10) | collective-permute-done | bytes 65568 | tf_op jit(solution)/shard_map/ppermute | solution.py:560
  60.8 2.9 collective-permute-start.4
  70.8 5.4 %collective-permute-done.6.refs_15_ = bf16[1,800,128]{2,1,0:T(8,128)(2,1)S(1)} collective-permute-done((bf16[1,800,128]{2,1,0:T(8,128)(2,1)S(1)}, bf16[1,800,128]{2,1,0:T(8,128)(2,1)S(1)}, u32[]{:S(2)}, u32[]{:S(2)}) %collective-permute-start.6) | collective-permute-done | bytes 204832 | tf_op jit(solution)/shard_map/ppermute | solution.py:553
  81.9 12.2 %delta_terms.1 = (bf16[4,3,1024,128]{3,2,1,0:T(8,128)(2,1)}, bf16[4,3,264,128]{3,2,1,0:T(8,128)(2,1)}, bf16[4,3,256,128]{3,2,1,0:T(8,128)(2,1)}, f32[4,256,256]{...) custom-call(s32[6]{0:T(128)} %pad_add_fusion.refs_0_.meta, ...), custom_call_target="tpu_custom_call" | custom-call | flops 41400000512 | bytes 1000000 | tf_op jit(solution)/shard_map/delta_terms/pallas_call | solution.py:534
  104.7 5.7 %collective-permute-done.18.refs_12_.refs_6_ = bf16[4,2,128,128]{3,2,1,0:T(8,128)(2,1)S(1)} collective-permute-done((bf16[4,2,128,128]{3,2,1,0:T(8,128)(2,1)}, bf16[4,2,128,128]{3,2,1,0:T(8,128)(2,1)S(1)}, u32[]{:S(2)}, u32[]{:S(2)}) %collective-permute-start.18) | collective-permute-done | bytes 262176 | tf_op jit(solution)/shard_map/ppermute | solution.py:553
  111.1 6.5 %delta_outputs.1 = (bf16[4,1024,128]{2,1,0:T(8,128)(2,1)}, f32[4,256,128]{2,1,0:T(8,128)}, f32[4,256,128]{2,1,0:T(8,128)}, f32[4,128,128]{2,1,0:T(8,128)}, bf16[...) custom-call(s32[6]{0:T(128)} %pad_add_fusion.refs_0_.meta, f32[4,256,256]{2,1,0:T(8,128)} %get-tuple-element.93.refs_1_.y_ref.refs_10_, ...), custom_call_target="tpu_custom_call" | custom-call | flops 22424999936 | bytes 1000000 | tf_op jit(solution)/shard_map/delta_outputs/pallas_call | solution.py:534
  117.7 9.0 %collective-permute-done.20.refs_8_ = bf16[3,256,768]{2,1,0:T(8,128)(2,1)S(1)} collective-permute-done((bf16[3,256,768]{2,1,0:T(8,128)(2,1)S(1)}, bf16[3,256,768]{2,1,0:T(8,128)(2,1)S(1)}, u32[]{:S(2)}, u32[]{:S(2)}) %collective-permute-start.20) | collective-permute-done | bytes 1179680 | tf_op jit(solution)/shard_map/ppermute | solution.py:553
  130.7 6.8 %collective-permute-done.22.refs_10_ = bf16[3,256,384]{2,1,0:T(8,128)(2,1)S(1)} collective-permute-done((bf16[3,256,384]{2,1,0:T(8,128)(2,1)S(1)}, bf16[3,256,384]{2,1,0:T(8,128)(2,1)S(1)}, u32[]{:S(2)}, u32[]{:S(2)}) %collective-permute-start.22) | collective-permute-done | bytes 589856 | tf_op jit(solution)/shard_map/ppermute | solution.py:553
  138.9 12.2 %mlp.1 = (f32[256,1024]{1,0:T(8,128)}, bf16[1024,256]{1,0:T(8,128)(2,1)}, bf16[1408,256]{1,0:T(8,128)(2,1)}, bf16[4,256,768]{2,1,0:T(8,128)(2,1)}, bf16[256,1024...) custom-call(s32[6]{0:T(128)} %pad_add_fusion.refs_0_.meta, bf16[256,1024]{1,0:T(8,128)(2,1)} %x_ref.1, ...), custom_call_target="tpu_custom_call" | custom-call | flops 42090000384 | bytes 1000000 | tf_op jit(solution)/shard_map/mlp/pallas_call | solution.py:534
  151.2 4.4 %collective-permute-done.24.other_ref = f32[512,1024]{1,0:T(8,128)S(1)} collective-permute-done((f32[512,1024]{1,0:T(8,128)}, f32[512,1024]{1,0:T(8,128)S(1)}, u32[]{:S(2)}, u32[]{:S(2)}) %collective-permute-start.24) | collective-permute-done | bytes 2097184 | tf_op jit(solution)/shard_map/ppermute | solution.py:553
  156.9 9.6 %middle_back.1 = (bf16[256,1024]{1,0:T(8,128)(2,1)}, f32[256,1024]{1,0:T(8,128)}, bf16[4,1024,128]{2,1,0:T(8,128)(2,1)}, f32[4,256,128]{2,1,0:T(8,128)}, f32[4,2...) custom-call(s32[6]{0:T(128)} %pad_add_fusion.refs_0_.meta, ...), custom_call_target="tpu_custom_call" | custom-call | flops 33120000000 | bytes 1000000 | tf_op jit(solution)/shard_map/middle_back/pallas_call | solution.py:534
  170.0 6.8 %mlp_grads.1 = (bf16[2,1024,384]{2,1,0:T(8,128)(2,1)}, bf16[2,1024,384]{2,1,0:T(8,128)(2,1)}, bf16[1024,384]{1,0:T(8,128)(2,1)}, bf16[1024,384]{1,0:T(8,128)(2,1...) custom-call(bf16[1024,256]{1,0:T(8,128)(2,1)} %get-tuple-element.110.nt_ref, ...), custom_call_target="tpu_custom_call" | custom-call | flops 22424999936 | bytes 1000000 | tf_op jit(solution)/shard_map/mlp_grads/pallas_call | solution.py:534
  180.2 22.4 %delta_back.1 = (bf16[2,1024,256]{2,1,0:T(8,128)(2,1)}, bf16[2,1024,256]{2,1,0:T(8,128)(2,1)}, bf16[2,1024,256]{2,1,0:T(8,128)(2,1)}, bf16[1024,256]{1,0:T(8,128...) custom-call(s32[6]{0:T(128)} %pad_add_fusion.refs_0_.meta, ...), custom_call_target="tpu_custom_call" | custom-call | flops 75900002304 | bytes 1000000 | tf_op jit(solution)/shard_map/delta_back/pallas_call | solution.py:534
  202.7 10.2 %collective-permute-done.28 = bf16[2,1024,384]{2,1,0:T(8,128)(2,1)S(1)} collective-permute-done((bf16[2,1024,384]{2,1,0:T(8,128)(2,1)}, bf16[2,1024,384]{2,1,0:T(8,128)(2,1)S(1)}, u32[]{:S(2)}, u32[]{:S(2)}) %collective-permute-start.28) | collective-permute-done | bytes 1572896 | tf_op jit(solution)/shard_map/ppermute | solution.py:553
  217.6 14.8 %collective-permute-done.49 = bf16[1024,384]{1,0:T(8,128)(2,1)S(1)} collective-permute-done((bf16[1024,384]{1,0:T(8,128)(2,1)S(1)}, bf16[1024,384]{1,0:T(8,128)(2,1)S(1)}, u32[]{:S(2)}, u32[]{:S(2)}) %collective-permute-start.49) | collective-permute-done | bytes 786464 | tf_op jit(solution)/shard_map/ppermute | solution.py:553
  237.8 20.2 %collective-permute-done.32 = bf16[2,1024,256]{2,1,0:T(8,128)(2,1)S(1)} collective-permute-done((bf16[2,1024,256]{2,1,0:T(8,128)(2,1)}, bf16[2,1024,256]{2,1,0:T(8,128)(2,1)S(1)}, u32[]{:S(2)}, u32[]{:S(2)}) %collective-permute-start.32) | collective-permute-done | bytes 1048608 | tf_op jit(solution)/shard_map/ppermute | solution.py:553
  267.5 2.4 collective-permute-start.33
  270.0 2.5 collective-permute-done.37.rim_ref
  272.5 2.4 collective-permute-start.34
  278.4 6.6 %collective-permute-done.33 = bf16[1024,256]{1,0:T(8,128)(2,1)} collective-permute-done((bf16[1024,256]{1,0:T(8,128)(2,1)}, bf16[1024,256]{1,0:T(8,128)(2,1)}, u32[]{:S(2)}, u32[]{:S(2)}) %collective-permute-start.33) | collective-permute-done | bytes 524320 | tf_op jit(solution)/shard_map/ppermute | solution.py:553
  289.2 5.6 %collective-permute-done.51.a1 = bf16[256,384]{1,0:T(8,128)(2,1)S(1)} collective-permute-done((bf16[256,384]{1,0:T(8,128)(2,1)S(1)}, bf16[256,384]{1,0:T(8,128)(2,1)S(1)}, u32[]{:S(2)}, u32[]{:S(2)}) %collective-permute-start.51) | collective-permute-done | bytes 196640 | tf_op jit(solution)/shard_map/ppermute | solution.py:553
  296.5 3.7 %input_back.1 = (f32[256,1024]{1,0:T(8,128)}, f32[24,1024]{1,0:T(8,128)}) custom-call(bf16[256,1024]{1,0:T(8,128)(2,1)} %x_ref.1, f32[1,1024]{1,0:T(1,128)} %bitcast.92, f32[272,1024]{1,0:T(8,128)} %get-tuple-element.141.part_ref, f32[272,1024]{1,0:T(8,128)} %collective-permute-done.30.other_ref, f32[8,1024]{1,0:T(8,128)} %copy-done.56, ...), custom_call_target="tpu_custom_call" | custom-call | flops 12764999680 | bytes 1000000 | tf_op jit(solution)/shard_map/input_back/pallas_call | solution.py:534
  301.3 3.8 %collective-permute-done.39 = f32[24,1024]{1,0:T(8,128)S(1)} collective-permute-done((f32[24,1024]{1,0:T(8,128)}, f32[24,1024]{1,0:T(8,128)S(1)}, u32[]{:S(2)}, u32[]{:S(2)}) %collective-permute-start.39) | collective-permute-done | bytes 98336 | tf_op jit(solution)/shard_map/ppermute | solution.py:553
  306.9 3.1 collective-permute-start.43
  309.9 2.4 collective-permute-start.44
  312.3 2.8 collective-permute-start.45
  315.9 3.3 gate_up_whole.1
  319.2 3.4 collective-permute-done.40
  340.5 2.9 mixer_whole.1
  (292 shorter events, 108.4 us)
Async XLA Ops:
  7.2 90.4 %all-gather.7.cloned.1.call-start = ((), (), s32[]{:S(2)}) async-start(), calls=%async_computation.5 | async-start | bytes 1966080 | tf_op jit(solution)/shard_map/all_gather | solution.py:640
  37.8 101.1 %all-gather.5.cloned.1.call-start = ((), (), s32[]{:S(2)}) async-start(), calls=%async_computation.2 | async-start | bytes 3604480 | tf_op jit(solution)/shard_map/all_gather | solution.py:641
  38.0 25.8 %collective-permute-start.5 = (bf16[1,800,128]{2,1,0:T(8,128)(2,1)S(1)}, bf16[1,800,128]{2,1,0:T(8,128)(2,1)S(1)}, u32[]{:S(2)}, u32[]{:S(2)}) collective-permute-start(bf16[1,800,128]{2,1,0:T(8,128)(2,1)S(1)} %get-tuple-element.187.refs_8_), channel_id=1, source_target_pairs={{0,4},{2,6},{4,0},{6,2},{1,5},{3,7},{5,1},{7,3},{8,12},{10,14},{12... | collective-permute-start | bytes 614408 | tf_op jit(solution)/shard_map/ppermute | solution.py:553
  39.6 26.3 %collective-permute-start.2 = (bf16[1,800,128]{2,1,0:T(8,128)(2,1)S(1)}, bf16[1,800,128]{2,1,0:T(8,128)(2,1)S(1)}, u32[]{:S(2)}, u32[]{:S(2)}) collective-permute-start(bf16[1,800,128]{2,1,0:T(8,128)(2,1)S(1)} %get-tuple-element.187.refs_8_), channel_id=1, source_target_pairs={{0,2},{2,0},{4,6},{6,4},{1,3},{3,1},{5,7},{7,5},{8,10},{10,8},{12,... | collective-permute-start | bytes 614408 | tf_op jit(solution)/shard_map/ppermute | solution.py:553
  45.5 215.1 %reduce-scatter.3.cloned.1.call-start = ((), (), s32[]{:S(2)}) async-start(), calls=%async_computation.3 | async-start | bytes 3604480 | tf_op jit(solution)/shard_map/reduce_scatter | solution.py:762
  46.9 16.8 %collective-permute-start.1 = (bf16[1,800,128]{2,1,0:T(8,128)(2,1)S(1)}, bf16[1,800,128]{2,1,0:T(8,128)(2,1)S(1)}, u32[]{:S(2)}, u32[]{:S(2)}) collective-permute-start(bf16[1,800,128]{2,1,0:T(8,128)(2,1)S(1)} %get-tuple-element.188.refs_7_), channel_id=1, source_target_pairs={{0,2},{2,0},{4,6},{6,4},{1,3},{3,1},{5,7},{7,5},{8,10},{10,8},{12,... | collective-permute-start | bytes 614408 | tf_op jit(solution)/shard_map/ppermute | solution.py:553
  49.4 16.4 %collective-permute-start.3 = (bf16[1,800,128]{2,1,0:T(8,128)(2,1)S(1)}, bf16[1,800,128]{2,1,0:T(8,128)(2,1)S(1)}, u32[]{:S(2)}, u32[]{:S(2)}) collective-permute-start(bf16[1,800,128]{2,1,0:T(8,128)(2,1)S(1)} %get-tuple-element.186.refs_9_), channel_id=1, source_target_pairs={{0,2},{2,0},{4,6},{6,4},{1,3},{3,1},{5,7},{7,5},{8,10},{10,8},{12,... | collective-permute-start | bytes 614408 | tf_op jit(solution)/shard_map/ppermute | solution.py:553
  63.8 15.2 %collective-permute-start.7 = (bf16[1,800,128]{2,1,0:T(8,128)(2,1)S(1)}, bf16[1,800,128]{2,1,0:T(8,128)(2,1)S(1)}, u32[]{:S(2)}, u32[]{:S(2)}) collective-permute-start(bf16[1,800,128]{2,1,0:T(8,128)(2,1)S(1)} %collective-permute-done.1.refs_10_), channel_id=1, source_target_pairs={{0,4},{2,6},{4,0},{6,2},{1,5},{3,7},{5,1},{7,3},{8,12},{10,14},{12... | collective-permute-start | bytes 614408 | tf_op jit(solution)/shard_map/ppermute | solution.py:553
  65.8 14.8 %collective-permute-start.8 = (bf16[1,800,128]{2,1,0:T(8,128)(2,1)S(1)}, bf16[1,800,128]{2,1,0:T(8,128)(2,1)S(1)}, u32[]{:S(2)}, u32[]{:S(2)}) collective-permute-start(bf16[1,800,128]{2,1,0:T(8,128)(2,1)S(1)} %collective-permute-done.5.refs_14_), channel_id=1, source_target_pairs={{0,2},{2,0},{4,6},{6,4},{1,3},{3,1},{5,7},{7,5},{8,10},{10,8},{12,... | collective-permute-start | bytes 614408 | tf_op jit(solution)/shard_map/ppermute | solution.py:553
  65.9 15.3 %collective-permute-start.9 = (bf16[1,800,128]{2,1,0:T(8,128)(2,1)S(1)}, bf16[1,800,128]{2,1,0:T(8,128)(2,1)S(1)}, u32[]{:S(2)}, u32[]{:S(2)}) collective-permute-start(bf16[1,800,128]{2,1,0:T(8,128)(2,1)S(1)} %collective-permute-done.3.refs_12_), channel_id=1, source_target_pairs={{0,4},{2,6},{4,0},{6,2},{1,5},{3,7},{5,1},{7,3},{8,12},{10,14},{12... | collective-permute-start | bytes 614408 | tf_op jit(solution)/shard_map/ppermute | solution.py:553
  69.7 26.5 %collective-permute-start.13 = (bf16[3,256,128]{2,1,0:T(8,128)(2,1)S(1)}, bf16[3,256,128]{2,1,0:T(8,128)(2,1)S(1)}, u32[]{:S(2)}, u32[]{:S(2)}) collective-permute-start(bf16[3,256,128]{2,1,0:T(8,128)(2,1)S(1)} %pad_maximum_fusion.5.refs_6_), channel_id=1, source_target_pairs={{0,2},{2,0},{4,6},{6,4},{1,3},{3,1},{5,7},{7,5},{8,10},{10,8},{12,... | collective-permute-start | bytes 589832 | tf_op jit(solution)/shard_map/ppermute | solution.py:553
  76.2 22.9 %collective-permute-start.14 = (bf16[3,256,128]{2,1,0:T(8,128)(2,1)S(1)}, bf16[3,256,128]{2,1,0:T(8,128)(2,1)S(1)}, u32[]{:S(2)}, u32[]{:S(2)}) collective-permute-start(bf16[3,256,128]{2,1,0:T(8,128)(2,1)S(1)} %pad_maximum_fusion.5.refs_6_), channel_id=1, source_target_pairs={{0,4},{2,6},{4,0},{6,2},{1,5},{3,7},{5,1},{7,3},{8,12},{10,14},{12... | collective-permute-start | bytes 589832 | tf_op jit(solution)/shard_map/ppermute | solution.py:553
  79.0 21.3 %collective-permute-start.15 = (bf16[3,256,128]{2,1,0:T(8,128)(2,1)S(1)}, bf16[3,256,128]{2,1,0:T(8,128)(2,1)}, u32[]{:S(2)}, u32[]{:S(2)}) collective-permute-start(bf16[3,256,128]{2,1,0:T(8,128)(2,1)S(1)} %pad_maximum_fusion.5.refs_6_), channel_id=1, source_target_pairs={{0,6},{2,4},{4,2},{6,0},{1,7},{3,5},{5,3},{7,1},{8,14},{10,12},{12... | collective-permute-start | bytes 589832 | tf_op jit(solution)/shard_map/ppermute | solution.py:553
  99.1 27.5 %collective-permute-start.20 = (bf16[3,256,768]{2,1,0:T(8,128)(2,1)S(1)}, bf16[3,256,768]{2,1,0:T(8,128)(2,1)S(1)}, u32[]{:S(2)}, u32[]{:S(2)}) collective-permute-start(bf16[3,256,768]{2,1,0:T(8,128)(2,1)S(1)} %pad_maximum_fusion.2), channel_id=1, source_target_pairs={{0,2},{2,0},{4,6},{6,4},{1,3},{3,1},{5,7},{7,5},{8,10},{10,8},{12,... | collective-permute-start | bytes 3538952 | tf_op jit(solution)/shard_map/ppermute | solution.py:553
  100.3 28.4 %collective-permute-start.21 = (bf16[3,256,768]{2,1,0:T(8,128)(2,1)S(1)}, bf16[3,256,768]{2,1,0:T(8,128)(2,1)S(1)}, u32[]{:S(2)}, u32[]{:S(2)}) collective-permute-start(bf16[3,256,768]{2,1,0:T(8,128)(2,1)S(1)} %pad_maximum_fusion.2), channel_id=1, source_target_pairs={{0,4},{2,6},{4,0},{6,2},{1,5},{3,7},{5,1},{7,3},{8,12},{10,14},{12... | collective-permute-start | bytes 3538952 | tf_op jit(solution)/shard_map/ppermute | solution.py:553
  176.8 98.0 %reduce-scatter.5.cloned.1.call-start = ((), (), s32[]{:S(2)}) async-start(), calls=%async_computation.4 | async-start | bytes 1966080 | tf_op jit(solution)/shard_map/reduce_scatter | solution.py:796
  176.9 35.9 %collective-permute-start.28 = (bf16[2,1024,384]{2,1,0:T(8,128)(2,1)}, bf16[2,1024,384]{2,1,0:T(8,128)(2,1)S(1)}, u32[]{:S(2)}, u32[]{:S(2)}) collective-permute-start(bf16[2,1024,384]{2,1,0:T(8,128)(2,1)} %get-tuple-element.116), channel_id=1, source_target_pairs={{0,2},{2,0},{4,6},{6,4},{1,3},{3,1},{5,7},{7,5},{8,10},{10,8},{12,... | collective-permute-start | bytes 4718600 | tf_op jit(solution)/shard_map/ppermute | solution.py:553
  178.3 35.6 %collective-permute-start.29 = (bf16[2,1024,384]{2,1,0:T(8,128)(2,1)S(1)}, bf16[2,1024,384]{2,1,0:T(8,128)(2,1)S(1)}, u32[]{:S(2)}, u32[]{:S(2)}) collective-permute-start(bf16[2,1024,384]{2,1,0:T(8,128)(2,1)S(1)} %copy-done.27), channel_id=1, source_target_pairs={{0,4},{2,6},{4,0},{6,2},{1,5},{3,7},{5,1},{7,3},{8,12},{10,14},{12... | collective-permute-start | bytes 4718600 | tf_op jit(solution)/shard_map/ppermute | solution.py:553
  214.4 18.0 %collective-permute-start.49 = (bf16[1024,384]{1,0:T(8,128)(2,1)S(1)}, bf16[1024,384]{1,0:T(8,128)(2,1)S(1)}, u32[]{:S(2)}, u32[]{:S(2)}) collective-permute-start(bf16[1024,384]{1,0:T(8,128)(2,1)S(1)} %get-tuple-element.170), channel_id=1, source_target_pairs={{0,4},{2,6},{4,0},{6,2},{1,5},{3,7},{5,1},{7,3},{8,12},{10,14},{12... | collective-permute-start | bytes 2359304 | tf_op jit(solution)/shard_map/ppermute | solution.py:553
  216.0 17.5 %collective-permute-start.50 = (bf16[1024,384]{1,0:T(8,128)(2,1)S(1)}, bf16[1024,384]{1,0:T(8,128)(2,1)S(1)}, u32[]{:S(2)}, u32[]{:S(2)}) collective-permute-start(bf16[1024,384]{1,0:T(8,128)(2,1)S(1)} %get-tuple-element.171), channel_id=1, source_target_pairs={{0,2},{2,0},{4,6},{6,4},{1,3},{3,1},{5,7},{7,5},{8,10},{10,8},{12,... | collective-permute-start | bytes 2359304 | tf_op jit(solution)/shard_map/ppermute | solution.py:553
  235.4 22.6 %collective-permute-start.32 = (bf16[2,1024,256]{2,1,0:T(8,128)(2,1)}, bf16[2,1024,256]{2,1,0:T(8,128)(2,1)S(1)}, u32[]{:S(2)}, u32[]{:S(2)}) collective-permute-start(bf16[2,1024,256]{2,1,0:T(8,128)(2,1)} %get-tuple-element.152), channel_id=1, source_target_pairs={{0,4},{2,6},{4,0},{6,2},{1,5},{3,7},{5,1},{7,3},{8,12},{10,14},{12... | collective-permute-start | bytes 3145736 | tf_op jit(solution)/shard_map/ppermute | solution.py:553
  236.1 22.6 %collective-permute-start.31 = (bf16[2,1024,256]{2,1,0:T(8,128)(2,1)}, bf16[2,1024,256]{2,1,0:T(8,128)(2,1)S(1)}, u32[]{:S(2)}, u32[]{:S(2)}) collective-permute-start(bf16[2,1024,256]{2,1,0:T(8,128)(2,1)} %get-tuple-element.149), channel_id=1, source_target_pairs={{0,2},{2,0},{4,6},{6,4},{1,3},{3,1},{5,7},{7,5},{8,10},{10,8},{12,... | collective-permute-start | bytes 3145736 | tf_op jit(solution)/shard_map/ppermute | solution.py:553
  237.8 58.7 %collective-permute-start.30 = (f32[272,1024]{1,0:T(8,128)}, f32[272,1024]{1,0:T(8,128)}, u32[]{:S(2)}, u32[]{:S(2)}) collective-permute-start(f32[272,1024]{1,0:T(8,128)} %get-tuple-element.141.part_ref), channel_id=1, source_target_pairs={{0,1},{1,0},{2,3},{3,2},{4,5},{5,4},{6,7},{7,6},{8,9},{9,8},{10,11... | collective-permute-start | bytes 3342344 | tf_op jit(solution)/shard_map/ppermute | solution.py:553
  267.5 17.4 %collective-permute-start.33 = (bf16[1024,256]{1,0:T(8,128)(2,1)}, bf16[1024,256]{1,0:T(8,128)(2,1)}, u32[]{:S(2)}, u32[]{:S(2)}) collective-permute-start(bf16[1024,256]{1,0:T(8,128)(2,1)} %fusion.5), channel_id=1, source_target_pairs={{0,4},{2,6},{4,0},{6,2},{1,5},{3,7},{5,1},{7,3},{8,12},{10,14},{12... | collective-permute-start | bytes 1572872 | tf_op jit(solution)/shard_map/ppermute | solution.py:553
  276.1 19.3 %collective-permute-start.54 = (bf16[256,384]{1,0:T(8,128)(2,1)S(1)}, bf16[256,384]{1,0:T(8,128)(2,1)S(1)}, u32[]{:S(2)}, u32[]{:S(2)}) collective-permute-start(bf16[256,384]{1,0:T(8,128)(2,1)S(1)} %get-tuple-element.193.b0), channel_id=1, source_target_pairs={{0,4},{2,6},{4,0},{6,2},{1,5},{3,7},{5,1},{7,3},{8,12},{10,14},{12... | collective-permute-start | bytes 589832 | tf_op jit(solution)/shard_map/ppermute | solution.py:553
  284.9 21.9 %collective-permute-start.52 = (bf16[256,384]{1,0:T(8,128)(2,1)S(1)}, bf16[256,384]{1,0:T(8,128)(2,1)S(1)}, u32[]{:S(2)}, u32[]{:S(2)}) collective-permute-start(bf16[256,384]{1,0:T(8,128)(2,1)S(1)} %get-tuple-element.193.b0), channel_id=1, source_target_pairs={{0,2},{2,0},{4,6},{6,4},{1,3},{3,1},{5,7},{7,5},{8,10},{10,8},{12,... | collective-permute-start | bytes 589832 | tf_op jit(solution)/shard_map/ppermute | solution.py:553
  288.6 21.3 %collective-permute-start.53 = (bf16[256,384]{1,0:T(8,128)(2,1)S(1)}, bf16[256,384]{1,0:T(8,128)(2,1)S(1)}, u32[]{:S(2)}, u32[]{:S(2)}) collective-permute-start(bf16[256,384]{1,0:T(8,128)(2,1)S(1)} %get-tuple-element.194.a0), channel_id=1, source_target_pairs={{0,4},{2,6},{4,0},{6,2},{1,5},{3,7},{5,1},{7,3},{8,12},{10,14},{12... | collective-permute-start | bytes 589832 | tf_op jit(solution)/shard_map/ppermute | solution.py:553
  294.8 17.5 %collective-permute-start.55 = (bf16[256,384]{1,0:T(8,128)(2,1)S(1)}, bf16[256,384]{1,0:T(8,128)(2,1)S(1)}, u32[]{:S(2)}, u32[]{:S(2)}) collective-permute-start(bf16[256,384]{1,0:T(8,128)(2,1)S(1)} %collective-permute-done.51.a1), channel_id=1, source_target_pairs={{0,4},{2,6},{4,0},{6,2},{1,5},{3,7},{5,1},{7,3},{8,12},{10,14},{12... | collective-permute-start | bytes 589832 | tf_op jit(solution)/shard_map/ppermute | solution.py:553
  295.4 19.8 %collective-permute-start.56 = (bf16[256,384]{1,0:T(8,128)(2,1)S(1)}, bf16[256,384]{1,0:T(8,128)(2,1)S(1)}, u32[]{:S(2)}, u32[]{:S(2)}) collective-permute-start(bf16[256,384]{1,0:T(8,128)(2,1)S(1)} %collective-permute-done.54.b2), channel_id=1, source_target_pairs={{0,2},{2,0},{4,6},{6,4},{1,3},{3,1},{5,7},{7,5},{8,10},{10,8},{12,... | collective-permute-start | bytes 589832 | tf_op jit(solution)/shard_map/ppermute | solution.py:553
  305.1 23.8 %collective-permute-start.57 = (bf16[704,256]{1,0:T(8,128)(2,1)S(1)}, bf16[704,256]{1,0:T(8,128)(2,1)S(1)}, u32[]{:S(2)}, u32[]{:S(2)}) collective-permute-start(bf16[704,256]{1,0:T(8,128)(2,1)S(1)} %get-tuple-element.172), channel_id=1, source_target_pairs={{0,4},{2,6},{4,0},{6,2},{1,5},{3,7},{5,1},{7,3},{8,12},{10,14},{12... | collective-permute-start | bytes 1081352 | tf_op jit(solution)/shard_map/ppermute | solution.py:553
  306.9 15.8 %collective-permute-start.43 = (bf16[256,512]{1,0:T(8,128)(2,1)S(1)}, bf16[256,512]{1,0:T(8,128)(2,1)S(1)}, u32[]{:S(2)}, u32[]{:S(2)}) collective-permute-start(bf16[256,512]{1,0:T(8,128)(2,1)S(1)} %get-tuple-element.181), channel_id=1, source_target_pairs={{0,8},{8,16},{16,24},{24,0},{1,9},{9,17},{17,25},{25,1},{2,10},{10... | collective-permute-start | bytes 786440 | tf_op jit(solution)/shard_map/ppermute | solution.py:582
  323.5 15.5 %collective-permute-start.46 = (bf16[256,512]{1,0:T(8,128)(2,1)S(1)}, bf16[256,512]{1,0:T(8,128)(2,1)S(1)}, u32[]{:S(2)}, u32[]{:S(2)}) collective-permute-start(bf16[256,512]{1,0:T(8,128)(2,1)S(1)} %add_convert_fusion.2.p0), channel_id=1, source_target_pairs={{0,2},{2,0},{4,6},{6,4},{1,3},{3,1},{5,7},{7,5},{8,10},{10,8},{12,... | collective-permute-start | bytes 786440 | tf_op jit(solution)/shard_map/ppermute | solution.py:553
  (89 other events, 934.4 us)
Sparse Core Ops, SparseCore 0:
  37.9 37.8 all-gather.6
  77.3 58.0 all-gather.4
  176.9 57.4 reduce-scatter.2
  237.2 35.1 reduce-scatter.4
where the time goes:
time: 354 us; the launch traced here: 350 us
  waiting for transfers between devices  122 us (34%)
  Pallas kernels  79.5 us (22%)
  starting transfers between devices  74.1 us (21%)
  local copies, waits for them, and re-layouts  27.4 us (8%)
  blocking collectives  21.7 us (6%)
  between operations  15.7 us (4%)
  other arithmetic  10.4 us (3%)
    ppermute x51, waiting for transfers between devices, swapped(): lax.ppermute(value, axis, [(s, s ^ mask) for s in range(lax.axis_size(axi...  112 us
    pallas_call x9, Pallas kernels, call(): pl.pallas_call(body, name=name, in_specs=in_specs, out_specs=jax.tree.map...  79.5 us
    ppermute x51, starting transfers between devices, swapped(): lax.ppermute(value, axis, [(s, s ^ mask) for s in range(lax.axis_size(axi...  58.7 us
    all_gather x1, blocking collectives, local(): packs = lax.all_gather(pack, 'fsdp', axis=0)  21.7 us
    unnamed x124, local copies, waits for them, and re-layouts  10.1 us
    ppermute x3, starting transfers between devices, scatter_sum(): lax.ppermute(part, 'fsdp', [(s, (s + r) % count) for s in range(count)])  8.29 us
  transfers between devices with their start and end apart: 63, of which 27 were waited for; matrix products, arithmetic and copies ran while one was open for 7% of the time, Pallas kernels for 16%

commit v1 on v0

--- a/solution.py
+++ b/solution.py
@@ -20,7 +20,8 @@
 COST = 3.0
 US = {'delta_terms': 12, 'delta_outputs': 6.5, 'mlp': 12.2, 'mlp_grads': 6.5, 'middle_back': 9.6, 'delta_back': 22, 'input_back': 3.7, 'mixer_sum': 3.5, 'mixer_total': 2.3, 'gate_up_whole': 3.3, 'mixer_whole': 2.9}
 GU_BLOCKS = 6
-SMALL_ROWS = 24
+SMALL_ROWS = 32
+WIDE_ROWS = 6
 
 ANY = pl.BlockSpec(memory_space=pl.ANY)
 SMEM = pl.BlockSpec(memory_space=pltpu.SMEM)
@@ -133,31 +134,37 @@
     return value_grad, jnp.sum(grad * scaled, 0, keepdims=True)
 
 
-def terms_kernel(*refs, lengths, n_fsdp, n_blocks):
-    (meta, x_ref, gain_ref, bw_ref, taps_ref, local_ref, own_ref), refs = refs[:7], refs[7:]
-    pieces = [refs[j * n_blocks : (j + 1) * n_blocks] for j in range(4)]
-    (w_ref, pre_ref, act_ref, tt_ref, y_ref, ms_ref, xt_ref, xh_ref, beta_ref, sem) = refs[4 * n_blocks :]
+def terms_kernel(*refs, lengths, n_fsdp, cut):
+    (meta, x_ref, gain_ref, bw_ref, taps_ref, local_ref, own_ref, one, two, three_a, three_b,
+     w_ref, pre_ref, act_ref, tt_ref, y_ref, ms_ref, xt_ref, xh_ref, beta_ref, sem) = refs
     heads = w_ref.shape[0]
     d_loc = local_ref.shape[1]
     rows = x_ref.shape[0] - PAD
     ctx, fsdp = meta[0], meta[1]
 
-    def fill(source, head, i, shard):
-        at = pl.multiple_of(shard * d_loc, d_loc)
-        pltpu.make_async_copy(source, w_ref.at[head, i, pl.ds(at, d_loc), :], sem).start()
-
-    for j, blocks in enumerate(pieces):
+    def fill(source, first, end, head, shard, skip=0):
+        for i in range(3):
+            start, stop = max(first, i * d_loc), min(end, (i + 1) * d_loc)
+            if start < stop:
+                at = pl.multiple_of(shard * d_loc + (start - i * d_loc), 16)
+                target = w_ref.at[head, i, pl.ds(at, stop - start), :]
+                pltpu.make_async_copy(source.at[pl.ds(start - skip, stop - start), :], target, sem).start()
+
+    for f in range(n_fsdp):
+        fill(own_ref.at[f], 0, 3 * d_loc, ctx, f)
+    for j in range(1, 4):
         head = ctx ^ j
         for i in range(3):
-            if j:
-                fill(local_ref.at[i, :, pl.ds(pl.multiple_of(head * HD, HD), HD)], head, i, fsdp)
+            target = w_ref.at[head, i, pl.ds(pl.multiple_of(fsdp * d_loc, d_loc), d_loc), :]
+            source = local_ref.at[i, :, pl.ds(pl.multiple_of(head * HD, HD), HD)]
+            pltpu.make_async_copy(source, target, sem).start()
+        for r in range(1, n_fsdp):
+            shard = lax.rem(fsdp + n_fsdp - r, n_fsdp)
+            if j < 3:
+                fill((one, two)[j - 1].at[r - 1], 0, 3 * d_loc, head, shard)
             else:
-                fill(own_ref.at[pl.ds(i * d_loc, d_loc), :], head, i, fsdp)
-            r = 0
-            for block in blocks:
-                for k in range(block.shape[0]):
-                    r += 1
-                    fill(block.at[k, pl.ds(i * d_loc, d_loc), :], head, i, lax.rem(fsdp + n_fsdp - r, n_fsdp))
+                fill(three_a.at[r - 1], 0, cut, head, shard)
+                fill(three_b.at[r - 1], cut, 3 * d_loc, head, shard, cut)
 
     x_wide = x_ref[...].astype(F32)
     normed = (x_wide * rms_ratio(x_wide) * gain_ref[...]).astype(BF16)
@@ -208,20 +215,20 @@
 
 
 def output_kernel(*refs, lengths, sources, n_fsdp):
-    (meta, y_ref, act_ref, gain_ref, local_ref, own_ref, o0, o1, o2, o3), refs = refs[:10], refs[10:]
+    (meta, y_ref, act_ref, gain_ref, local_ref, own_ref, o1, o2, o3), refs = refs[:9], refs[9:]
     arrived, (ow_ref, mixed_ref, r_ref, s_ref, n_ref, attn_ref, sem) = refs[:sources], refs[sources:]
     heads, rows = y_ref.shape[:2]
     ctx = meta[0]
     fsdp = meta[1]
-    d_loc = own_ref.shape[0]
+    d_loc = local_ref.shape[0]
 
     def fill(source, head, shard):
         at = pl.multiple_of(shard * d_loc, d_loc)
         pltpu.make_async_copy(source, ow_ref.at[head, pl.ds(at, d_loc), :], sem).start()
 
-    for j, piece in enumerate((o0, o1, o2, o3)):
+    for j, piece in enumerate((own_ref, o1, o2, o3)):
         head = ctx ^ j
-        fill(local_ref.at[:, pl.ds(pl.multiple_of(head * HD, HD), HD)] if j else own_ref, head, fsdp)
+        fill(local_ref.at[:, pl.ds(pl.multiple_of(head * HD, HD), HD)], head, fsdp)
         for r in range(1, n_fsdp):
             fill(piece.at[r - 1], head, lax.rem(fsdp + n_fsdp - r, n_fsdp))
     lb, _ = slots(meta, rows, 0, lengths)
@@ -319,17 +326,17 @@
     part_ref[rows:] = pdot(act, down_ref[...])
 
 
-def mlp_grads_kernel(nt_ref, g_ref, at_ref, gf_ref, x_ref, y_ref, late_x_ref, late_y_ref, own_ref, down_ref):
+def mlp_grads_kernel(nt_ref, g_ref, at_ref, gf_ref, x3_ref, y3_ref, x1_ref, y2_ref, late_x_ref, late_y_ref, own_ref, down_ref):
     half = g_ref.shape[2] // 2
     nt = nt_ref[...]
 
     def put(ref, j, side):
         ref[...] = pdot(nt, g_ref[j, :, side * half : (side + 1) * half]).astype(BF16)
 
-    put(x_ref.at[0], 3, 0)
-    put(y_ref.at[0], 3, 1)
-    put(x_ref.at[1], 1, 0)
-    put(y_ref.at[1], 2, 1)
+    put(x3_ref, 3, 0)
+    put(y3_ref, 3, 1)
+    put(x1_ref, 1, 0)
+    put(y2_ref, 2, 1)
     put(late_x_ref, 1, 1)
     put(late_y_ref, 2, 0)
     put(own_ref.at[0], 0, 0)
@@ -476,11 +483,11 @@
     bg_ref[...] = lax.dot_general(logits, xt, (((0,), (1,)), ((), ())), preferred_element_type=F32)[:PAD]
 
 
-def last_kernel(x_ref, gain_ref, part_ref, other_ref, rim_ref, rim2_ref, gm_ref, sm_ref, st_ref, bg_ref, cg_ref, grad_ref, small_ref):
+def last_kernel(x_ref, gain_ref, part_ref, other_ref, rim_ref, gm_ref, sm_ref, st_ref, bg_ref, cg_ref, grad_ref, small_ref):
     rows, width = x_ref.shape
     heads = cg_ref.shape[0]
     total = part_ref[...] + other_ref[...]
-    grad = jnp.concatenate([total[: rows - PAD], total[rows - PAD : rows] + (rim_ref[...] + rim2_ref[...])])
+    grad = jnp.concatenate([total[: rows - PAD], total[rows - PAD : rows] + rim_ref[...]])
     value_grad, gain_grad = norm_back(x_ref[...].astype(F32), gain_ref[...], grad)
     grad_ref[...] = gm_ref[...] + value_grad
     small_ref[...] = jnp.zeros_like(small_ref)
@@ -490,28 +497,75 @@
     small_ref[6:9] = st_ref[0:3]
     small_ref[9:11] = sm_ref[2:4]
     small_ref[11:12] = sm_ref[4:5]
-    small_ref[12:13, :HD] = total[rows + PAD : rows + PAD + 1, :HD]
-    per = width // HD
+    at = WIDE_ROWS + 6
     for h in range(heads):
-        for k in range(3 * CONV):
-            at = h * 3 * CONV + k
-            small_ref[13 + at // per : 14 + at // per, (at % per) * HD : (at % per + 1) * HD] = cg_ref[h, k : k + 1]
-
-
-def gate_up_whole_kernel(meta, a0, b0, a1, b1, a2, b2, a3, b3, gu_ref):
-    ctx = meta[0]
+        small_ref[at : at + 3 * CONV, h * HD : (h + 1) * HD] = cg_ref[h, : 3 * CONV]
+    at += 3 * CONV
+    small_ref[at : at + 1, :HD] = total[rows + PAD : rows + PAD + 1, :HD]
+
+
+def mixer_sum_kernel(meta, keep_ref, x_ref, y_ref, late_y_ref, late_x_ref, s0, s1, s2, s3, *outs, n_fsdp):
+    width, half = x_ref.shape[1:]
+    d_loc = width // n_fsdp
+    grouped = len(outs) < n_fsdp
+    small = (s0[...] + s1[...]) + (s2[...] + s3[...])
+    rows, lanes = iota((SMALL_ROWS, 2 * half), 0), iota((SMALL_ROWS, 2 * half), 1)
+    stats = jnp.sum(small, -1, keepdims=True)
+    high = stats.astype(BF16).astype(F32)
+    common = jnp.where(rows < WIDE_ROWS + 6, jnp.where(lanes < half + HD, high, stats - high), small[:, : 2 * half])
+    for r in range(n_fsdp):
+        shard = r if grouped else lax.rem(meta[1] + r, n_fsdp)
+        ref, first = (outs[0], r * (d_loc + SMALL_ROWS)) if grouped else (outs[r], 0)
+        at = pl.ds(r * d_loc if grouped else pl.multiple_of(shard * d_loc, d_loc), d_loc)
+        a = keep_ref[0, at, :].astype(F32) + x_ref[1, at, :].astype(F32) + late_y_ref[at, :].astype(F32)
+        b = keep_ref[1, at, :].astype(F32) + y_ref[1, at, :].astype(F32) + late_x_ref[at, :].astype(F32)
+        ref[first : first + d_loc, :half] = a.astype(BF16)
+        ref[first : first + d_loc, half:] = b.astype(BF16)
+        slices = [small[:, k * d_loc : (k + 1) * d_loc] for k in ([r] if grouped else range(n_fsdp))]
+        mine = slices[0]
+        for k in range(1, len(slices)):
+            mine = jnp.where(shard == k, slices[k], mine)
+        mine = jnp.concatenate([mine, jnp.zeros((SMALL_ROWS, 2 * half - d_loc), F32)], -1)
+        ref[first + d_loc : first + d_loc + SMALL_ROWS] = jnp.where(rows < WIDE_ROWS, mine, common).astype(BF16)
+
+
+def mixer_total_kernel(meta, own_ref, *refs, width):
+    far, (mix_ref, first_ref, second_ref, beta_ref, conv_ref, head_ref, rms_ref) = refs[:-7], refs[-7:]
+    count, rows = len(far) + 1, mix_ref.shape[0]
+    heads, hd_loc = conv_ref.shape[1:]
+    total = None
+    for f in range(count):
+        part = own_ref[...]
+        for r, ref in enumerate(far):
+            part = jnp.where(lax.rem(meta[1] + count - (r + 1), count) == f, ref[...], part)
+        part = part.astype(F32)
+        total = part if total is None else total + part
+    mix_ref[...] = total[:rows].astype(BF16)
+    small = total[rows:]
+    first_ref[...] = small[0:1, :rows]
+    second_ref[...] = small[1:2, :rows]
+    beta_ref[...] = small[:8, :rows].T[:, 2 : 2 + heads]
+    for h in range(heads):
+        lanes = small[WIDE_ROWS + 6 :, h * HD : (h + 1) * HD]
+        mine = lanes[:, :hd_loc]
+        for k in range(1, HD // hd_loc):
+            mine = jnp.where(meta[1] == k, lanes[:, k * hd_loc : (k + 1) * hd_loc], mine)
+        conv_ref[:, h, :] = mine[: 3 * CONV]
+        if h == 0:
+            head_ref[...] = mine[3 * CONV : 3 * CONV + 1]
+    stats = small[WIDE_ROWS : WIDE_ROWS + 6, 2 * HD : 2 * HD + 1] + small[WIDE_ROWS : WIDE_ROWS + 6, 3 * HD : 3 * HD + 1]
+    rms_ref[...] = jnp.sqrt(stats[:5] / (stats[5:] * width))
+
+
+def gate_up_whole_kernel(p_ref, d0, d1, e0, e1, gu_ref, down_ref):
     units = gu_ref.shape[2]
-    side = GU_BLOCKS // 2
-    for q in range(4):
-        for j, pair in enumerate(((a0, b0), (a1, b1), (a2, b2), (a3, b3))):
-
-            @pl.when(ctx ^ j == q)
-            def _(pair=pair, q=q):
-                for k in range(GU_BLOCKS):
-                    at = (q * GU_BLOCKS + k) * HD
-                    if at < 2 * units:
-                        block = pair[k // side][:, k % side * HD : (k % side + 1) * HD]
-                        gu_ref[at // units, :, at % units : at % units + HD] = block.astype(F32)
+    down_ref[: d0.shape[0]] = d0[...].astype(F32) + d1[...].astype(F32)
+    down_ref[d0.shape[0] :] = e0[...].astype(F32) + e1[...].astype(F32)
+    for q in range(p_ref.shape[0]):
+        for k in range(GU_BLOCKS):
+            at = (q * GU_BLOCKS + k) * HD
+            if at < 2 * units:
+                gu_ref[at // units, :, at % units : at % units + HD] = p_ref[q, :, k * HD : (k + 1) * HD].astype(F32)
 
 
 def mixer_whole_kernel(meta, p0, p1, p2, p3, qkv_ref, out_ref):
@@ -554,7 +608,7 @@
 
 
 def far_shards(value):
-    count, here = lax.axis_size("fsdp"), lax.axis_index("fsdp")
+    count = lax.axis_size("fsdp")
     if count <= 4:
         turns = [[(s, (s + r) % count) for s in range(count)] for r in range(1, count)]
         return [lax.ppermute(value, "fsdp", turn)[None] for turn in turns]
@@ -568,44 +622,6 @@
 def other(value, r):
     count, here = lax.axis_size("fsdp"), lax.axis_index("fsdp")
     return lax.dynamic_index_in_dim(value, (here + count - r) % count, 0)
-
-
-def scatter_sum(halves):
-    count, here = lax.axis_size("fsdp"), lax.axis_index("fsdp")
-    if count > 4:
-        return lax.psum_scatter(jnp.concatenate(halves, -1), "fsdp", scatter_dimension=0, tiled=True)
-    value = jnp.concatenate(halves, -1)
-    rows = value.shape[0] // count
-    total = lax.dynamic_slice_in_dim(value, here * rows, rows, 0).astype(F32)
-    for r in range(1, count):
-        part = lax.dynamic_slice_in_dim(value, (here + r) % count * rows, rows, 0)
-        total = total + lax.ppermute(part, "fsdp", [(s, (s + r) % count) for s in range(count)]).astype(F32)
-    return total.astype(BF16)
-
-
-def plane_gather(a, b):
-    a1, b2 = swapped(a, "ctx", 1), swapped(b, "ctx", 2)
-    b1, a2 = swapped(b, "ctx", 1), swapped(a, "ctx", 2)
-    return [(a1, b1), (a2, b2), (swapped(a1, "ctx", 2), swapped(b2, "ctx", 1))]
-
-
-def in_order(pieces):
-    here = lax.axis_index("ctx")
-    stacked = jnp.stack(pieces)
-    return [lax.dynamic_index_in_dim(stacked, here ^ k, 0, False) for k in range(len(pieces))]
-
-
-def plane_sum(pieces):
-    return (pieces[0].astype(F32) + pieces[1].astype(F32)) + (pieces[2].astype(F32) + pieces[3].astype(F32))
-
-
-def butterfly(value):
-    for axis in ("ctx", "fsdp"):
-        mask = 1
-        while mask < lax.axis_size(axis):
-            value = value + swapped(value, axis, mask)
-            mask *= 2
-    return value
 
 
 def local(
@@ -630,22 +646,25 @@
     out_part = lax.dynamic_slice_in_dim(out_weight, ctx * HD, HD, 0).T
     pack = jnp.concatenate([qkv_part, small])
     packs = lax.all_gather(pack, "fsdp", axis=0)
-    pack_far = [others(packs)] if n_fsdp > 4 else [other(packs, r) for r in range(1, n_fsdp)]
+    pack_far = others(packs)
     out_local = out_weight.T
-    out_part, gate_up_weight, _ = lax.optimization_barrier((out_part, gate_up_weight, packs))
-    out_far = far_shards(out_part)
     gu_local = jnp.concatenate(
         [gate_up_weight[0], gate_up_weight[1], jnp.zeros((d_loc, n_ctx * step - 2 * units), BF16)], -1
     )
-    gu_own = lax.all_gather(lax.dynamic_slice_in_dim(gu_local, ctx * step, step, 1), "fsdp", axis=0)
+    gu_part = lax.dynamic_slice_in_dim(gu_local, ctx * step, step, 1)
+    gu_own = lax.all_gather(gu_part, "fsdp", axis=0)
+    gu_far = others(gu_own)
     down_full = lax.all_gather(down_weight, "fsdp", axis=1, tiled=True)
     x_ext = jnp.concatenate([shifted(tokens[rows - PAD :], "ctx", 1), tokens])
 
-    one = [swapped(p, "ctx", 1) for p in pack_far]
-    two = [swapped(p, "ctx", 2) for p in pack_far]
-    three = [swapped(two[k], "ctx", 1) if k % 2 else swapped(one[k], "ctx", 2) for k in range(len(pack_far))]
+    cut = 3 * d_loc // 2
+    pack_far, out_part = lax.optimization_barrier((pack_far, out_part))
+    one, two = swapped(pack_far, "ctx", 1), swapped(pack_far, "ctx", 2)
+    out_far = far_shards(out_part)
+    three_a, three_b = swapped(one[:, :cut], "ctx", 2), swapped(two[:, cut:], "ctx", 1)
+    three_a, three_b, out_far = lax.optimization_barrier((three_a, three_b, out_far))
     out_far = jnp.concatenate(out_far)
-    out_pieces = [out_far] + [swapped(out_far, "ctx", j) for j in range(1, n_ctx)]
+    out_pieces = [swapped(out_far, "ctx", j) for j in range(1, n_ctx)]
 
     flat = packs[:, 3 * d_loc :].reshape(n_fsdp, -1)
     at = 0
@@ -661,7 +680,7 @@
     conv_full = conv_full.transpose(3, 1, 2, 0, 4).reshape(heads, 3, CONV, HD).astype(F32)
 
     qkv_full, pre, acts, turned, solved, ends_map, normed_t, normed_far, beta = call(
-        functools.partial(terms_kernel, lengths=n_len, n_fsdp=n_fsdp, n_blocks=len(pack_far)),
+        functools.partial(terms_kernel, lengths=n_len, n_fsdp=n_fsdp, cut=cut),
         "delta_terms",
         (
             sds(heads, 3, width, HD, dtype=BF16),
@@ -674,15 +693,14 @@
             sds(width, PAD, dtype=BF16),
             sds(rows, HD),
         ),
-        [SMEM] + [VMEM] * 4 + [ANY] * (2 + 4 * len(pack_far)),
-        (meta, x_ext, first_gain, beta_full, conv_full, qkv_weight, pack, *pack_far, *one, *two, *three),
+        [SMEM] + [VMEM] * 4 + [ANY] * 6,
+        (meta, x_ext, first_gain, beta_full, conv_full, qkv_weight, packs, one, two, three_a, three_b),
         [pltpu.SemaphoreType.DMA],
         gflops=15,
         mbytes=8,
     )
     arrived = [swapped(ends_map, "ctx", j) for j in range(1, n_ctx)]
-    gu_far, _ = lax.optimization_barrier((others(gu_own), ends_map))
-    gu_one, gu_two = swapped(gu_far, "ctx", 1), swapped(gu_far, "ctx", 2)
+    gu_one, gu_two = lax.optimization_barrier((swapped(gu_far, "ctx", 1), swapped(gu_far, "ctx", 2)))
     gu_three = (swapped(gu_one[:, :, : step // 2], "ctx", 2), swapped(gu_two[:, :, step // 2 :], "ctx", 1))
     out_full, mixed, fresh, state, head_out, attn_part = call(
         functools.partial(output_kernel, lengths=n_len, sources=n_ctx - 1, n_fsdp=n_fsdp),
@@ -695,8 +713,8 @@
             sds(rows, heads * HD, dtype=BF16),
             sds(rows, width),
         ),
-        [SMEM] + [VMEM] * 3 + [ANY] * (2 + n_ctx) + [VMEM] * len(arrived),
-        (meta, solved, acts, head_full, out_local, out_part, *out_pieces, *arrived),
+        [SMEM] + [VMEM] * 3 + [ANY] * (1 + n_ctx) + [VMEM] * len(arrived),
+        (meta, solved, acts, head_full, out_local, out_far, *out_pieces, *arrived),
         [pltpu.SemaphoreType.DMA],
         gflops=6,
         mbytes=6,
@@ -724,6 +742,20 @@
         mbytes=14,
     )
     mlp_other = swapped(mlp_part, "tp", 1)
+    quarter = sds(width, step // 2, dtype=BF16)
+    double = sds(2, width, step // 2, dtype=BF16)
+    gu_grads = call(
+        mlp_grads_kernel,
+        "mlp_grads",
+        (quarter,) * 6 + (double, sds(units, width, dtype=BF16)),
+        [VMEM] * 4,
+        (normed_mid_t, g_gu, act_t, g_ffn),
+        gflops=4,
+        mbytes=12,
+    )
+    mlp_other, gu_grads = lax.optimization_barrier((mlp_other, gu_grads))
+    gu_x3, gu_y3, gu_x1, gu_y2, gu_late_x, gu_late_y, gu_keep, down_grad = gu_grads
+    from_x3, from_y3 = swapped(gu_x3, "ctx", 1), swapped(gu_y3, "ctx", 2)
 
     result, g_middle, out_grads, d_mixed, d_fresh, d_state, sums = call(
         functools.partial(middle_kernel, lengths=n_len),
@@ -747,22 +779,16 @@
     )
     behind = [swapped(d_state, "ctx", j) for j in range(1, n_ctx)]
 
-    normed_mid_t, g_gu, g_ffn, _ = lax.optimization_barrier((normed_mid_t, g_gu, g_ffn, d_state))
-    quarter = sds(width, step // 2, dtype=BF16)
-    double = sds(2, width, step // 2, dtype=BF16)
-    gu_x, gu_y, gu_late_x, gu_late_y, gu_keep, down_grad = call(
-        mlp_grads_kernel,
-        "mlp_grads",
-        (double, double, quarter, quarter, double, sds(units, width, dtype=BF16)),
-        [VMEM] * 4,
-        (normed_mid_t, g_gu, act_t, g_ffn),
-        gflops=4,
-        mbytes=12,
-    )
     down_sh = lax.psum_scatter(down_grad, "fsdp", scatter_dimension=1, tiled=True)
-    behind, gu_x, gu_y = lax.optimization_barrier((behind, gu_x, gu_y))
-    from_x, from_y = swapped(gu_x, "ctx", 1), swapped(gu_y, "ctx", 2)
-
+
+    def add(left, right):
+        return (left.astype(F32) + right.astype(F32)).astype(BF16)
+
+    gu_x1, gu_y2, _ = lax.optimization_barrier((gu_x1, gu_y2, d_state))
+    from_x1, from_y2 = swapped(gu_x1, "ctx", 1), swapped(gu_y2, "ctx", 2)
+    gu_late_y, gu_late_x = add(gu_late_y, from_x3), add(gu_late_x, from_y3)
+    behind, gu_late_x, gu_late_y = lax.optimization_barrier((behind, gu_late_x, gu_late_y))
+    gu_late_y, gu_late_x = swapped(gu_late_y, "ctx", 2), swapped(gu_late_x, "ctx", 1)
     half = sds(width, 2 * HD, dtype=BF16)
     double = sds(2, width, 2 * HD, dtype=BF16)
     back = call(
@@ -778,71 +804,82 @@
         mbytes=16,
     )
 
-    def add(left, right):
-        return (left.astype(F32) + right.astype(F32)).astype(BF16)
-
-    from_x, from_y, back = lax.optimization_barrier((from_x, from_y, back))
     mix_keep, mix_x, mix_y, mix_late_x, mix_late_y, in_part, beta_grad, conv_grad = back
-    gu_late_y, gu_late_x = add(gu_late_y, from_x[0]), add(gu_late_x, from_y[0])
-    rim = shifted(in_part[rows:ext], "ctx", -1)
-    gu_late_y, gu_late_x, mix_x, mix_y = lax.optimization_barrier((gu_late_y, gu_late_x, mix_x, mix_y))
-    gu_late_y, gu_late_x = swapped(gu_late_y, "ctx", 2), swapped(gu_late_x, "ctx", 1)
+    from_x1, from_y2, gu_late_x, gu_late_y, mix_keep, down_sh = lax.optimization_barrier(
+        (from_x1, from_y2, gu_late_x, gu_late_y, mix_keep, down_sh)
+    )
+    in_other = swapped(in_part, "tp", 1)
+    rim = shifted(in_part[rows:ext] + in_other[rows:ext], "ctx", -1)
     mix_from_x, mix_from_y = swapped(mix_x, "ctx", 1), swapped(mix_y, "ctx", 2)
-    in_other = swapped(in_part, "tp", 1)
-    gu_sum = [
-        (gu_keep[0].astype(F32) + from_x[1].astype(F32) + gu_late_y.astype(F32)).astype(BF16),
-        (gu_keep[1].astype(F32) + from_y[1].astype(F32) + gu_late_x.astype(F32)).astype(BF16),
-    ]
-    gu_sh = lax.psum_scatter(jnp.concatenate(gu_sum, -1), "fsdp", scatter_dimension=0, tiled=True)
-
-    mix_late_y, mix_late_x = add(mix_late_y, mix_from_x[0]), add(mix_late_x, mix_from_y[0])
-    mix_late_y, mix_late_x, down_sh = lax.optimization_barrier((mix_late_y, mix_late_x, down_sh))
-    mix_late_y, mix_late_x = swapped(mix_late_y, "ctx", 2), swapped(mix_late_x, "ctx", 1)
-    side = units // 2
-    down_a, down_b = down_sh[:side], down_sh[side:]
-    down_a, down_b = add(down_a, swapped(down_a, "ctx", 1)), add(down_b, swapped(down_b, "ctx", 2))
-    mix_sum = [
-        (mix_keep[0].astype(F32) + mix_from_x[1].astype(F32) + mix_late_y.astype(F32)).astype(BF16),
-        (mix_keep[1].astype(F32) + mix_from_y[1].astype(F32) + mix_late_x.astype(F32)).astype(BF16),
-    ]
-    rim_other = swapped(rim, "tp", 1)
-    mix_sum, down_a, down_b, rim, rim_other = lax.optimization_barrier((mix_sum, down_a, down_b, rim, rim_other))
-    mix_sh = scatter_sum(mix_sum)
-    down_out = jnp.concatenate(
-        [
-            down_a.astype(F32) + swapped(down_a, "ctx", 2).astype(F32),
-            down_b.astype(F32) + swapped(down_b, "ctx", 1).astype(F32),
-        ]
-    )
-
+    mix_from_x, mix_from_y, rim, down_sh = lax.optimization_barrier((mix_from_x, mix_from_y, rim, down_sh))
     input_grad, smalls = call(
         last_kernel,
         "input_back",
         (sds(rows, width), sds(SMALL_ROWS, width)),
-        [VMEM] * 11,
-        (tokens, first_gain, in_part, in_other, rim, rim_other, g_middle, sums, stats, beta_grad, conv_grad),
+        [VMEM] * 10,
+        (tokens, first_gain, in_part, in_other, rim, g_middle, sums, stats, beta_grad, conv_grad),
         gflops=1,
         mbytes=6,
     )
-    smalls = butterfly(smalls)
-    mine = lax.dynamic_slice_in_dim(smalls[:6], fsdp * d_loc, d_loc, 1)
-    first_out, second_out, beta_out = mine[0], mine[1], mine[2 : 2 + heads].T
-    head_out_grad = lax.dynamic_slice_in_dim(smalls[12], fsdp * hd_loc, hd_loc)
-    conv_out = smalls[13 : 13 + heads * 3 * CONV * HD // width].reshape(heads, 3, CONV, HD)
-    conv_out = lax.dynamic_slice_in_dim(conv_out, fsdp * hd_loc, hd_loc, 3).transpose(1, 2, 0, 3)
-    stat = jnp.sum(smalls[6:12], -1)
-    rms = jnp.sqrt(stat[:5] / (stat[5] * width))
-
+    small_pieces = [smalls] + [swapped(smalls, "ctx", j) for j in range(1, n_ctx)]
+    gu_sum = [
+        (gu_keep[0].astype(F32) + from_x1.astype(F32) + gu_late_y.astype(F32)).astype(BF16),
+        (gu_keep[1].astype(F32) + from_y2.astype(F32) + gu_late_x.astype(F32)).astype(BF16),
+    ]
+    gu_sh = lax.psum_scatter(jnp.concatenate(gu_sum, -1), "fsdp", scatter_dimension=0, tiled=True)
+
+    mix_late_y, mix_late_x = add(mix_late_y, mix_from_x[0]), add(mix_late_x, mix_from_y[0])
+    mix_late_y, mix_late_x = lax.optimization_barrier((swapped(mix_late_y, "ctx", 2), swapped(mix_late_x, "ctx", 1)))
+    side = units // 2
+    down_a, down_b = down_sh[:side], down_sh[side:]
+    down_other = swapped(down_a, "ctx", 1), swapped(down_b, "ctx", 2)
+    count = n_fsdp if n_fsdp <= 4 else 1
+    mix_rows = n_fsdp // count * (d_loc + SMALL_ROWS)
+    mix_own, *mix_far = call(
+        functools.partial(mixer_sum_kernel, n_fsdp=n_fsdp),
+        "mixer_sum",
+        (sds(mix_rows, 4 * HD, dtype=BF16),) * count,
+        [SMEM] + [VMEM] * (5 + n_ctx),
+        (meta, mix_keep, mix_from_x, mix_from_y, mix_late_y, mix_late_x, *small_pieces),
+        gflops=1,
+        mbytes=6,
+    )
+    mix_own, down_other, gu_sh = lax.optimization_barrier((mix_own, down_other, gu_sh))
+    down_a, down_b = add(down_a, down_other[0]), add(down_b, down_other[1])
+    down_parts = (down_a, swapped(down_a, "ctx", 2), down_b, swapped(down_b, "ctx", 1))
+    gu_all = lax.all_gather(gu_sh, "ctx", axis=0)
+    if count > 1:
+        turns = [[(i, (i + r) % n_fsdp) for i in range(n_fsdp)] for r in range(1, n_fsdp)]
+        mix_far = [lax.ppermute(part, "fsdp", turn) for part, turn in zip(mix_far, turns, strict=True)]
+        mix_far, down_a, down_b = lax.optimization_barrier((mix_far, down_a, down_b))
+    else:
+        mix_own = lax.psum_scatter(mix_own, "fsdp", scatter_dimension=0, tiled=True)
+    mix_sh, first_out, second_out, beta_out, conv_out, head_out_grad, rms = call(
+        functools.partial(mixer_total_kernel, width=width),
+        "mixer_total",
+        (
+            sds(d_loc, 4 * HD, dtype=BF16),
+            sds(1, d_loc),
+            sds(1, d_loc),
+            sds(d_loc, heads),
+            sds(3 * CONV, heads, hd_loc),
+            sds(1, hd_loc),
+            sds(5, 1),
+        ),
+        [SMEM] + [VMEM] * count,
+        (meta, mix_own, *mix_far),
+        gflops=1,
+        mbytes=1,
+    )
     def pieces(part):
         return [part] + [swapped(part, "ctx", j) for j in range(1, n_ctx)]
 
-    gu_pairs = plane_gather(gu_sh[:, : step // 2], gu_sh[:, step // 2 :])
-    gu_out = call(
+    gu_out, down_out = call(
         gate_up_whole_kernel,
         "gate_up_whole",
-        sds(2, d_loc, units),
-        [SMEM] + [VMEM] * (2 * n_ctx),
-        (meta, gu_sh[:, : step // 2], gu_sh[:, step // 2 :], *[p for pair in gu_pairs for p in pair]),
+        (sds(2, d_loc, units), sds(units, d_loc)),
+        [VMEM] * 5,
+        (gu_all, *down_parts),
         gflops=1,
         mbytes=6,
     )
@@ -858,16 +895,16 @@
     return (
         result,
         input_grad,
-        first_out,
+        first_out.reshape(-1),
         qkv_out,
         beta_out,
-        conv_out,
-        head_out_grad,
+        conv_out.reshape(3, CONV, heads, hd_loc),
+        head_out_grad.reshape(-1),
         out_out,
-        second_out,
+        second_out.reshape(-1),
         gu_out,
         down_out,
-        rms,
+        rms.reshape(-1),
     )
 
 

time: 354 us -> 336 us (0.949)
  starting transfers between devices: 74.1 us -> 58.4 us
  local copies, waits for them, and re-layouts: 27.4 us -> 16.8 us
  waiting for transfers between devices: 122 us -> 113 us
  blocking collectives: 21.7 us -> 30.2 us
  Pallas kernels: 79.5 us -> 85.8 us
    ppermute x51 -> x40, waiting for transfers between devices: 112 us -> 81.8 us  [swapped(): lax.ppermute(value, axis, [(s, s ^ mask) for s in range(lax.axis_size(axi...]
    ppermute x3, waiting for transfers between devices: 0.01 us -> 16.6 us  [local(): lax.ppermute(part, 'fsdp', turn)]
    ppermute x51 -> x40, starting transfers between devices: 58.7 us -> 43.8 us  [swapped(): lax.ppermute(value, axis, [(s, s ^ mask) for s in range(lax.axis_size(axi...]
    reduce_scatter x1, waiting for transfers between devices: 0.01 us -> 9.25 us  [local(): lax.psum_scatter(down_grad, 'fsdp', scatter_dimension=1, tiled=True)]
    all_gather x1, blocking collectives: 21.7 us -> 30.2 us  [local(): packs = lax.all_gather(pack, 'fsdp', axis=0)]
    pallas_call x9 -> x11, Pallas kernels: 79.5 us -> 85.8 us  [call(): pl.pallas_call(body, name=name, in_specs=in_specs, out_specs=jax.tree.map...]
    unnamed x124 -> x109, local copies, waits for them, and re-layouts: 10.1 us -> 8.18 us
  transfers between devices with their start and end apart: 63 -> 53, of which waited for: 27 -> 26; matrix products, arithmetic and copies ran while one was open for 7% -> 6% of each run, Pallas kernels for 16% -> 21%
where the time goes in v1:
time: 336 us; the launch traced here: 330 us
  waiting for transfers between devices  113 us (34%)
  Pallas kernels  85.8 us (26%)
  starting transfers between devices  58.4 us (17%)
  blocking collectives  30.2 us (9%)
  local copies, waits for them, and re-layouts  16.8 us (5%)
  between operations  14.9 us (4%)
  other arithmetic  11.5 us (3%)
    pallas_call x11, Pallas kernels, call(): pl.pallas_call(body, name=name, in_specs=in_specs, out_specs=jax.tree.map...  85.8 us
    ppermute x40, waiting for transfers between devices, swapped(): lax.ppermute(value, axis, [(s, s ^ mask) for s in range(lax.axis_size(axi...  81.8 us
    ppermute x40, starting transfers between devices, swapped(): lax.ppermute(value, axis, [(s, s ^ mask) for s in range(lax.axis_size(axi...  43.8 us
    all_gather x1, blocking collectives, local(): packs = lax.all_gather(pack, 'fsdp', axis=0)  30.2 us
    ppermute x3, waiting for transfers between devices, local(): lax.ppermute(part, 'fsdp', turn)  16.6 us
    reduce_scatter x1, waiting for transfers between devices, local(): lax.psum_scatter(down_grad, 'fsdp', scatter_dimension=1, tiled=True)  9.25 us
    unnamed x109, local copies, waits for them, and re-layouts  8.18 us
  transfers between devices with their start and end apart: 53, of which 26 were waited for; matrix products, arithmetic and copies ran while one was open for 6% of the time, Pallas kernels for 21%

profile of v1, /device:TPU:0, one launch (start us, length us, event | category | flops | bytes accessed | tf_op | source)
XLA Modules:
  0.0 330.5 jit_solution(5561195721005828125)
XLA Ops:
  12.3 30.2 %all-gather = bf16[3200,128]{1,0:T(8,128)(2,1)S(1)} all-gather(bf16[800,128]{1,0:T(8,128)(2,1)S(1)} %pad_maximum_fusion.4), channel_id=2, replica_groups=mesh['fsdp'=4,'ctx'=4,'tp'=2] {'fsdp'}, dimensions={0}, use_global_device_ids=true | all-gather | bytes 1024000 | tf_op jit(solution)/shard_map/all_gather | solution.py:648
  42.7 4.4 %collective-permute-start.7 = (bf16[256,128]{1,0:T(8,128)(2,1)}, bf16[256,128]{1,0:T(8,128)(2,1)S(1)}, u32[]{:S(2)}, u32[]{:S(2)}) collective-permute-start(bf16[256,128]{1,0:T(8,128)(2,1)} %dynamic-slice_bitcast_fusion), channel_id=1, source_target_pairs={{0,24},{8,0},{16,8},{24,16},{1,25},{9,1},{17,9},{25,17},{2,26},{10... | collective-permute-start | bytes 196616 | tf_op jit(solution)/shard_map/ppermute | solution.py:614
  52.5 7.3 %collective-permute-done.2.refs_8_ = bf16[3,800,128]{2,1,0:T(8,128)(2,1)S(1)} collective-permute-done((bf16[3,800,128]{2,1,0:T(8,128)(2,1)S(1)}, bf16[3,800,128]{2,1,0:T(8,128)(2,1)S(1)}, u32[]{:S(2)}, u32[]{:S(2)}) %collective-permute-start.2) | collective-permute-done | bytes 614432 | tf_op jit(solution)/shard_map/ppermute | solution.py:607
  69.6 4.8 %collective-permute-done.5 = bf16[256,128]{1,0:T(8,128)(2,1)S(1)} collective-permute-done((bf16[256,128]{1,0:T(8,128)(2,1)}, bf16[256,128]{1,0:T(8,128)(2,1)S(1)}, u32[]{:S(2)}, u32[]{:S(2)}) %collective-permute-start.5) | collective-permute-done | bytes 65568 | tf_op jit(solution)/shard_map/ppermute | solution.py:614
  74.5 3.2 collective-permute-start.10
  78.4 11.9 %delta_terms.1 = (bf16[4,3,1024,128]{3,2,1,0:T(8,128)(2,1)}, bf16[4,3,264,128]{3,2,1,0:T(8,128)(2,1)}, bf16[4,3,256,128]{3,2,1,0:T(8,128)(2,1)}, f32[4,256,256]{...) custom-call(s32[6]{0:T(128)} %pad_add_fusion.refs_0_.meta, ...), custom_call_target="tpu_custom_call" | custom-call | flops 41400000512 | bytes 1000000 | tf_op jit(solution)/shard_map/delta_terms/pallas_call | solution.py:588
  90.3 2.9 collective-permute-start.13
  100.7 3.8 %collective-permute-done.12.refs_10_.refs_5_ = bf16[4,2,128,128]{3,2,1,0:T(8,128)(2,1)S(1)} collective-permute-done((bf16[4,2,128,128]{3,2,1,0:T(8,128)(2,1)}, bf16[4,2,128,128]{3,2,1,0:T(8,128)(2,1)S(1)}, u32[]{:S(2)}, u32[]{:S(2)}) %collective-permute-start.12) | collective-permute-done | bytes 262176 | tf_op jit(solution)/shard_map/ppermute | solution.py:607
  106.5 6.5 %delta_outputs.1 = (bf16[4,1024,128]{2,1,0:T(8,128)(2,1)}, f32[4,256,128]{2,1,0:T(8,128)}, f32[4,256,128]{2,1,0:T(8,128)}, f32[4,128,128]{2,1,0:T(8,128)}, bf16[...) custom-call(s32[6]{0:T(128)} %pad_add_fusion.refs_0_.meta, f32[4,256,256]{2,1,0:T(8,128)} %get-tuple-element.122.refs_1_.y_ref.refs_10_, ...), custom_call_target="tpu_custom_call" | custom-call | flops 22424999936 | bytes 1000000 | tf_op jit(solution)/shard_map/delta_outputs/pallas_call | solution.py:588
  113.0 12.6 %collective-permute-done.16.refs_9_ = bf16[3,256,768]{2,1,0:T(8,128)(2,1)S(1)} collective-permute-done((bf16[3,256,768]{2,1,0:T(8,128)(2,1)S(1)}, bf16[3,256,768]{2,1,0:T(8,128)(2,1)S(1)}, u32[]{:S(2)}, u32[]{:S(2)}) %collective-permute-start.16) | collective-permute-done | bytes 1179680 | tf_op jit(solution)/shard_map/ppermute | solution.py:607
  128.8 6.9 %collective-permute-done.18.refs_11_ = bf16[3,256,384]{2,1,0:T(8,128)(2,1)S(1)} collective-permute-done((bf16[3,256,384]{2,1,0:T(8,128)(2,1)S(1)}, bf16[3,256,384]{2,1,0:T(8,128)(2,1)S(1)}, u32[]{:S(2)}, u32[]{:S(2)}) %collective-permute-start.18) | collective-permute-done | bytes 589856 | tf_op jit(solution)/shard_map/ppermute | solution.py:607
  136.6 12.3 %mlp.1 = (f32[256,1024]{1,0:T(8,128)}, bf16[1024,256]{1,0:T(8,128)(2,1)}, bf16[1408,256]{1,0:T(8,128)(2,1)}, bf16[4,256,768]{2,1,0:T(8,128)(2,1)}, bf16[256,1024...) custom-call(s32[6]{0:T(128)} %pad_add_fusion.refs_0_.meta, bf16[256,1024]{1,0:T(8,128)(2,1)} %x_ref.1, ...), custom_call_target="tpu_custom_call" | custom-call | flops 42090000384 | bytes 1000000 | tf_op jit(solution)/shard_map/mlp/pallas_call | solution.py:588
  149.0 6.6 %mlp_grads.1 = (bf16[1024,384]{1,0:T(8,128)(2,1)}, bf16[1024,384]{1,0:T(8,128)(2,1)}, bf16[1024,384]{1,0:T(8,128)(2,1)}, bf16[1024,384]{1,0:T(8,128)(2,1)}, bf16...) custom-call(bf16[1024,256]{1,0:T(8,128)(2,1)} %get-tuple-element.132, ...), custom_call_target="tpu_custom_call" | custom-call | flops 22424999936 | bytes 1000000 | tf_op jit(solution)/shard_map/mlp_grads/pallas_call | solution.py:588
  159.1 9.7 %middle_back.1 = (bf16[256,1024]{1,0:T(8,128)(2,1)}, f32[256,1024]{1,0:T(8,128)}, bf16[4,1024,128]{2,1,0:T(8,128)(2,1)}, f32[4,256,128]{2,1,0:T(8,128)}, f32[4,2...) custom-call(s32[6]{0:T(128)} %pad_add_fusion.refs_0_.meta, ...), custom_call_target="tpu_custom_call" | custom-call | flops 33120000000 | bytes 1000000 | tf_op jit(solution)/shard_map/middle_back/pallas_call | solution.py:588
  172.5 3.9 %collective-permute-done.23 = bf16[1024,384]{1,0:T(8,128)(2,1)S(1)} collective-permute-done((bf16[1024,384]{1,0:T(8,128)(2,1)}, bf16[1024,384]{1,0:T(8,128)(2,1)S(1)}, u32[]{:S(2)}, u32[]{:S(2)}) %collective-permute-start.23) | collective-permute-done | bytes 786464 | tf_op jit(solution)/shard_map/ppermute | solution.py:607
  185.4 22.0 %delta_back.1 = (bf16[2,1024,256]{2,1,0:T(8,128)(2,1)}, bf16[2,1024,256]{2,1,0:T(8,128)(2,1)}, bf16[2,1024,256]{2,1,0:T(8,128)(2,1)}, bf16[1024,256]{1,0:T(8,128...) custom-call(s32[6]{0:T(128)} %pad_add_fusion.refs_0_.meta, ...), custom_call_target="tpu_custom_call" | custom-call | flops 75900002304 | bytes 1000000 | tf_op jit(solution)/shard_map/delta_back/pallas_call | solution.py:588
  210.2 7.6 %collective-permute-done.31 = bf16[1024,384]{1,0:T(8,128)(2,1)} collective-permute-done((bf16[1024,384]{1,0:T(8,128)(2,1)S(1)}, bf16[1024,384]{1,0:T(8,128)(2,1)}, u32[]{:S(2)}, u32[]{:S(2)}) %collective-permute-start.31) | collective-permute-done | bytes 786464 | tf_op jit(solution)/shard_map/ppermute | solution.py:607
  217.9 9.3 %reduce-scatter.3.cloned.1.call-done = bf16[1408,256]{1,0:T(8,128)(2,1)} async-done(((bf16[1408,1024]{1,0:T(8,128)(2,1)}), bf16[1408,256]{1,0:T(8,128)(2,1)}) %reduce-scatter.3.cloned.1.call-update) | async-done | bytes 720912 | tf_op jit(solution)/shard_map/reduce_scatter | solution.py:782
  232.6 7.4 %collective-permute-done.26.x_ref = bf16[2,1024,256]{2,1,0:T(8,128)(2,1)} collective-permute-done((bf16[2,1024,256]{2,1,0:T(8,128)(2,1)}, bf16[2,1024,256]{2,1,0:T(8,128)(2,1)}, u32[]{:S(2)}, u32[]{:S(2)}) %collective-permute-start.26) | collective-permute-done | bytes 1048608 | tf_op jit(solution)/shard_map/ppermute | solution.py:607
  244.2 3.7 %input_back.1 = (f32[256,1024]{1,0:T(8,128)}, f32[32,1024]{1,0:T(8,128)}) custom-call(bf16[256,1024]{1,0:T(8,128)(2,1)} %x_ref.1, f32[1,1024]{1,0:T(1,128)} %bitcast.67, f32[272,1024]{1,0:T(8,128)} %get-tuple-element.170.part_ref, f32[272,1024]{1,0:T(8,128)} %collective-permute-done.25.other_ref, f32[8,1024]{1,0:T(8,128)} %copy-done.49, ...), custom_call_target="tpu_custom_call" | custom-call | flops 12764999680 | bytes 1000000 | tf_op jit(solution)/shard_map/input_back/pallas_call | solution.py:588
  251.4 4.9 %collective-permute-done.34.late_x_ref = bf16[1024,256]{1,0:T(8,128)(2,1)S(1)} collective-permute-done((bf16[1024,256]{1,0:T(8,128)(2,1)S(1)}, bf16[1024,256]{1,0:T(8,128)(2,1)S(1)}, u32[]{:S(2)}, u32[]{:S(2)}) %collective-permute-start.34) | collective-permute-done | bytes 524320 | tf_op jit(solution)/shard_map/ppermute | solution.py:607
  256.6 4.9 %collective-permute-done.33.late_y_ref = bf16[1024,256]{1,0:T(8,128)(2,1)S(1)} collective-permute-done((bf16[1024,256]{1,0:T(8,128)(2,1)S(1)}, bf16[1024,256]{1,0:T(8,128)(2,1)S(1)}, u32[]{:S(2)}, u32[]{:S(2)}) %collective-permute-start.33) | collective-permute-done | bytes 524320 | tf_op jit(solution)/shard_map/ppermute | solution.py:607
  265.6 3.6 %mixer_sum.1 = (bf16[288,512]{1,0:T(8,128)(2,1)}, bf16[288,512]{1,0:T(8,128)(2,1)}, bf16[288,512]{1,0:T(8,128)(2,1)}, bf16[288,512]{1,0:T(8,128)(2,1)}) custom-call(s32[6]{0:T(128)} %pad_add_fusion.refs_0_.meta, bf16[2,1024,256]{2,1,0:T(8,128)(2,1)} %get-tuple-element.188.keep_ref, bf16[2,1024,256]{2,1,0:T(8,128)(2,1)} %collective-permute-done.26.x_ref, ...), custom_call_target="tpu_custom_call" | custom-call | flops 12074999808 | bytes 1000000 | tf_op jit(solution)/shard_map/mixer_sum/pallas_call | solution.py:588
  272.6 2.8 collective-permute-start.42
  275.7 6.7 %collective-permute-done.40.refs_0_ = bf16[288,512]{1,0:T(8,128)(2,1)S(1)} collective-permute-done((bf16[288,512]{1,0:T(8,128)(2,1)}, bf16[288,512]{1,0:T(8,128)(2,1)S(1)}, u32[]{:S(2)}, u32[]{:S(2)}) %collective-permute-start.40) | collective-permute-done | bytes 294944 | tf_op jit(solution)/shard_map/ppermute | solution.py:853
  282.3 10.0 %collective-permute-done.41.refs_1_ = bf16[288,512]{1,0:T(8,128)(2,1)S(1)} collective-permute-done((bf16[288,512]{1,0:T(8,128)(2,1)}, bf16[288,512]{1,0:T(8,128)(2,1)S(1)}, u32[]{:S(2)}, u32[]{:S(2)}) %collective-permute-start.41) | collective-permute-done | bytes 294944 | tf_op jit(solution)/shard_map/ppermute | solution.py:853
  293.1 2.7 mixer_total.1
  304.1 2.8 collective-permute-done.45.p3
  306.9 4.4 %collective-permute-done.44.p2 = bf16[256,512]{1,0:T(8,128)(2,1)S(1)} collective-permute-done((bf16[256,512]{1,0:T(8,128)(2,1)}, bf16[256,512]{1,0:T(8,128)(2,1)S(1)}, u32[]{:S(2)}, u32[]{:S(2)}) %collective-permute-start.44) | collective-permute-done | bytes 262176 | tf_op jit(solution)/shard_map/ppermute | solution.py:607
  312.8 2.9 mixer_whole.1
  315.7 2.9 collective-permute-done.47.e1
  319.5 4.0 %gate_up_whole.1 = (f32[2,256,1408]{2,1,0:T(8,128)}, f32[1408,256]{1,0:T(8,128)}) custom-call(bf16[4,256,768]{2,1,0:T(8,128)(2,1)} %bitcast.71, bf16[704,256]{1,0:T(8,128)(2,1)} %copy-done.11, bf16[704,256]{1,0:T(8,128)(2,1)} %copy-done.31, bf16[704,256]{1,0:T(8,128)(2,1)} %copy-done.10, bf16[704,256]{1,0:T(8,128)(2,1)} %copy-done.30), custom_call_target="tpu_custom_call" | custom-call | flops 11384999936 | bytes 1000000 | tf_op jit(solution)/shard_map/gate_up_whole/pallas_call | solution.py:588
  (244 shorter events, 86.0 us)
Async XLA Ops:
  7.2 86.7 %all-gather.9.cloned.1.call-start = ((), (), s32[]{:S(2)}) async-start(), calls=%async_computation.5 | async-start | bytes 1966080 | tf_op jit(solution)/shard_map/all_gather | solution.py:655
  9.9 126.7 %all-gather.7.cloned.1.call-start = ((), (), s32[]{:S(2)}) async-start(), calls=%async_computation.2 | async-start | bytes 3604480 | tf_op jit(solution)/shard_map/all_gather | solution.py:657
  42.7 27.0 %collective-permute-start.7 = (bf16[256,128]{1,0:T(8,128)(2,1)}, bf16[256,128]{1,0:T(8,128)(2,1)S(1)}, u32[]{:S(2)}, u32[]{:S(2)}) collective-permute-start(bf16[256,128]{1,0:T(8,128)(2,1)} %dynamic-slice_bitcast_fusion), channel_id=1, source_target_pairs={{0,24},{8,0},{16,8},{24,16},{1,25},{9,1},{17,9},{25,17},{2,26},{10... | collective-permute-start | bytes 196616 | tf_op jit(solution)/shard_map/ppermute | solution.py:614
  47.0 22.6 %collective-permute-start.6 = (bf16[256,128]{1,0:T(8,128)(2,1)}, bf16[256,128]{1,0:T(8,128)(2,1)S(1)}, u32[]{:S(2)}, u32[]{:S(2)}) collective-permute-start(bf16[256,128]{1,0:T(8,128)(2,1)} %dynamic-slice_bitcast_fusion), channel_id=1, source_target_pairs={{0,16},{8,24},{16,0},{24,8},{1,17},{9,25},{17,1},{25,9},{2,18},{10... | collective-permute-start | bytes 196616 | tf_op jit(solution)/shard_map/ppermute | solution.py:614
  48.4 14.8 %collective-permute-start.1 = (bf16[3,800,128]{2,1,0:T(8,128)(2,1)S(1)}, bf16[3,800,128]{2,1,0:T(8,128)(2,1)S(1)}, u32[]{:S(2)}, u32[]{:S(2)}) collective-permute-start(bf16[3,800,128]{2,1,0:T(8,128)(2,1)S(1)} %pad_maximum_fusion.2), channel_id=1, source_target_pairs={{0,2},{2,0},{4,6},{6,4},{1,3},{3,1},{5,7},{7,5},{8,10},{10,8},{12,... | collective-permute-start | bytes 1843208 | tf_op jit(solution)/shard_map/ppermute | solution.py:607
  49.9 17.8 %collective-permute-start = (bf16[8,1024]{1,0:T(8,128)(2,1)S(1)}, bf16[8,1024]{1,0:T(8,128)(2,1)S(1)}, u32[]{:S(2)}, u32[]{:S(2)}) collective-permute-start(bf16[8,1024]{1,0:T(8,128)(2,1)S(1)} %slice.63), channel_id=1, source_target_pairs={{0,2},{2,4},{4,6},{1,3},{3,5},{5,7},{8,10},{10,12},{12,14},{9,11},... | collective-permute-start | bytes 49160 | tf_op jit(solution)/shard_map/ppermute | solution.py:603
  52.4 174.8 %reduce-scatter.3.cloned.1.call-start = ((), (), s32[]{:S(2)}) async-start(), calls=%async_computation.3 | async-start | bytes 3604480 | tf_op jit(solution)/shard_map/reduce_scatter | solution.py:782
  59.9 14.6 %collective-permute-start.4 = (bf16[3,416,128]{2,1,0:T(8,128)(2,1)S(1)}, bf16[3,416,128]{2,1,0:T(8,128)(2,1)}, u32[]{:S(2)}, u32[]{:S(2)}) collective-permute-start(bf16[3,416,128]{2,1,0:T(8,128)(2,1)S(1)} %slice.89), channel_id=1, source_target_pairs={{0,2},{2,0},{4,6},{6,4},{1,3},{3,1},{5,7},{7,5},{8,10},{10,8},{12,... | collective-permute-start | bytes 958472 | tf_op jit(solution)/shard_map/ppermute | solution.py:607
  74.5 18.7 %collective-permute-start.10 = (bf16[3,256,128]{2,1,0:T(8,128)(2,1)S(1)}, bf16[3,256,128]{2,1,0:T(8,128)(2,1)S(1)}, u32[]{:S(2)}, u32[]{:S(2)}) collective-permute-start(bf16[3,256,128]{2,1,0:T(8,128)(2,1)S(1)} %constant_dynamic-update-slice_fusion.refs_5_), channel_id=1, source_target_pairs={{0,6},{2,4},{4,2},{6,0},{1,7},{3,5},{5,3},{7,1},{8,14},{10,12},{12... | collective-permute-start | bytes 589832 | tf_op jit(solution)/shard_map/ppermute | solution.py:607
  77.7 17.6 %collective-permute-start.9 = (bf16[3,256,128]{2,1,0:T(8,128)(2,1)S(1)}, bf16[3,256,128]{2,1,0:T(8,128)(2,1)S(1)}, u32[]{:S(2)}, u32[]{:S(2)}) collective-permute-start(bf16[3,256,128]{2,1,0:T(8,128)(2,1)S(1)} %constant_dynamic-update-slice_fusion.refs_5_), channel_id=1, source_target_pairs={{0,4},{2,6},{4,0},{6,2},{1,5},{3,7},{5,1},{7,3},{8,12},{10,14},{12... | collective-permute-start | bytes 589832 | tf_op jit(solution)/shard_map/ppermute | solution.py:607
  77.7 19.2 %collective-permute-start.8 = (bf16[3,256,128]{2,1,0:T(8,128)(2,1)S(1)}, bf16[3,256,128]{2,1,0:T(8,128)(2,1)}, u32[]{:S(2)}, u32[]{:S(2)}) collective-permute-start(bf16[3,256,128]{2,1,0:T(8,128)(2,1)S(1)} %constant_dynamic-update-slice_fusion.refs_5_), channel_id=1, source_target_pairs={{0,2},{2,0},{4,6},{6,4},{1,3},{3,1},{5,7},{7,5},{8,10},{10,8},{12,... | collective-permute-start | bytes 589832 | tf_op jit(solution)/shard_map/ppermute | solution.py:607
  95.4 30.3 %collective-permute-start.16 = (bf16[3,256,768]{2,1,0:T(8,128)(2,1)S(1)}, bf16[3,256,768]{2,1,0:T(8,128)(2,1)S(1)}, u32[]{:S(2)}, u32[]{:S(2)}) collective-permute-start(bf16[3,256,768]{2,1,0:T(8,128)(2,1)S(1)} %pad_maximum_fusion.1), channel_id=1, source_target_pairs={{0,4},{2,6},{4,0},{6,2},{1,5},{3,7},{5,1},{7,3},{8,12},{10,14},{12... | collective-permute-start | bytes 3538952 | tf_op jit(solution)/shard_map/ppermute | solution.py:607
  96.9 28.7 %collective-permute-start.15 = (bf16[3,256,768]{2,1,0:T(8,128)(2,1)S(1)}, bf16[3,256,768]{2,1,0:T(8,128)(2,1)S(1)}, u32[]{:S(2)}, u32[]{:S(2)}) collective-permute-start(bf16[3,256,768]{2,1,0:T(8,128)(2,1)S(1)} %pad_maximum_fusion.1), channel_id=1, source_target_pairs={{0,2},{2,0},{4,6},{6,4},{1,3},{3,1},{5,7},{7,5},{8,10},{10,8},{12,... | collective-permute-start | bytes 3538952 | tf_op jit(solution)/shard_map/ppermute | solution.py:607
  113.0 15.9 %collective-permute-start.14 = (f32[256,1024]{1,0:T(8,128)}, f32[256,1024]{1,0:T(8,128)S(1)}, u32[]{:S(2)}, u32[]{:S(2)}) collective-permute-start(f32[256,1024]{1,0:T(8,128)} %get-tuple-element.128.refs_2_), channel_id=1, source_target_pairs={{0,1},{1,0},{2,3},{3,2},{4,5},{5,4},{6,7},{7,6},{8,9},{9,8},{10,11... | collective-permute-start | bytes 3145736 | tf_op jit(solution)/shard_map/ppermute | solution.py:607
  155.6 20.8 %collective-permute-start.23 = (bf16[1024,384]{1,0:T(8,128)(2,1)}, bf16[1024,384]{1,0:T(8,128)(2,1)S(1)}, u32[]{:S(2)}, u32[]{:S(2)}) collective-permute-start(bf16[1024,384]{1,0:T(8,128)(2,1)} %get-tuple-element.152), channel_id=1, source_target_pairs={{0,4},{2,6},{4,0},{6,2},{1,5},{3,7},{5,1},{7,3},{8,12},{10,14},{12... | collective-permute-start | bytes 2359304 | tf_op jit(solution)/shard_map/ppermute | solution.py:607
  157.8 20.7 %collective-permute-start.24 = (bf16[1024,384]{1,0:T(8,128)(2,1)}, bf16[1024,384]{1,0:T(8,128)(2,1)}, u32[]{:S(2)}, u32[]{:S(2)}) collective-permute-start(bf16[1024,384]{1,0:T(8,128)(2,1)} %get-tuple-element.154), channel_id=1, source_target_pairs={{0,2},{2,0},{4,6},{6,4},{1,3},{3,1},{5,7},{7,5},{8,10},{10,8},{12,... | collective-permute-start | bytes 2359304 | tf_op jit(solution)/shard_map/ppermute | solution.py:607
  172.4 97.8 %reduce-scatter.5.cloned.1.call-start = ((), (), s32[]{:S(2)}) async-start(), calls=%async_computation.4 | async-start | bytes 1966080 | tf_op jit(solution)/shard_map/reduce_scatter | solution.py:829
  176.4 31.1 %collective-permute-start.29 = (bf16[1024,384]{1,0:T(8,128)(2,1)}, bf16[1024,384]{1,0:T(8,128)(2,1)S(1)}, u32[]{:S(2)}, u32[]{:S(2)}) collective-permute-start(bf16[1024,384]{1,0:T(8,128)(2,1)} %get-tuple-element.175), channel_id=1, source_target_pairs={{0,2},{2,0},{4,6},{6,4},{1,3},{3,1},{5,7},{7,5},{8,10},{10,8},{12,... | collective-permute-start | bytes 2359304 | tf_op jit(solution)/shard_map/ppermute | solution.py:607
  178.5 29.8 %collective-permute-start.30 = (bf16[1024,384]{1,0:T(8,128)(2,1)S(1)}, bf16[1024,384]{1,0:T(8,128)(2,1)S(1)}, u32[]{:S(2)}, u32[]{:S(2)}) collective-permute-start(bf16[1024,384]{1,0:T(8,128)(2,1)S(1)} %copy-done.26), channel_id=1, source_target_pairs={{0,4},{2,6},{4,0},{6,2},{1,5},{3,7},{5,1},{7,3},{8,12},{10,14},{12... | collective-permute-start | bytes 2359304 | tf_op jit(solution)/shard_map/ppermute | solution.py:607
  184.0 33.8 %collective-permute-start.31 = (bf16[1024,384]{1,0:T(8,128)(2,1)S(1)}, bf16[1024,384]{1,0:T(8,128)(2,1)}, u32[]{:S(2)}, u32[]{:S(2)}) collective-permute-start(bf16[1024,384]{1,0:T(8,128)(2,1)S(1)} %add_convert_fusion.1), channel_id=1, source_target_pairs={{0,2},{2,0},{4,6},{6,4},{1,3},{3,1},{5,7},{7,5},{8,10},{10,8},{12,... | collective-permute-start | bytes 2359304 | tf_op jit(solution)/shard_map/ppermute | solution.py:607
  185.3 32.5 %collective-permute-start.32 = (bf16[1024,384]{1,0:T(8,128)(2,1)S(1)}, bf16[1024,384]{1,0:T(8,128)(2,1)}, u32[]{:S(2)}, u32[]{:S(2)}) collective-permute-start(bf16[1024,384]{1,0:T(8,128)(2,1)S(1)} %add_convert_fusion), channel_id=1, source_target_pairs={{0,4},{2,6},{4,0},{6,2},{1,5},{3,7},{5,1},{7,3},{8,12},{10,14},{12... | collective-permute-start | bytes 2359304 | tf_op jit(solution)/shard_map/ppermute | solution.py:607
  207.4 23.0 %collective-permute-start.25 = (f32[272,1024]{1,0:T(8,128)}, f32[272,1024]{1,0:T(8,128)}, u32[]{:S(2)}, u32[]{:S(2)}) collective-permute-start(f32[272,1024]{1,0:T(8,128)} %get-tuple-element.170.part_ref), channel_id=1, source_target_pairs={{0,1},{1,0},{2,3},{3,2},{4,5},{5,4},{6,7},{7,6},{8,9},{9,8},{10,11... | collective-permute-start | bytes 3342344 | tf_op jit(solution)/shard_map/ppermute | solution.py:607
  207.5 32.5 %collective-permute-start.26 = (bf16[2,1024,256]{2,1,0:T(8,128)(2,1)}, bf16[2,1024,256]{2,1,0:T(8,128)(2,1)}, u32[]{:S(2)}, u32[]{:S(2)}) collective-permute-start(bf16[2,1024,256]{2,1,0:T(8,128)(2,1)} %get-tuple-element.171), channel_id=1, source_target_pairs={{0,2},{2,0},{4,6},{6,4},{1,3},{3,1},{5,7},{7,5},{8,10},{10,8},{12,... | collective-permute-start | bytes 3145736 | tf_op jit(solution)/shard_map/ppermute | solution.py:607
  208.2 31.7 %collective-permute-start.27 = (bf16[2,1024,256]{2,1,0:T(8,128)(2,1)}, bf16[2,1024,256]{2,1,0:T(8,128)(2,1)}, u32[]{:S(2)}, u32[]{:S(2)}) collective-permute-start(bf16[2,1024,256]{2,1,0:T(8,128)(2,1)} %get-tuple-element.172), channel_id=1, source_target_pairs={{0,4},{2,6},{4,0},{6,2},{1,5},{3,7},{5,1},{7,3},{8,12},{10,14},{12... | collective-permute-start | bytes 3145736 | tf_op jit(solution)/shard_map/ppermute | solution.py:607
  230.4 88.3 %all-gather.11.cloned.1.call-start = ((), (), s32[]{:S(2)}) async-start(), calls=%async_computation.6 | async-start | bytes 1966080 | tf_op jit(solution)/shard_map/all_gather | solution.py:850
  241.4 14.9 %collective-permute-start.34 = (bf16[1024,256]{1,0:T(8,128)(2,1)S(1)}, bf16[1024,256]{1,0:T(8,128)(2,1)S(1)}, u32[]{:S(2)}, u32[]{:S(2)}) collective-permute-start(bf16[1024,256]{1,0:T(8,128)(2,1)S(1)} %fusion.4), channel_id=1, source_target_pairs={{0,2},{2,0},{4,6},{6,4},{1,3},{3,1},{5,7},{7,5},{8,10},{10,8},{12,... | collective-permute-start | bytes 1572872 | tf_op jit(solution)/shard_map/ppermute | solution.py:607
  243.8 17.7 %collective-permute-start.33 = (bf16[1024,256]{1,0:T(8,128)(2,1)S(1)}, bf16[1024,256]{1,0:T(8,128)(2,1)S(1)}, u32[]{:S(2)}, u32[]{:S(2)}) collective-permute-start(bf16[1024,256]{1,0:T(8,128)(2,1)S(1)} %fusion.5), channel_id=1, source_target_pairs={{0,4},{2,6},{4,0},{6,2},{1,5},{3,7},{5,1},{7,3},{8,12},{10,14},{12... | collective-permute-start | bytes 1572872 | tf_op jit(solution)/shard_map/ppermute | solution.py:607
  247.9 14.5 %collective-permute-start.37 = (f32[32,1024]{1,0:T(8,128)}, f32[32,1024]{1,0:T(8,128)S(1)}, u32[]{:S(2)}, u32[]{:S(2)}) collective-permute-start(f32[32,1024]{1,0:T(8,128)} %get-tuple-element.195.s0), channel_id=1, source_target_pairs={{0,6},{2,4},{4,2},{6,0},{1,7},{3,5},{5,3},{7,1},{8,14},{10,12},{12... | collective-permute-start | bytes 393224 | tf_op jit(solution)/shard_map/ppermute | solution.py:607
  271.3 21.0 %collective-permute-start.41 = (bf16[288,512]{1,0:T(8,128)(2,1)}, bf16[288,512]{1,0:T(8,128)(2,1)S(1)}, u32[]{:S(2)}, u32[]{:S(2)}) collective-permute-start(bf16[288,512]{1,0:T(8,128)(2,1)} %get-tuple-element.205), channel_id=1, source_target_pairs={{0,16},{8,24},{16,0},{24,8},{1,17},{9,25},{17,1},{25,9},{2,18},{10... | collective-permute-start | bytes 884744 | tf_op jit(solution)/shard_map/ppermute | solution.py:853
  272.6 19.7 %collective-permute-start.42 = (bf16[288,512]{1,0:T(8,128)(2,1)}, bf16[288,512]{1,0:T(8,128)(2,1)S(1)}, u32[]{:S(2)}, u32[]{:S(2)}) collective-permute-start(bf16[288,512]{1,0:T(8,128)(2,1)} %get-tuple-element.206), channel_id=1, source_target_pairs={{0,24},{8,0},{16,8},{24,16},{1,25},{9,1},{17,9},{25,17},{2,26},{10... | collective-permute-start | bytes 884744 | tf_op jit(solution)/shard_map/ppermute | solution.py:853
  299.3 19.3 %collective-permute-start.47 = (bf16[704,256]{1,0:T(8,128)(2,1)S(1)}, bf16[704,256]{1,0:T(8,128)(2,1)S(1)}, u32[]{:S(2)}, u32[]{:S(2)}) collective-permute-start(bf16[704,256]{1,0:T(8,128)(2,1)S(1)} %get-tuple-element.258.e0), channel_id=1, source_target_pairs={{0,2},{2,0},{4,6},{6,4},{1,3},{3,1},{5,7},{7,5},{8,10},{10,8},{12,... | collective-permute-start | bytes 1081352 | tf_op jit(solution)/shard_map/ppermute | solution.py:607
  300.3 18.4 %collective-permute-start.46 = (bf16[704,256]{1,0:T(8,128)(2,1)S(1)}, bf16[704,256]{1,0:T(8,128)(2,1)S(1)}, u32[]{:S(2)}, u32[]{:S(2)}) collective-permute-start(bf16[704,256]{1,0:T(8,128)(2,1)S(1)} %get-tuple-element.259.d0), channel_id=1, source_target_pairs={{0,4},{2,6},{4,0},{6,2},{1,5},{3,7},{5,1},{7,3},{8,12},{10,14},{12... | collective-permute-start | bytes 1081352 | tf_op jit(solution)/shard_map/ppermute | solution.py:607
  (71 other events, 636.5 us)
Sparse Core Ops, SparseCore 0:
  10.2 51.8 all-gather.8
  63.6 60.7 all-gather.6
  172.5 54.5 reduce-scatter.2
  230.5 35.1 reduce-scatter.4
  270.3 32.3 all-gather.10

commit v2 on v1

--- a/solution.py
+++ b/solution.py
@@ -17,8 +17,8 @@
 NT = (((1,), (1,)), ((), ()))
 TN = (((0,), (0,)), ((), ()))
 SCALE = HD ** (-0.5)
-COST = 3.0
-US = {'delta_terms': 12, 'delta_outputs': 6.5, 'mlp': 12.2, 'mlp_grads': 6.5, 'middle_back': 9.6, 'delta_back': 22, 'input_back': 3.7, 'mixer_sum': 3.5, 'mixer_total': 2.3, 'gate_up_whole': 3.3, 'mixer_whole': 2.9}
+COST = 1.0
+US = {'delta_terms': 108, 'delta_outputs': 58.5, 'mlp': 36.6, 'mlp_grads': 19.5, 'middle_back': 14.4, 'delta_back': 396, 'input_back': 1.1, 'mixer_sum': 10.5, 'mixer_total': 6.9, 'gate_up_whole': 9.9, 'mixer_whole': 8.7}
 GU_BLOCKS = 6
 SMALL_ROWS = 32
 WIDE_ROWS = 6
@@ -851,7 +851,7 @@
     if count > 1:
         turns = [[(i, (i + r) % n_fsdp) for i in range(n_fsdp)] for r in range(1, n_fsdp)]
         mix_far = [lax.ppermute(part, "fsdp", turn) for part, turn in zip(mix_far, turns, strict=True)]
-        mix_far, down_a, down_b = lax.optimization_barrier((mix_far, down_a, down_b))
+        mix_far, down_parts = lax.optimization_barrier((mix_far, down_parts))
     else:
         mix_own = lax.psum_scatter(mix_own, "fsdp", scatter_dimension=0, tiled=True)
     mix_sh, first_out, second_out, beta_out, conv_out, head_out_grad, rms = call(

time: 336 us -> 331 us (0.985)
  the two profiles are of different devices: /device:TPU:0 before, /device:TPU:9 now
where the time goes in v2:
time: 331 us; the launch traced here: 328 us
  waiting for transfers between devices  98.8 us (30%)
  Pallas kernels  85.8 us (26%)
  starting transfers between devices  74.2 us (22%)
  blocking collectives  25 us (8%)
  local copies, waits for them, and re-layouts  17.3 us (5%)
  between operations  14.9 us (5%)
  other arithmetic  12.2 us (4%)
    pallas_call x11, Pallas kernels, call(): pl.pallas_call(body, name=name, in_specs=in_specs, out_specs=jax.tree.map...  85.8 us
    ppermute x40, waiting for transfers between devices, swapped(): lax.ppermute(value, axis, [(s, s ^ mask) for s in range(lax.axis_size(axi...  60.6 us
    ppermute x40, starting transfers between devices, swapped(): lax.ppermute(value, axis, [(s, s ^ mask) for s in range(lax.axis_size(axi...  59.7 us
    all_gather x1, blocking collectives, local(): packs = lax.all_gather(pack, 'fsdp', axis=0)  25 us
    ppermute x3, waiting for transfers between devices, local(): lax.ppermute(part, 'fsdp', turn)  24.8 us
    reduce_scatter x1, waiting for transfers between devices, local(): lax.psum_scatter(down_grad, 'fsdp', scatter_dimension=1, tiled=True)  11.9 us
    unnamed x115, local copies, waits for them, and re-layouts  9.33 us
  transfers between devices with their start and end apart: 53, of which 23 were waited for; matrix products, arithmetic and copies ran while one was open for 6% of the time, Pallas kernels for 21%

profile of v2, /device:TPU:9, one launch (start us, length us, event | category | flops | bytes accessed | tf_op | source)
XLA Modules:
  0.0 328.2 jit_solution(7236158735187661577)
XLA Ops:
  12.8 25.0 %all-gather = bf16[3200,128]{1,0:T(8,128)(2,1)S(1)} all-gather(bf16[800,128]{1,0:T(8,128)(2,1)S(1)} %pad_maximum_fusion.4), channel_id=2, replica_groups=mesh['fsdp'=4,'ctx'=4,'tp'=2] {'fsdp'}, dimensions={0}, use_global_device_ids=true | all-gather | bytes 1024000 | tf_op jit(solution)/shard_map/all_gather | solution.py:648
  38.2 2.9 collective-permute-start.6
  46.3 6.0 %collective-permute-done.2.refs_8_ = bf16[3,800,128]{2,1,0:T(8,128)(2,1)S(1)} collective-permute-done((bf16[3,800,128]{2,1,0:T(8,128)(2,1)S(1)}, bf16[3,800,128]{2,1,0:T(8,128)(2,1)S(1)}, u32[]{:S(2)}, u32[]{:S(2)}) %collective-permute-start.2) | collective-permute-done | bytes 614432 | tf_op jit(solution)/shard_map/ppermute | solution.py:607
  65.6 11.9 %delta_terms.1 = (bf16[4,3,1024,128]{3,2,1,0:T(8,128)(2,1)}, bf16[4,3,264,128]{3,2,1,0:T(8,128)(2,1)}, bf16[4,3,256,128]{3,2,1,0:T(8,128)(2,1)}, f32[4,256,256]{...) custom-call(s32[6]{0:T(128)} %pad_add_fusion.refs_0_.meta, ...), custom_call_target="tpu_custom_call" | custom-call | flops 124200001536 | bytes 1000000 | tf_op jit(solution)/shard_map/delta_terms/pallas_call | solution.py:588
  84.0 2.8 collective-permute-done.12.refs_10_.refs_5_
  87.8 6.5 %delta_outputs.1 = (bf16[4,1024,128]{2,1,0:T(8,128)(2,1)}, f32[4,256,128]{2,1,0:T(8,128)}, f32[4,256,128]{2,1,0:T(8,128)}, f32[4,128,128]{2,1,0:T(8,128)}, bf16[...) custom-call(s32[6]{0:T(128)} %pad_add_fusion.refs_0_.meta, f32[4,256,256]{2,1,0:T(8,128)} %get-tuple-element.126.refs_1_.y_ref.refs_10_, ...), custom_call_target="tpu_custom_call" | custom-call | flops 67275001856 | bytes 1000000 | tf_op jit(solution)/shard_map/delta_outputs/pallas_call | solution.py:588
  94.3 16.2 %collective-permute-start.14 = (f32[256,1024]{1,0:T(8,128)}, f32[256,1024]{1,0:T(8,128)S(1)}, u32[]{:S(2)}, u32[]{:S(2)}) collective-permute-start(f32[256,1024]{1,0:T(8,128)} %get-tuple-element.132.refs_2_), channel_id=1, source_target_pairs={{0,1},{1,0},{2,3},{3,2},{4,5},{5,4},{6,7},{7,6},{8,9},{9,8},{10,11... | collective-permute-start | bytes 3145736 | tf_op jit(solution)/shard_map/ppermute | solution.py:607
  114.1 9.8 %collective-permute-done.18.refs_11_ = bf16[3,256,384]{2,1,0:T(8,128)(2,1)S(1)} collective-permute-done((bf16[3,256,384]{2,1,0:T(8,128)(2,1)S(1)}, bf16[3,256,384]{2,1,0:T(8,128)(2,1)S(1)}, u32[]{:S(2)}, u32[]{:S(2)}) %collective-permute-start.18) | collective-permute-done | bytes 589856 | tf_op jit(solution)/shard_map/ppermute | solution.py:607
  124.8 12.3 %mlp.1 = (f32[256,1024]{1,0:T(8,128)}, bf16[1024,256]{1,0:T(8,128)(2,1)}, bf16[1408,256]{1,0:T(8,128)(2,1)}, bf16[4,256,768]{2,1,0:T(8,128)(2,1)}, bf16[256,1024...) custom-call(s32[6]{0:T(128)} %pad_add_fusion.refs_0_.meta, bf16[256,1024]{1,0:T(8,128)(2,1)} %x_ref.1, ...), custom_call_target="tpu_custom_call" | custom-call | flops 42090000384 | bytes 1000000 | tf_op jit(solution)/shard_map/mlp/pallas_call | solution.py:588
  137.0 8.9 %collective-permute-start.19 = (f32[512,1024]{1,0:T(8,128)}, f32[512,1024]{1,0:T(8,128)}, u32[]{:S(2)}, u32[]{:S(2)}) collective-permute-start(f32[512,1024]{1,0:T(8,128)} %get-tuple-element.135.part_ref), channel_id=1, source_target_pairs={{0,1},{1,0},{2,3},{3,2},{4,5},{5,4},{6,7},{7,6},{8,9},{9,8},{10,11... | collective-permute-start | bytes 6291464 | tf_op jit(solution)/shard_map/ppermute | solution.py:607
  145.9 6.6 %mlp_grads.1 = (bf16[1024,384]{1,0:T(8,128)(2,1)}, bf16[1024,384]{1,0:T(8,128)(2,1)}, bf16[1024,384]{1,0:T(8,128)(2,1)}, bf16[1024,384]{1,0:T(8,128)(2,1)}, bf16...) custom-call(bf16[1024,256]{1,0:T(8,128)(2,1)} %get-tuple-element.136, ...), custom_call_target="tpu_custom_call" | custom-call | flops 22424999936 | bytes 1000000 | tf_op jit(solution)/shard_map/mlp_grads/pallas_call | solution.py:588
  153.6 9.7 %middle_back.1 = (bf16[256,1024]{1,0:T(8,128)(2,1)}, f32[256,1024]{1,0:T(8,128)}, bf16[4,1024,128]{2,1,0:T(8,128)(2,1)}, f32[4,256,128]{2,1,0:T(8,128)}, f32[4,2...) custom-call(s32[6]{0:T(128)} %pad_add_fusion.refs_0_.meta, ...), custom_call_target="tpu_custom_call" | custom-call | flops 16560000000 | bytes 1000000 | tf_op jit(solution)/shard_map/middle_back/pallas_call | solution.py:588
  166.1 5.7 %collective-permute-done.23 = bf16[1024,384]{1,0:T(8,128)(2,1)S(1)} collective-permute-done((bf16[1024,384]{1,0:T(8,128)(2,1)}, bf16[1024,384]{1,0:T(8,128)(2,1)S(1)}, u32[]{:S(2)}, u32[]{:S(2)}) %collective-permute-start.23) | collective-permute-done | bytes 786464 | tf_op jit(solution)/shard_map/ppermute | solution.py:607
  179.8 22.0 %delta_back.1 = (bf16[2,1024,256]{2,1,0:T(8,128)(2,1)}, bf16[2,1024,256]{2,1,0:T(8,128)(2,1)}, bf16[2,1024,256]{2,1,0:T(8,128)(2,1)}, bf16[1024,256]{1,0:T(8,128...) custom-call(s32[6]{0:T(128)} %pad_add_fusion.refs_0_.meta, ...), custom_call_target="tpu_custom_call" | custom-call | flops 455399997440 | bytes 1000000 | tf_op jit(solution)/shard_map/delta_back/pallas_call | solution.py:588
  202.6 2.5 collective-permute-start.25
  205.1 6.1 %collective-permute-done.31 = bf16[1024,384]{1,0:T(8,128)(2,1)} collective-permute-done((bf16[1024,384]{1,0:T(8,128)(2,1)}, bf16[1024,384]{1,0:T(8,128)(2,1)}, u32[]{:S(2)}, u32[]{:S(2)}) %collective-permute-start.31) | collective-permute-done | bytes 786464 | tf_op jit(solution)/shard_map/ppermute | solution.py:607
  211.2 11.9 %reduce-scatter.3.cloned.1.call-done = bf16[1408,256]{1,0:T(8,128)(2,1)} async-done(((bf16[1408,1024]{1,0:T(8,128)(2,1)}), bf16[1408,256]{1,0:T(8,128)(2,1)}) %reduce-scatter.3.cloned.1.call-update) | async-done | bytes 720912 | tf_op jit(solution)/shard_map/reduce_scatter | solution.py:782
  229.0 4.7 %collective-permute-done.26.x_ref = bf16[2,1024,256]{2,1,0:T(8,128)(2,1)S(1)} collective-permute-done((bf16[2,1024,256]{2,1,0:T(8,128)(2,1)}, bf16[2,1024,256]{2,1,0:T(8,128)(2,1)S(1)}, u32[]{:S(2)}, u32[]{:S(2)}) %collective-permute-start.26) | collective-permute-done | bytes 1048608 | tf_op jit(solution)/shard_map/ppermute | solution.py:607
  237.8 3.7 %input_back.1 = (f32[256,1024]{1,0:T(8,128)}, f32[32,1024]{1,0:T(8,128)}) custom-call(bf16[256,1024]{1,0:T(8,128)(2,1)} %x_ref.1, f32[1,1024]{1,0:T(1,128)} %bitcast.67, f32[272,1024]{1,0:T(8,128)} %get-tuple-element.174.part_ref, f32[272,1024]{1,0:T(8,128)} %collective-permute-done.25.other_ref, f32[8,1024]{1,0:T(8,128)} %copy-done.52, ...), custom_call_target="tpu_custom_call" | custom-call | flops 1264999936 | bytes 1000000 | tf_op jit(solution)/shard_map/input_back/pallas_call | solution.py:588
  244.2 4.0 %collective-permute-done.34.late_x_ref = bf16[1024,256]{1,0:T(8,128)(2,1)S(1)} collective-permute-done((bf16[1024,256]{1,0:T(8,128)(2,1)S(1)}, bf16[1024,256]{1,0:T(8,128)(2,1)S(1)}, u32[]{:S(2)}, u32[]{:S(2)}) %collective-permute-start.34) | collective-permute-done | bytes 524320 | tf_op jit(solution)/shard_map/ppermute | solution.py:607
  251.3 3.4 %collective-permute-done.36.s2 = f32[32,1024]{1,0:T(8,128)S(1)} collective-permute-done((f32[32,1024]{1,0:T(8,128)}, f32[32,1024]{1,0:T(8,128)S(1)}, u32[]{:S(2)}, u32[]{:S(2)}) %collective-permute-start.36) | collective-permute-done | bytes 131104 | tf_op jit(solution)/shard_map/ppermute | solution.py:607
  256.1 3.6 %mixer_sum.1 = (bf16[288,512]{1,0:T(8,128)(2,1)}, bf16[288,512]{1,0:T(8,128)(2,1)}, bf16[288,512]{1,0:T(8,128)(2,1)}, bf16[288,512]{1,0:T(8,128)(2,1)}) custom-call(s32[6]{0:T(128)} %pad_add_fusion.refs_0_.meta, bf16[2,1024,256]{2,1,0:T(8,128)(2,1)} %get-tuple-element.192.keep_ref, bf16[2,1024,256]{2,1,0:T(8,128)(2,1)} %copy-done.14, ...), custom_call_target="tpu_custom_call" | custom-call | flops 12074999808 | bytes 1000000 | tf_op jit(solution)/shard_map/mixer_sum/pallas_call | solution.py:588
  259.7 2.8 collective-permute-done.39
  264.2 2.5 collective-permute-start.40
  266.7 2.8 collective-permute-start.41
  269.5 2.7 collective-permute-done.40.refs_0_
  272.3 16.9 %collective-permute-done.41.refs_1_ = bf16[288,512]{1,0:T(8,128)(2,1)S(1)} collective-permute-done((bf16[288,512]{1,0:T(8,128)(2,1)S(1)}, bf16[288,512]{1,0:T(8,128)(2,1)S(1)}, u32[]{:S(2)}, u32[]{:S(2)}) %collective-permute-start.41) | collective-permute-done | bytes 294944 | tf_op jit(solution)/shard_map/ppermute | solution.py:853
  289.1 5.2 %collective-permute-done.42.refs_2_ = bf16[288,512]{1,0:T(8,128)(2,1)S(1)} collective-permute-done((bf16[288,512]{1,0:T(8,128)(2,1)S(1)}, bf16[288,512]{1,0:T(8,128)(2,1)S(1)}, u32[]{:S(2)}, u32[]{:S(2)}) %collective-permute-start.42) | collective-permute-done | bytes 294944 | tf_op jit(solution)/shard_map/ppermute | solution.py:853
  295.1 2.8 mixer_total.1
  305.6 7.3 %collective-permute-done.46.p2 = bf16[256,512]{1,0:T(8,128)(2,1)S(1)} collective-permute-done((bf16[256,512]{1,0:T(8,128)(2,1)}, bf16[256,512]{1,0:T(8,128)(2,1)S(1)}, u32[]{:S(2)}, u32[]{:S(2)}) %collective-permute-start.46) | collective-permute-done | bytes 262176 | tf_op jit(solution)/shard_map/ppermute | solution.py:607
  314.3 2.9 mixer_whole.1
  317.2 4.0 %gate_up_whole.1 = (f32[2,256,1408]{2,1,0:T(8,128)}, f32[1408,256]{1,0:T(8,128)}) custom-call(bf16[4,256,768]{2,1,0:T(8,128)(2,1)} %bitcast.71, bf16[704,256]{1,0:T(8,128)(2,1)} %copy-done.11, bf16[704,256]{1,0:T(8,128)(2,1)} %copy-done.31, bf16[704,256]{1,0:T(8,128)(2,1)} %copy-done.10, bf16[704,256]{1,0:T(8,128)(2,1)} %copy-done.30), custom_call_target="tpu_custom_call" | custom-call | flops 11384999936 | bytes 1000000 | tf_op jit(solution)/shard_map/gate_up_whole/pallas_call | solution.py:588
  (250 shorter events, 77.2 us)
Async XLA Ops:
  7.2 73.1 %all-gather.9.cloned.1.call-start = ((), (), s32[]{:S(2)}) async-start(), calls=%async_computation.5 | async-start | bytes 1966080 | tf_op jit(solution)/shard_map/all_gather | solution.py:655
  11.0 113.7 %all-gather.7.cloned.1.call-start = ((), (), s32[]{:S(2)}) async-start(), calls=%async_computation.2 | async-start | bytes 3604480 | tf_op jit(solution)/shard_map/all_gather | solution.py:657
  37.9 24.1 %collective-permute-start.7 = (bf16[256,128]{1,0:T(8,128)(2,1)S(1)}, bf16[256,128]{1,0:T(8,128)(2,1)S(1)}, u32[]{:S(2)}, u32[]{:S(2)}) collective-permute-start(bf16[256,128]{1,0:T(8,128)(2,1)S(1)} %dynamic-slice_bitcast_fusion), channel_id=1, source_target_pairs={{0,24},{8,0},{16,8},{24,16},{1,25},{9,1},{17,9},{25,17},{2,26},{10... | collective-permute-start | bytes 196616 | tf_op jit(solution)/shard_map/ppermute | solution.py:614
  38.2 23.8 %collective-permute-start.6 = (bf16[256,128]{1,0:T(8,128)(2,1)S(1)}, bf16[256,128]{1,0:T(8,128)(2,1)S(1)}, u32[]{:S(2)}, u32[]{:S(2)}) collective-permute-start(bf16[256,128]{1,0:T(8,128)(2,1)S(1)} %dynamic-slice_bitcast_fusion), channel_id=1, source_target_pairs={{0,16},{8,24},{16,0},{24,8},{1,17},{9,25},{17,1},{25,9},{2,18},{10... | collective-permute-start | bytes 196616 | tf_op jit(solution)/shard_map/ppermute | solution.py:614
  43.4 15.4 %collective-permute-start = (bf16[8,1024]{1,0:T(8,128)(2,1)S(1)}, bf16[8,1024]{1,0:T(8,128)(2,1)S(1)}, u32[]{:S(2)}, u32[]{:S(2)}) collective-permute-start(bf16[8,1024]{1,0:T(8,128)(2,1)S(1)} %slice.63), channel_id=1, source_target_pairs={{0,2},{2,4},{4,6},{1,3},{3,5},{5,7},{8,10},{10,12},{12,14},{9,11},... | collective-permute-start | bytes 49160 | tf_op jit(solution)/shard_map/ppermute | solution.py:603
  45.6 177.5 %reduce-scatter.3.cloned.1.call-start = ((), (), s32[]{:S(2)}) async-start(), calls=%async_computation.3 | async-start | bytes 3604480 | tf_op jit(solution)/shard_map/reduce_scatter | solution.py:782
  62.9 16.0 %collective-permute-start.10 = (bf16[3,256,128]{2,1,0:T(8,128)(2,1)S(1)}, bf16[3,256,128]{2,1,0:T(8,128)(2,1)S(1)}, u32[]{:S(2)}, u32[]{:S(2)}) collective-permute-start(bf16[3,256,128]{2,1,0:T(8,128)(2,1)S(1)} %constant_dynamic-update-slice_fusion.refs_5_), channel_id=1, source_target_pairs={{0,6},{2,4},{4,2},{6,0},{1,7},{3,5},{5,3},{7,1},{8,14},{10,12},{12... | collective-permute-start | bytes 589832 | tf_op jit(solution)/shard_map/ppermute | solution.py:607
  63.6 18.1 %collective-permute-start.9 = (bf16[3,256,128]{2,1,0:T(8,128)(2,1)S(1)}, bf16[3,256,128]{2,1,0:T(8,128)(2,1)}, u32[]{:S(2)}, u32[]{:S(2)}) collective-permute-start(bf16[3,256,128]{2,1,0:T(8,128)(2,1)S(1)} %constant_dynamic-update-slice_fusion.refs_5_), channel_id=1, source_target_pairs={{0,4},{2,6},{4,0},{6,2},{1,5},{3,7},{5,1},{7,3},{8,12},{10,14},{12... | collective-permute-start | bytes 589832 | tf_op jit(solution)/shard_map/ppermute | solution.py:607
  64.3 17.6 %collective-permute-start.8 = (bf16[3,256,128]{2,1,0:T(8,128)(2,1)S(1)}, bf16[3,256,128]{2,1,0:T(8,128)(2,1)}, u32[]{:S(2)}, u32[]{:S(2)}) collective-permute-start(bf16[3,256,128]{2,1,0:T(8,128)(2,1)S(1)} %constant_dynamic-update-slice_fusion.refs_5_), channel_id=1, source_target_pairs={{0,2},{2,0},{4,6},{6,4},{1,3},{3,1},{5,7},{7,5},{8,10},{10,8},{12,... | collective-permute-start | bytes 589832 | tf_op jit(solution)/shard_map/ppermute | solution.py:607
  81.7 28.8 %collective-permute-start.16 = (bf16[3,256,768]{2,1,0:T(8,128)(2,1)S(1)}, bf16[3,256,768]{2,1,0:T(8,128)(2,1)S(1)}, u32[]{:S(2)}, u32[]{:S(2)}) collective-permute-start(bf16[3,256,768]{2,1,0:T(8,128)(2,1)S(1)} %pad_maximum_fusion.1), channel_id=1, source_target_pairs={{0,4},{2,6},{4,0},{6,2},{1,5},{3,7},{5,1},{7,3},{8,12},{10,14},{12... | collective-permute-start | bytes 3538952 | tf_op jit(solution)/shard_map/ppermute | solution.py:607
  81.9 28.6 %collective-permute-start.15 = (bf16[3,256,768]{2,1,0:T(8,128)(2,1)S(1)}, bf16[3,256,768]{2,1,0:T(8,128)(2,1)S(1)}, u32[]{:S(2)}, u32[]{:S(2)}) collective-permute-start(bf16[3,256,768]{2,1,0:T(8,128)(2,1)S(1)} %pad_maximum_fusion.1), channel_id=1, source_target_pairs={{0,2},{2,0},{4,6},{6,4},{1,3},{3,1},{5,7},{7,5},{8,10},{10,8},{12,... | collective-permute-start | bytes 3538952 | tf_op jit(solution)/shard_map/ppermute | solution.py:607
  94.3 19.8 %collective-permute-start.14 = (f32[256,1024]{1,0:T(8,128)}, f32[256,1024]{1,0:T(8,128)S(1)}, u32[]{:S(2)}, u32[]{:S(2)}) collective-permute-start(f32[256,1024]{1,0:T(8,128)} %get-tuple-element.132.refs_2_), channel_id=1, source_target_pairs={{0,1},{1,0},{2,3},{3,2},{4,5},{5,4},{6,7},{7,6},{8,9},{9,8},{10,11... | collective-permute-start | bytes 3145736 | tf_op jit(solution)/shard_map/ppermute | solution.py:607
  110.7 13.2 %collective-permute-start.18 = (bf16[3,256,384]{2,1,0:T(8,128)(2,1)S(1)}, bf16[3,256,384]{2,1,0:T(8,128)(2,1)S(1)}, u32[]{:S(2)}, u32[]{:S(2)}) collective-permute-start(bf16[3,256,384]{2,1,0:T(8,128)(2,1)S(1)} %slice.75), channel_id=1, source_target_pairs={{0,2},{2,0},{4,6},{6,4},{1,3},{3,1},{5,7},{7,5},{8,10},{10,8},{12,... | collective-permute-start | bytes 1769480 | tf_op jit(solution)/shard_map/ppermute | solution.py:607
  137.0 15.5 %collective-permute-start.19 = (f32[512,1024]{1,0:T(8,128)}, f32[512,1024]{1,0:T(8,128)}, u32[]{:S(2)}, u32[]{:S(2)}) collective-permute-start(f32[512,1024]{1,0:T(8,128)} %get-tuple-element.135.part_ref), channel_id=1, source_target_pairs={{0,1},{1,0},{2,3},{3,2},{4,5},{5,4},{6,7},{7,6},{8,9},{9,8},{10,11... | collective-permute-start | bytes 6291464 | tf_op jit(solution)/shard_map/ppermute | solution.py:607
  152.5 19.4 %collective-permute-start.23 = (bf16[1024,384]{1,0:T(8,128)(2,1)}, bf16[1024,384]{1,0:T(8,128)(2,1)S(1)}, u32[]{:S(2)}, u32[]{:S(2)}) collective-permute-start(bf16[1024,384]{1,0:T(8,128)(2,1)} %get-tuple-element.156), channel_id=1, source_target_pairs={{0,4},{2,6},{4,0},{6,2},{1,5},{3,7},{5,1},{7,3},{8,12},{10,14},{12... | collective-permute-start | bytes 2359304 | tf_op jit(solution)/shard_map/ppermute | solution.py:607
  152.5 21.6 %collective-permute-start.24 = (bf16[1024,384]{1,0:T(8,128)(2,1)}, bf16[1024,384]{1,0:T(8,128)(2,1)S(1)}, u32[]{:S(2)}, u32[]{:S(2)}) collective-permute-start(bf16[1024,384]{1,0:T(8,128)(2,1)} %get-tuple-element.158), channel_id=1, source_target_pairs={{0,2},{2,0},{4,6},{6,4},{1,3},{3,1},{5,7},{7,5},{8,10},{10,8},{12,... | collective-permute-start | bytes 2359304 | tf_op jit(solution)/shard_map/ppermute | solution.py:607
  166.1 96.5 %reduce-scatter.5.cloned.1.call-start = ((), (), s32[]{:S(2)}) async-start(), calls=%async_computation.4 | async-start | bytes 1966080 | tf_op jit(solution)/shard_map/reduce_scatter | solution.py:829
  171.9 30.4 %collective-permute-start.29 = (bf16[1024,384]{1,0:T(8,128)(2,1)}, bf16[1024,384]{1,0:T(8,128)(2,1)}, u32[]{:S(2)}, u32[]{:S(2)}) collective-permute-start(bf16[1024,384]{1,0:T(8,128)(2,1)} %get-tuple-element.179), channel_id=1, source_target_pairs={{0,2},{2,0},{4,6},{6,4},{1,3},{3,1},{5,7},{7,5},{8,10},{10,8},{12,... | collective-permute-start | bytes 2359304 | tf_op jit(solution)/shard_map/ppermute | solution.py:607
  174.1 28.6 %collective-permute-start.30 = (bf16[1024,384]{1,0:T(8,128)(2,1)}, bf16[1024,384]{1,0:T(8,128)(2,1)}, u32[]{:S(2)}, u32[]{:S(2)}) collective-permute-start(bf16[1024,384]{1,0:T(8,128)(2,1)} %get-tuple-element.180), channel_id=1, source_target_pairs={{0,4},{2,6},{4,0},{6,2},{1,5},{3,7},{5,1},{7,3},{8,12},{10,14},{12... | collective-permute-start | bytes 2359304 | tf_op jit(solution)/shard_map/ppermute | solution.py:607
  177.6 33.6 %collective-permute-start.31 = (bf16[1024,384]{1,0:T(8,128)(2,1)}, bf16[1024,384]{1,0:T(8,128)(2,1)}, u32[]{:S(2)}, u32[]{:S(2)}) collective-permute-start(bf16[1024,384]{1,0:T(8,128)(2,1)} %add_convert_fusion.1), channel_id=1, source_target_pairs={{0,2},{2,0},{4,6},{6,4},{1,3},{3,1},{5,7},{7,5},{8,10},{10,8},{12,... | collective-permute-start | bytes 2359304 | tf_op jit(solution)/shard_map/ppermute | solution.py:607
  178.7 32.5 %collective-permute-start.32 = (bf16[1024,384]{1,0:T(8,128)(2,1)}, bf16[1024,384]{1,0:T(8,128)(2,1)}, u32[]{:S(2)}, u32[]{:S(2)}) collective-permute-start(bf16[1024,384]{1,0:T(8,128)(2,1)} %add_convert_fusion), channel_id=1, source_target_pairs={{0,4},{2,6},{4,0},{6,2},{1,5},{3,7},{5,1},{7,3},{8,12},{10,14},{12... | collective-permute-start | bytes 2359304 | tf_op jit(solution)/shard_map/ppermute | solution.py:607
  201.8 31.9 %collective-permute-start.26 = (bf16[2,1024,256]{2,1,0:T(8,128)(2,1)}, bf16[2,1024,256]{2,1,0:T(8,128)(2,1)S(1)}, u32[]{:S(2)}, u32[]{:S(2)}) collective-permute-start(bf16[2,1024,256]{2,1,0:T(8,128)(2,1)} %get-tuple-element.175), channel_id=1, source_target_pairs={{0,2},{2,0},{4,6},{6,4},{1,3},{3,1},{5,7},{7,5},{8,10},{10,8},{12,... | collective-permute-start | bytes 3145736 | tf_op jit(solution)/shard_map/ppermute | solution.py:607
  202.3 31.4 %collective-permute-start.27 = (bf16[2,1024,256]{2,1,0:T(8,128)(2,1)}, bf16[2,1024,256]{2,1,0:T(8,128)(2,1)}, u32[]{:S(2)}, u32[]{:S(2)}) collective-permute-start(bf16[2,1024,256]{2,1,0:T(8,128)(2,1)} %get-tuple-element.176), channel_id=1, source_target_pairs={{0,4},{2,6},{4,0},{6,2},{1,5},{3,7},{5,1},{7,3},{8,12},{10,14},{12... | collective-permute-start | bytes 3145736 | tf_op jit(solution)/shard_map/ppermute | solution.py:607
  202.6 24.3 %collective-permute-start.25 = (f32[272,1024]{1,0:T(8,128)}, f32[272,1024]{1,0:T(8,128)}, u32[]{:S(2)}, u32[]{:S(2)}) collective-permute-start(f32[272,1024]{1,0:T(8,128)} %get-tuple-element.174.part_ref), channel_id=1, source_target_pairs={{0,1},{1,0},{2,3},{3,2},{4,5},{5,4},{6,7},{7,6},{8,9},{9,8},{10,11... | collective-permute-start | bytes 3342344 | tf_op jit(solution)/shard_map/ppermute | solution.py:607
  226.8 90.4 %all-gather.11.cloned.1.call-start = ((), (), s32[]{:S(2)}) async-start(), calls=%async_computation.6 | async-start | bytes 1966080 | tf_op jit(solution)/shard_map/all_gather | solution.py:850
  248.2 14.4 %collective-permute-start.39 = (bf16[704,256]{1,0:T(8,128)(2,1)S(1)}, bf16[704,256]{1,0:T(8,128)(2,1)S(1)}, u32[]{:S(2)}, u32[]{:S(2)}) collective-permute-start(bf16[704,256]{1,0:T(8,128)(2,1)S(1)} %get-tuple-element.268), channel_id=1, source_target_pairs={{0,4},{2,6},{4,0},{6,2},{1,5},{3,7},{5,1},{7,3},{8,12},{10,14},{12... | collective-permute-start | bytes 1081352 | tf_op jit(solution)/shard_map/ppermute | solution.py:607
  262.8 31.6 %collective-permute-start.44 = (bf16[704,256]{1,0:T(8,128)(2,1)S(1)}, bf16[704,256]{1,0:T(8,128)(2,1)S(1)}, u32[]{:S(2)}, u32[]{:S(2)}) collective-permute-start(bf16[704,256]{1,0:T(8,128)(2,1)S(1)} %get-tuple-element.227.e0), channel_id=1, source_target_pairs={{0,2},{2,0},{4,6},{6,4},{1,3},{3,1},{5,7},{7,5},{8,10},{10,8},{12,... | collective-permute-start | bytes 1081352 | tf_op jit(solution)/shard_map/ppermute | solution.py:607
  263.1 31.2 %collective-permute-start.43 = (bf16[704,256]{1,0:T(8,128)(2,1)S(1)}, bf16[704,256]{1,0:T(8,128)(2,1)S(1)}, u32[]{:S(2)}, u32[]{:S(2)}) collective-permute-start(bf16[704,256]{1,0:T(8,128)(2,1)S(1)} %get-tuple-element.225.d0), channel_id=1, source_target_pairs={{0,4},{2,6},{4,0},{6,2},{1,5},{3,7},{5,1},{7,3},{8,12},{10,14},{12... | collective-permute-start | bytes 1081352 | tf_op jit(solution)/shard_map/ppermute | solution.py:607
  266.7 22.5 %collective-permute-start.41 = (bf16[288,512]{1,0:T(8,128)(2,1)S(1)}, bf16[288,512]{1,0:T(8,128)(2,1)S(1)}, u32[]{:S(2)}, u32[]{:S(2)}) collective-permute-start(bf16[288,512]{1,0:T(8,128)(2,1)S(1)} %copy-done.34), channel_id=1, source_target_pairs={{0,16},{8,24},{16,0},{24,8},{1,17},{9,25},{17,1},{25,9},{2,18},{10... | collective-permute-start | bytes 884744 | tf_op jit(solution)/shard_map/ppermute | solution.py:853
  269.5 24.8 %collective-permute-start.42 = (bf16[288,512]{1,0:T(8,128)(2,1)S(1)}, bf16[288,512]{1,0:T(8,128)(2,1)S(1)}, u32[]{:S(2)}, u32[]{:S(2)}) collective-permute-start(bf16[288,512]{1,0:T(8,128)(2,1)S(1)} %copy-done.33), channel_id=1, source_target_pairs={{0,24},{8,0},{16,8},{24,16},{1,25},{9,1},{17,9},{25,17},{2,26},{10... | collective-permute-start | bytes 884744 | tf_op jit(solution)/shard_map/ppermute | solution.py:853
  299.2 13.7 %collective-permute-start.46 = (bf16[256,512]{1,0:T(8,128)(2,1)}, bf16[256,512]{1,0:T(8,128)(2,1)S(1)}, u32[]{:S(2)}, u32[]{:S(2)}) collective-permute-start(bf16[256,512]{1,0:T(8,128)(2,1)} %get-tuple-element.217.p0), channel_id=1, source_target_pairs={{0,4},{2,6},{4,0},{6,2},{1,5},{3,7},{5,1},{7,3},{8,12},{10,14},{12... | collective-permute-start | bytes 786440 | tf_op jit(solution)/shard_map/ppermute | solution.py:607
  299.5 13.4 %collective-permute-start.45 = (bf16[256,512]{1,0:T(8,128)(2,1)}, bf16[256,512]{1,0:T(8,128)(2,1)S(1)}, u32[]{:S(2)}, u32[]{:S(2)}) collective-permute-start(bf16[256,512]{1,0:T(8,128)(2,1)} %get-tuple-element.217.p0), channel_id=1, source_target_pairs={{0,2},{2,0},{4,6},{6,4},{1,3},{3,1},{5,7},{7,5},{8,10},{10,8},{12,... | collective-permute-start | bytes 786440 | tf_op jit(solution)/shard_map/ppermute | solution.py:607
  (74 other events, 663.3 us)
Sparse Core Ops, SparseCore 0:
  11.1 48.8 all-gather.8
  61.6 57.3 all-gather.6
  166.2 56.8 reduce-scatter.2
  227.0 33.8 reduce-scatter.4
  262.7 32.7 all-gather.10

commit v3 on v2

--- a/solution.py
+++ b/solution.py
@@ -263,7 +263,7 @@
 
 def mlp_kernel(*refs, lengths, n_fsdp):
     (meta, x_ref, attn_ref, other_ref, gain_ref, cot_ref, local_ref, own_ref, f1, f2, a3, b3, down_ref,
-     mid_ref, nt_ref, at_ref, g_ref, gf_ref, part_ref, st_ref, w, gu, sem) = refs
+     mid_ref, nt_ref, at_ref, g_ref, gf_ref, part_ref, st_ref, x3_ref, y3_ref, w, gu, sem) = refs
     rows, width = x_ref.shape
     units = down_ref.shape[0]
     d_loc = local_ref.shape[0]
@@ -324,17 +324,17 @@
         part = term if part is None else part + term
     part_ref[:rows] = part
     part_ref[rows:] = pdot(act, down_ref[...])
-
-
-def mlp_grads_kernel(nt_ref, g_ref, at_ref, gf_ref, x3_ref, y3_ref, x1_ref, y2_ref, late_x_ref, late_y_ref, own_ref, down_ref):
+    x3_ref[...] = pdot(nt_ref[...], g_ref[3, :, :half]).astype(BF16)
+    y3_ref[...] = pdot(nt_ref[...], g_ref[3, :, half:]).astype(BF16)
+
+
+def mlp_grads_kernel(nt_ref, g_ref, at_ref, gf_ref, x1_ref, y2_ref, late_x_ref, late_y_ref, own_ref, down_ref):
     half = g_ref.shape[2] // 2
     nt = nt_ref[...]
 
     def put(ref, j, side):
         ref[...] = pdot(nt, g_ref[j, :, side * half : (side + 1) * half]).astype(BF16)
 
-    put(x3_ref, 3, 0)
-    put(y3_ref, 3, 1)
     put(x1_ref, 1, 0)
     put(y2_ref, 2, 1)
     put(late_x_ref, 1, 1)
@@ -721,7 +721,7 @@
     )
     attn_other = swapped(attn_part, "tp", 1)
 
-    middle, normed_mid_t, act_t, g_gu, g_ffn, mlp_part, stats = call(
+    middle, normed_mid_t, act_t, g_gu, g_ffn, mlp_part, stats, gu_x3, gu_y3 = call(
         functools.partial(mlp_kernel, lengths=n_len, n_fsdp=n_fsdp),
         "mlp",
         (
@@ -732,6 +732,8 @@
             sds(rows, width, dtype=BF16),
             sds(2 * rows, width),
             sds(8, width),
+            sds(width, step // 2, dtype=BF16),
+            sds(width, step // 2, dtype=BF16),
         ),
         [SMEM] + [VMEM] * 5 + [ANY] * 6 + [VMEM],
         (
@@ -747,14 +749,14 @@
     gu_grads = call(
         mlp_grads_kernel,
         "mlp_grads",
-        (quarter,) * 6 + (double, sds(units, width, dtype=BF16)),
+        (quarter,) * 4 + (double, sds(units, width, dtype=BF16)),
         [VMEM] * 4,
         (normed_mid_t, g_gu, act_t, g_ffn),
         gflops=4,
         mbytes=12,
     )
     mlp_other, gu_grads = lax.optimization_barrier((mlp_other, gu_grads))
-    gu_x3, gu_y3, gu_x1, gu_y2, gu_late_x, gu_late_y, gu_keep, down_grad = gu_grads
+    gu_x1, gu_y2, gu_late_x, gu_late_y, gu_keep, down_grad = gu_grads
     from_x3, from_y3 = swapped(gu_x3, "ctx", 1), swapped(gu_y3, "ctx", 2)
 
     result, g_middle, out_grads, d_mixed, d_fresh, d_state, sums = call(

time: 331 us -> 328 us (level)
  the two profiles are of different devices: /device:TPU:9 before, /device:TPU:0 now
where the time goes in v3:
time: 328 us; the launch traced here: 322 us
  waiting for transfers between devices  104 us (32%)
  Pallas kernels  85.4 us (26%)
  starting transfers between devices  57.9 us (18%)
  blocking collectives  29.7 us (9%)
  local copies, waits for them, and re-layouts  17.3 us (5%)
  between operations  14.9 us (5%)
  other arithmetic  12.2 us (4%)
    pallas_call x11, Pallas kernels, call(): pl.pallas_call(body, name=name, in_specs=in_specs, out_specs=jax.tree.map...  85.4 us
    ppermute x40, waiting for transfers between devices, swapped(): lax.ppermute(value, axis, [(s, s ^ mask) for s in range(lax.axis_size(axi...  65.6 us
    ppermute x40, starting transfers between devices, swapped(): lax.ppermute(value, axis, [(s, s ^ mask) for s in range(lax.axis_size(axi...  44.2 us
    all_gather x1, blocking collectives, local(): packs = lax.all_gather(pack, 'fsdp', axis=0)  29.7 us
    ppermute x3, waiting for transfers between devices, local(): lax.ppermute(part, 'fsdp', turn)  18.4 us
    reduce_scatter x1, waiting for transfers between devices, local(): lax.psum_scatter(down_grad, 'fsdp', scatter_dimension=1, tiled=True)  13.5 us
    unnamed x115, local copies, waits for them, and re-layouts  9.35 us
  transfers between devices with their start and end apart: 53, of which 26 were waited for; matrix products, arithmetic and copies ran while one was open for 6% of the time, Pallas kernels for 21%

profile of v3, /device:TPU:0, one launch (start us, length us, event | category | flops | bytes accessed | tf_op | source)
XLA Modules:
  0.0 321.6 jit_solution(11526464824184676162)
XLA Ops:
  12.8 29.7 %all-gather = bf16[3200,128]{1,0:T(8,128)(2,1)S(1)} all-gather(bf16[800,128]{1,0:T(8,128)(2,1)S(1)} %pad_maximum_fusion.4), channel_id=2, replica_groups=mesh['fsdp'=4,'ctx'=4,'tp'=2] {'fsdp'}, dimensions={0}, use_global_device_ids=true | all-gather | bytes 1024000 | tf_op jit(solution)/shard_map/all_gather | solution.py:648
  42.6 4.4 %collective-permute-start.7 = (bf16[256,128]{1,0:T(8,128)(2,1)S(1)}, bf16[256,128]{1,0:T(8,128)(2,1)S(1)}, u32[]{:S(2)}, u32[]{:S(2)}) collective-permute-start(bf16[256,128]{1,0:T(8,128)(2,1)S(1)} %dynamic-slice_bitcast_fusion), channel_id=1, source_target_pairs={{0,24},{8,0},{16,8},{24,16},{1,25},{9,1},{17,9},{25,17},{2,26},{10... | collective-permute-start | bytes 196616 | tf_op jit(solution)/shard_map/ppermute | solution.py:614
  49.9 2.4 collective-permute-start
  53.2 6.7 %collective-permute-done.2.refs_8_ = bf16[3,800,128]{2,1,0:T(8,128)(2,1)S(1)} collective-permute-done((bf16[3,800,128]{2,1,0:T(8,128)(2,1)S(1)}, bf16[3,800,128]{2,1,0:T(8,128)(2,1)S(1)}, u32[]{:S(2)}, u32[]{:S(2)}) %collective-permute-start.2) | collective-permute-done | bytes 614432 | tf_op jit(solution)/shard_map/ppermute | solution.py:607
  69.6 4.6 %collective-permute-done.5 = bf16[256,128]{1,0:T(8,128)(2,1)S(1)} collective-permute-done((bf16[256,128]{1,0:T(8,128)(2,1)S(1)}, bf16[256,128]{1,0:T(8,128)(2,1)S(1)}, u32[]{:S(2)}, u32[]{:S(2)}) %collective-permute-start.5) | collective-permute-done | bytes 65568 | tf_op jit(solution)/shard_map/ppermute | solution.py:614
  74.3 3.1 collective-permute-start.10
  78.1 11.9 %delta_terms.1 = (bf16[4,3,1024,128]{3,2,1,0:T(8,128)(2,1)}, bf16[4,3,264,128]{3,2,1,0:T(8,128)(2,1)}, bf16[4,3,256,128]{3,2,1,0:T(8,128)(2,1)}, f32[4,256,256]{...) custom-call(s32[6]{0:T(128)} %pad_add_fusion.refs_0_.meta, ...), custom_call_target="tpu_custom_call" | custom-call | flops 124200001536 | bytes 1000000 | tf_op jit(solution)/shard_map/delta_terms/pallas_call | solution.py:588
  89.9 2.9 collective-permute-start.13
  100.4 3.8 %collective-permute-done.12.refs_10_.refs_5_ = bf16[4,2,128,128]{3,2,1,0:T(8,128)(2,1)S(1)} collective-permute-done((bf16[4,2,128,128]{3,2,1,0:T(8,128)(2,1)}, bf16[4,2,128,128]{3,2,1,0:T(8,128)(2,1)S(1)}, u32[]{:S(2)}, u32[]{:S(2)}) %collective-permute-start.12) | collective-permute-done | bytes 262176 | tf_op jit(solution)/shard_map/ppermute | solution.py:607
  106.8 6.5 %delta_outputs.1 = (bf16[4,1024,128]{2,1,0:T(8,128)(2,1)}, f32[4,256,128]{2,1,0:T(8,128)}, f32[4,256,128]{2,1,0:T(8,128)}, f32[4,128,128]{2,1,0:T(8,128)}, bf16[...) custom-call(s32[6]{0:T(128)} %pad_add_fusion.refs_0_.meta, f32[4,256,256]{2,1,0:T(8,128)} %get-tuple-element.124.refs_1_.y_ref.refs_10_, ...), custom_call_target="tpu_custom_call" | custom-call | flops 67275001856 | bytes 1000000 | tf_op jit(solution)/shard_map/delta_outputs/pallas_call | solution.py:588
  113.4 10.9 %collective-permute-done.16.refs_9_ = bf16[3,256,768]{2,1,0:T(8,128)(2,1)S(1)} collective-permute-done((bf16[3,256,768]{2,1,0:T(8,128)(2,1)S(1)}, bf16[3,256,768]{2,1,0:T(8,128)(2,1)S(1)}, u32[]{:S(2)}, u32[]{:S(2)}) %collective-permute-start.16) | collective-permute-done | bytes 1179680 | tf_op jit(solution)/shard_map/ppermute | solution.py:607
  128.3 6.2 %collective-permute-done.18.refs_11_ = bf16[3,256,384]{2,1,0:T(8,128)(2,1)S(1)} collective-permute-done((bf16[3,256,384]{2,1,0:T(8,128)(2,1)S(1)}, bf16[3,256,384]{2,1,0:T(8,128)(2,1)S(1)}, u32[]{:S(2)}, u32[]{:S(2)}) %collective-permute-start.18) | collective-permute-done | bytes 589856 | tf_op jit(solution)/shard_map/ppermute | solution.py:607
  135.6 12.3 %mlp.1 = (f32[256,1024]{1,0:T(8,128)}, bf16[1024,256]{1,0:T(8,128)(2,1)}, bf16[1408,256]{1,0:T(8,128)(2,1)}, bf16[4,256,768]{2,1,0:T(8,128)(2,1)}, bf16[256,1024...) custom-call(s32[6]{0:T(128)} %pad_add_fusion.refs_0_.meta, ...), custom_call_target="tpu_custom_call" | custom-call | flops 42090000384 | bytes 1000000 | tf_op jit(solution)/shard_map/mlp/pallas_call | solution.py:588
  148.0 2.7 collective-permute-start.23
  152.0 6.0 %mlp_grads.1 = (bf16[1024,384]{1,0:T(8,128)(2,1)}, bf16[1024,384]{1,0:T(8,128)(2,1)}, bf16[1024,384]{1,0:T(8,128)(2,1)}, bf16[1024,384]{1,0:T(8,128)(2,1)}, bf16...) custom-call(bf16[1024,256]{1,0:T(8,128)(2,1)} %get-tuple-element.134.nt_ref, ...), custom_call_target="tpu_custom_call" | custom-call | flops 22424999936 | bytes 1000000 | tf_op jit(solution)/shard_map/mlp_grads/pallas_call | solution.py:588
  158.0 9.8 %middle_back.1 = (bf16[256,1024]{1,0:T(8,128)(2,1)}, f32[256,1024]{1,0:T(8,128)}, bf16[4,1024,128]{2,1,0:T(8,128)(2,1)}, f32[4,256,128]{2,1,0:T(8,128)}, f32[4,2...) custom-call(s32[6]{0:T(128)} %pad_add_fusion.refs_0_.meta, ...), custom_call_target="tpu_custom_call" | custom-call | flops 16560000000 | bytes 1000000 | tf_op jit(solution)/shard_map/middle_back/pallas_call | solution.py:588
  179.4 22.0 %delta_back.1 = (bf16[2,1024,256]{2,1,0:T(8,128)(2,1)}, bf16[2,1024,256]{2,1,0:T(8,128)(2,1)}, bf16[2,1024,256]{2,1,0:T(8,128)(2,1)}, bf16[1024,256]{1,0:T(8,128...) custom-call(s32[6]{0:T(128)} %pad_add_fusion.refs_0_.meta, ...), custom_call_target="tpu_custom_call" | custom-call | flops 455399997440 | bytes 1000000 | tf_op jit(solution)/shard_map/delta_back/pallas_call | solution.py:588
  203.6 6.9 %collective-permute-done.31 = bf16[1024,384]{1,0:T(8,128)(2,1)} collective-permute-done((bf16[1024,384]{1,0:T(8,128)(2,1)}, bf16[1024,384]{1,0:T(8,128)(2,1)}, u32[]{:S(2)}, u32[]{:S(2)}) %collective-permute-start.31) | collective-permute-done | bytes 786464 | tf_op jit(solution)/shard_map/ppermute | solution.py:607
  211.2 13.5 %reduce-scatter.3.cloned.1.call-done = bf16[1408,256]{1,0:T(8,128)(2,1)} async-done(((bf16[1408,1024]{1,0:T(8,128)(2,1)}), bf16[1408,256]{1,0:T(8,128)(2,1)}) %reduce-scatter.3.cloned.1.call-update) | async-done | bytes 720912 | tf_op jit(solution)/shard_map/reduce_scatter | solution.py:784
  236.4 2.4 collective-permute-start.34
  239.1 3.7 %input_back.1 = (f32[256,1024]{1,0:T(8,128)}, f32[32,1024]{1,0:T(8,128)}) custom-call(bf16[256,1024]{1,0:T(8,128)(2,1)} %x_ref.1, f32[1,1024]{1,0:T(1,128)} %bitcast.67, f32[272,1024]{1,0:T(8,128)} %get-tuple-element.170.part_ref, f32[272,1024]{1,0:T(8,128)} %collective-permute-done.25.other_ref, f32[8,1024]{1,0:T(8,128)} %copy-done.52, ...), custom_call_target="tpu_custom_call" | custom-call | flops 1264999936 | bytes 1000000 | tf_op jit(solution)/shard_map/input_back/pallas_call | solution.py:588
  246.3 5.3 %collective-permute-done.34.late_x_ref = bf16[1024,256]{1,0:T(8,128)(2,1)S(1)} collective-permute-done((bf16[1024,256]{1,0:T(8,128)(2,1)S(1)}, bf16[1024,256]{1,0:T(8,128)(2,1)S(1)}, u32[]{:S(2)}, u32[]{:S(2)}) %collective-permute-start.34) | collective-permute-done | bytes 524320 | tf_op jit(solution)/shard_map/ppermute | solution.py:607
  252.8 3.9 %collective-permute-done.33.late_y_ref = bf16[1024,256]{1,0:T(8,128)(2,1)S(1)} collective-permute-done((bf16[1024,256]{1,0:T(8,128)(2,1)S(1)}, bf16[1024,256]{1,0:T(8,128)(2,1)S(1)}, u32[]{:S(2)}, u32[]{:S(2)}) %collective-permute-start.33) | collective-permute-done | bytes 524320 | tf_op jit(solution)/shard_map/ppermute | solution.py:607
  256.7 2.8 collective-permute-done.36.s2
  260.8 3.6 %mixer_sum.1 = (bf16[288,512]{1,0:T(8,128)(2,1)}, bf16[288,512]{1,0:T(8,128)(2,1)}, bf16[288,512]{1,0:T(8,128)(2,1)}, bf16[288,512]{1,0:T(8,128)(2,1)}) custom-call(s32[6]{0:T(128)} %pad_add_fusion.refs_0_.meta, bf16[2,1024,256]{2,1,0:T(8,128)(2,1)} %get-tuple-element.188.keep_ref, bf16[2,1024,256]{2,1,0:T(8,128)(2,1)} %copy-done.14, ...), custom_call_target="tpu_custom_call" | custom-call | flops 12074999808 | bytes 1000000 | tf_op jit(solution)/shard_map/mixer_sum/pallas_call | solution.py:588
  271.3 7.5 %collective-permute-done.40.refs_0_ = bf16[288,512]{1,0:T(8,128)(2,1)S(1)} collective-permute-done((bf16[288,512]{1,0:T(8,128)(2,1)S(1)}, bf16[288,512]{1,0:T(8,128)(2,1)S(1)}, u32[]{:S(2)}, u32[]{:S(2)}) %collective-permute-start.40) | collective-permute-done | bytes 294944 | tf_op jit(solution)/shard_map/ppermute | solution.py:855
  278.9 10.8 %collective-permute-done.41.refs_1_ = bf16[288,512]{1,0:T(8,128)(2,1)S(1)} collective-permute-done((bf16[288,512]{1,0:T(8,128)(2,1)S(1)}, bf16[288,512]{1,0:T(8,128)(2,1)S(1)}, u32[]{:S(2)}, u32[]{:S(2)}) %collective-permute-start.41) | collective-permute-done | bytes 294944 | tf_op jit(solution)/shard_map/ppermute | solution.py:855
  290.5 2.8 mixer_total.1
  299.8 4.0 %collective-permute-done.47.p3 = bf16[256,512]{1,0:T(8,128)(2,1)S(1)} collective-permute-done((bf16[256,512]{1,0:T(8,128)(2,1)}, bf16[256,512]{1,0:T(8,128)(2,1)S(1)}, u32[]{:S(2)}, u32[]{:S(2)}) %collective-permute-start.47) | collective-permute-done | bytes 262176 | tf_op jit(solution)/shard_map/ppermute | solution.py:607
  303.8 2.6 collective-permute-done.46.p2
  307.7 2.9 mixer_whole.1
  310.6 4.0 %gate_up_whole.1 = (f32[2,256,1408]{2,1,0:T(8,128)}, f32[1408,256]{1,0:T(8,128)}) custom-call(bf16[4,256,768]{2,1,0:T(8,128)(2,1)} %bitcast.71, bf16[704,256]{1,0:T(8,128)(2,1)} %copy-done.11, bf16[704,256]{1,0:T(8,128)(2,1)} %copy-done.31, bf16[704,256]{1,0:T(8,128)(2,1)} %copy-done.10, bf16[704,256]{1,0:T(8,128)(2,1)} %copy-done.30), custom_call_target="tpu_custom_call" | custom-call | flops 11384999936 | bytes 1000000 | tf_op jit(solution)/shard_map/gate_up_whole/pallas_call | solution.py:588
  (250 shorter events, 84.0 us)
Async XLA Ops:
  7.2 86.3 %all-gather.9.cloned.1.call-start = ((), (), s32[]{:S(2)}) async-start(), calls=%async_computation.5 | async-start | bytes 1966080 | tf_op jit(solution)/shard_map/all_gather | solution.py:655
  11.0 124.6 %all-gather.7.cloned.1.call-start = ((), (), s32[]{:S(2)}) async-start(), calls=%async_computation.2 | async-start | bytes 3604480 | tf_op jit(solution)/shard_map/all_gather | solution.py:657
  42.6 27.0 %collective-permute-start.7 = (bf16[256,128]{1,0:T(8,128)(2,1)S(1)}, bf16[256,128]{1,0:T(8,128)(2,1)S(1)}, u32[]{:S(2)}, u32[]{:S(2)}) collective-permute-start(bf16[256,128]{1,0:T(8,128)(2,1)S(1)} %dynamic-slice_bitcast_fusion), channel_id=1, source_target_pairs={{0,24},{8,0},{16,8},{24,16},{1,25},{9,1},{17,9},{25,17},{2,26},{10... | collective-permute-start | bytes 196616 | tf_op jit(solution)/shard_map/ppermute | solution.py:614
  47.1 22.6 %collective-permute-start.6 = (bf16[256,128]{1,0:T(8,128)(2,1)S(1)}, bf16[256,128]{1,0:T(8,128)(2,1)S(1)}, u32[]{:S(2)}, u32[]{:S(2)}) collective-permute-start(bf16[256,128]{1,0:T(8,128)(2,1)S(1)} %dynamic-slice_bitcast_fusion), channel_id=1, source_target_pairs={{0,16},{8,24},{16,0},{24,8},{1,17},{9,25},{17,1},{25,9},{2,18},{10... | collective-permute-start | bytes 196616 | tf_op jit(solution)/shard_map/ppermute | solution.py:614
  48.4 14.9 %collective-permute-start.1 = (bf16[3,800,128]{2,1,0:T(8,128)(2,1)S(1)}, bf16[3,800,128]{2,1,0:T(8,128)(2,1)S(1)}, u32[]{:S(2)}, u32[]{:S(2)}) collective-permute-start(bf16[3,800,128]{2,1,0:T(8,128)(2,1)S(1)} %pad_maximum_fusion.2), channel_id=1, source_target_pairs={{0,2},{2,0},{4,6},{6,4},{1,3},{3,1},{5,7},{7,5},{8,10},{10,8},{12,... | collective-permute-start | bytes 1843208 | tf_op jit(solution)/shard_map/ppermute | solution.py:607
  49.9 17.8 %collective-permute-start = (bf16[8,1024]{1,0:T(8,128)(2,1)S(1)}, bf16[8,1024]{1,0:T(8,128)(2,1)S(1)}, u32[]{:S(2)}, u32[]{:S(2)}) collective-permute-start(bf16[8,1024]{1,0:T(8,128)(2,1)S(1)} %slice.63), channel_id=1, source_target_pairs={{0,2},{2,4},{4,6},{1,3},{3,5},{5,7},{8,10},{10,12},{12,14},{9,11},... | collective-permute-start | bytes 49160 | tf_op jit(solution)/shard_map/ppermute | solution.py:603
  52.4 172.4 %reduce-scatter.3.cloned.1.call-start = ((), (), s32[]{:S(2)}) async-start(), calls=%async_computation.3 | async-start | bytes 3604480 | tf_op jit(solution)/shard_map/reduce_scatter | solution.py:784
  59.9 14.3 %collective-permute-start.4 = (bf16[3,416,128]{2,1,0:T(8,128)(2,1)S(1)}, bf16[3,416,128]{2,1,0:T(8,128)(2,1)}, u32[]{:S(2)}, u32[]{:S(2)}) collective-permute-start(bf16[3,416,128]{2,1,0:T(8,128)(2,1)S(1)} %slice.89), channel_id=1, source_target_pairs={{0,2},{2,0},{4,6},{6,4},{1,3},{3,1},{5,7},{7,5},{8,10},{10,8},{12,... | collective-permute-start | bytes 958472 | tf_op jit(solution)/shard_map/ppermute | solution.py:607
  74.3 18.6 %collective-permute-start.10 = (bf16[3,256,128]{2,1,0:T(8,128)(2,1)S(1)}, bf16[3,256,128]{2,1,0:T(8,128)(2,1)S(1)}, u32[]{:S(2)}, u32[]{:S(2)}) collective-permute-start(bf16[3,256,128]{2,1,0:T(8,128)(2,1)S(1)} %constant_dynamic-update-slice_fusion.refs_5_), channel_id=1, source_target_pairs={{0,6},{2,4},{4,2},{6,0},{1,7},{3,5},{5,3},{7,1},{8,14},{10,12},{12... | collective-permute-start | bytes 589832 | tf_op jit(solution)/shard_map/ppermute | solution.py:607
  77.4 17.6 %collective-permute-start.9 = (bf16[3,256,128]{2,1,0:T(8,128)(2,1)S(1)}, bf16[3,256,128]{2,1,0:T(8,128)(2,1)}, u32[]{:S(2)}, u32[]{:S(2)}) collective-permute-start(bf16[3,256,128]{2,1,0:T(8,128)(2,1)S(1)} %constant_dynamic-update-slice_fusion.refs_5_), channel_id=1, source_target_pairs={{0,4},{2,6},{4,0},{6,2},{1,5},{3,7},{5,1},{7,3},{8,12},{10,14},{12... | collective-permute-start | bytes 589832 | tf_op jit(solution)/shard_map/ppermute | solution.py:607
  77.4 19.2 %collective-permute-start.8 = (bf16[3,256,128]{2,1,0:T(8,128)(2,1)S(1)}, bf16[3,256,128]{2,1,0:T(8,128)(2,1)}, u32[]{:S(2)}, u32[]{:S(2)}) collective-permute-start(bf16[3,256,128]{2,1,0:T(8,128)(2,1)S(1)} %constant_dynamic-update-slice_fusion.refs_5_), channel_id=1, source_target_pairs={{0,2},{2,0},{4,6},{6,4},{1,3},{3,1},{5,7},{7,5},{8,10},{10,8},{12,... | collective-permute-start | bytes 589832 | tf_op jit(solution)/shard_map/ppermute | solution.py:607
  95.0 29.3 %collective-permute-start.16 = (bf16[3,256,768]{2,1,0:T(8,128)(2,1)S(1)}, bf16[3,256,768]{2,1,0:T(8,128)(2,1)S(1)}, u32[]{:S(2)}, u32[]{:S(2)}) collective-permute-start(bf16[3,256,768]{2,1,0:T(8,128)(2,1)S(1)} %pad_maximum_fusion.1), channel_id=1, source_target_pairs={{0,4},{2,6},{4,0},{6,2},{1,5},{3,7},{5,1},{7,3},{8,12},{10,14},{12... | collective-permute-start | bytes 3538952 | tf_op jit(solution)/shard_map/ppermute | solution.py:607
  96.7 27.7 %collective-permute-start.15 = (bf16[3,256,768]{2,1,0:T(8,128)(2,1)S(1)}, bf16[3,256,768]{2,1,0:T(8,128)(2,1)S(1)}, u32[]{:S(2)}, u32[]{:S(2)}) collective-permute-start(bf16[3,256,768]{2,1,0:T(8,128)(2,1)S(1)} %pad_maximum_fusion.1), channel_id=1, source_target_pairs={{0,2},{2,0},{4,6},{6,4},{1,3},{3,1},{5,7},{7,5},{8,10},{10,8},{12,... | collective-permute-start | bytes 3538952 | tf_op jit(solution)/shard_map/ppermute | solution.py:607
  113.3 14.9 %collective-permute-start.14 = (f32[256,1024]{1,0:T(8,128)}, f32[256,1024]{1,0:T(8,128)S(1)}, u32[]{:S(2)}, u32[]{:S(2)}) collective-permute-start(f32[256,1024]{1,0:T(8,128)} %get-tuple-element.130.refs_2_), channel_id=1, source_target_pairs={{0,1},{1,0},{2,3},{3,2},{4,5},{5,4},{6,7},{7,6},{8,9},{9,8},{10,11... | collective-permute-start | bytes 3145736 | tf_op jit(solution)/shard_map/ppermute | solution.py:607
  148.0 25.5 %collective-permute-start.23 = (bf16[1024,384]{1,0:T(8,128)(2,1)}, bf16[1024,384]{1,0:T(8,128)(2,1)S(1)}, u32[]{:S(2)}, u32[]{:S(2)}) collective-permute-start(bf16[1024,384]{1,0:T(8,128)(2,1)} %get-tuple-element.152), channel_id=1, source_target_pairs={{0,4},{2,6},{4,0},{6,2},{1,5},{3,7},{5,1},{7,3},{8,12},{10,14},{12... | collective-permute-start | bytes 2359304 | tf_op jit(solution)/shard_map/ppermute | solution.py:607
  150.7 20.7 %collective-permute-start.24 = (bf16[1024,384]{1,0:T(8,128)(2,1)}, bf16[1024,384]{1,0:T(8,128)(2,1)S(1)}, u32[]{:S(2)}, u32[]{:S(2)}) collective-permute-start(bf16[1024,384]{1,0:T(8,128)(2,1)} %get-tuple-element.154), channel_id=1, source_target_pairs={{0,2},{2,0},{4,6},{6,4},{1,3},{3,1},{5,7},{7,5},{8,10},{10,8},{12,... | collective-permute-start | bytes 2359304 | tf_op jit(solution)/shard_map/ppermute | solution.py:607
  171.4 93.1 %reduce-scatter.5.cloned.1.call-start = ((), (), s32[]{:S(2)}) async-start(), calls=%async_computation.4 | async-start | bytes 1966080 | tf_op jit(solution)/shard_map/reduce_scatter | solution.py:831
  171.4 31.3 %collective-permute-start.29 = (bf16[1024,384]{1,0:T(8,128)(2,1)}, bf16[1024,384]{1,0:T(8,128)(2,1)}, u32[]{:S(2)}, u32[]{:S(2)}) collective-permute-start(bf16[1024,384]{1,0:T(8,128)(2,1)} %get-tuple-element.175), channel_id=1, source_target_pairs={{0,2},{2,0},{4,6},{6,4},{1,3},{3,1},{5,7},{7,5},{8,10},{10,8},{12,... | collective-permute-start | bytes 2359304 | tf_op jit(solution)/shard_map/ppermute | solution.py:607
  173.4 30.2 %collective-permute-start.30 = (bf16[1024,384]{1,0:T(8,128)(2,1)}, bf16[1024,384]{1,0:T(8,128)(2,1)}, u32[]{:S(2)}, u32[]{:S(2)}) collective-permute-start(bf16[1024,384]{1,0:T(8,128)(2,1)} %get-tuple-element.176), channel_id=1, source_target_pairs={{0,4},{2,6},{4,0},{6,2},{1,5},{3,7},{5,1},{7,3},{8,12},{10,14},{12... | collective-permute-start | bytes 2359304 | tf_op jit(solution)/shard_map/ppermute | solution.py:607
  177.4 33.1 %collective-permute-start.31 = (bf16[1024,384]{1,0:T(8,128)(2,1)}, bf16[1024,384]{1,0:T(8,128)(2,1)}, u32[]{:S(2)}, u32[]{:S(2)}) collective-permute-start(bf16[1024,384]{1,0:T(8,128)(2,1)} %add_convert_fusion.1), channel_id=1, source_target_pairs={{0,2},{2,0},{4,6},{6,4},{1,3},{3,1},{5,7},{7,5},{8,10},{10,8},{12,... | collective-permute-start | bytes 2359304 | tf_op jit(solution)/shard_map/ppermute | solution.py:607
  178.6 32.6 %collective-permute-start.32 = (bf16[1024,384]{1,0:T(8,128)(2,1)}, bf16[1024,384]{1,0:T(8,128)(2,1)}, u32[]{:S(2)}, u32[]{:S(2)}) collective-permute-start(bf16[1024,384]{1,0:T(8,128)(2,1)} %add_convert_fusion), channel_id=1, source_target_pairs={{0,4},{2,6},{4,0},{6,2},{1,5},{3,7},{5,1},{7,3},{8,12},{10,14},{12... | collective-permute-start | bytes 2359304 | tf_op jit(solution)/shard_map/ppermute | solution.py:607
  201.4 31.1 %collective-permute-start.26 = (bf16[2,1024,256]{2,1,0:T(8,128)(2,1)}, bf16[2,1024,256]{2,1,0:T(8,128)(2,1)S(1)}, u32[]{:S(2)}, u32[]{:S(2)}) collective-permute-start(bf16[2,1024,256]{2,1,0:T(8,128)(2,1)} %get-tuple-element.171), channel_id=1, source_target_pairs={{0,2},{2,0},{4,6},{6,4},{1,3},{3,1},{5,7},{7,5},{8,10},{10,8},{12,... | collective-permute-start | bytes 3145736 | tf_op jit(solution)/shard_map/ppermute | solution.py:607
  202.7 30.5 %collective-permute-start.27 = (bf16[2,1024,256]{2,1,0:T(8,128)(2,1)}, bf16[2,1024,256]{2,1,0:T(8,128)(2,1)}, u32[]{:S(2)}, u32[]{:S(2)}) collective-permute-start(bf16[2,1024,256]{2,1,0:T(8,128)(2,1)} %get-tuple-element.172), channel_id=1, source_target_pairs={{0,4},{2,6},{4,0},{6,2},{1,5},{3,7},{5,1},{7,3},{8,12},{10,14},{12... | collective-permute-start | bytes 3145736 | tf_op jit(solution)/shard_map/ppermute | solution.py:607
  203.6 24.9 %collective-permute-start.25 = (f32[272,1024]{1,0:T(8,128)}, f32[272,1024]{1,0:T(8,128)}, u32[]{:S(2)}, u32[]{:S(2)}) collective-permute-start(f32[272,1024]{1,0:T(8,128)} %get-tuple-element.170.part_ref), channel_id=1, source_target_pairs={{0,1},{1,0},{2,3},{3,2},{4,5},{5,4},{6,7},{7,6},{8,9},{9,8},{10,11... | collective-permute-start | bytes 3342344 | tf_op jit(solution)/shard_map/ppermute | solution.py:607
  228.5 82.2 %all-gather.11.cloned.1.call-start = ((), (), s32[]{:S(2)}) async-start(), calls=%async_computation.6 | async-start | bytes 1966080 | tf_op jit(solution)/shard_map/all_gather | solution.py:852
  236.4 15.3 %collective-permute-start.34 = (bf16[1024,256]{1,0:T(8,128)(2,1)S(1)}, bf16[1024,256]{1,0:T(8,128)(2,1)S(1)}, u32[]{:S(2)}, u32[]{:S(2)}) collective-permute-start(bf16[1024,256]{1,0:T(8,128)(2,1)S(1)} %fusion.4), channel_id=1, source_target_pairs={{0,2},{2,0},{4,6},{6,4},{1,3},{3,1},{5,7},{7,5},{8,10},{10,8},{12,... | collective-permute-start | bytes 1572872 | tf_op jit(solution)/shard_map/ppermute | solution.py:607
  239.0 17.7 %collective-permute-start.33 = (bf16[1024,256]{1,0:T(8,128)(2,1)S(1)}, bf16[1024,256]{1,0:T(8,128)(2,1)S(1)}, u32[]{:S(2)}, u32[]{:S(2)}) collective-permute-start(bf16[1024,256]{1,0:T(8,128)(2,1)S(1)} %fusion.5), channel_id=1, source_target_pairs={{0,4},{2,6},{4,0},{6,2},{1,5},{3,7},{5,1},{7,3},{8,12},{10,14},{12... | collective-permute-start | bytes 1572872 | tf_op jit(solution)/shard_map/ppermute | solution.py:607
  244.2 15.3 %collective-permute-start.36 = (f32[32,1024]{1,0:T(8,128)}, f32[32,1024]{1,0:T(8,128)S(1)}, u32[]{:S(2)}, u32[]{:S(2)}) collective-permute-start(f32[32,1024]{1,0:T(8,128)} %get-tuple-element.195.s0), channel_id=1, source_target_pairs={{0,4},{2,6},{4,0},{6,2},{1,5},{3,7},{5,1},{7,3},{8,12},{10,14},{12... | collective-permute-start | bytes 393224 | tf_op jit(solution)/shard_map/ppermute | solution.py:607
  264.7 25.0 %collective-permute-start.44 = (bf16[704,256]{1,0:T(8,128)(2,1)S(1)}, bf16[704,256]{1,0:T(8,128)(2,1)S(1)}, u32[]{:S(2)}, u32[]{:S(2)}) collective-permute-start(bf16[704,256]{1,0:T(8,128)(2,1)S(1)} %get-tuple-element.223.e0), channel_id=1, source_target_pairs={{0,2},{2,0},{4,6},{6,4},{1,3},{3,1},{5,7},{7,5},{8,10},{10,8},{12,... | collective-permute-start | bytes 1081352 | tf_op jit(solution)/shard_map/ppermute | solution.py:607
  265.5 24.2 %collective-permute-start.43 = (bf16[704,256]{1,0:T(8,128)(2,1)S(1)}, bf16[704,256]{1,0:T(8,128)(2,1)S(1)}, u32[]{:S(2)}, u32[]{:S(2)}) collective-permute-start(bf16[704,256]{1,0:T(8,128)(2,1)S(1)} %get-tuple-element.221.d0), channel_id=1, source_target_pairs={{0,4},{2,6},{4,0},{6,2},{1,5},{3,7},{5,1},{7,3},{8,12},{10,14},{12... | collective-permute-start | bytes 1081352 | tf_op jit(solution)/shard_map/ppermute | solution.py:607
  267.4 22.3 %collective-permute-start.41 = (bf16[288,512]{1,0:T(8,128)(2,1)S(1)}, bf16[288,512]{1,0:T(8,128)(2,1)S(1)}, u32[]{:S(2)}, u32[]{:S(2)}) collective-permute-start(bf16[288,512]{1,0:T(8,128)(2,1)S(1)} %copy-done.34), channel_id=1, source_target_pairs={{0,16},{8,24},{16,0},{24,8},{1,17},{9,25},{17,1},{25,9},{2,18},{10... | collective-permute-start | bytes 884744 | tf_op jit(solution)/shard_map/ppermute | solution.py:855
  268.9 20.8 %collective-permute-start.42 = (bf16[288,512]{1,0:T(8,128)(2,1)S(1)}, bf16[288,512]{1,0:T(8,128)(2,1)S(1)}, u32[]{:S(2)}, u32[]{:S(2)}) collective-permute-start(bf16[288,512]{1,0:T(8,128)(2,1)S(1)} %copy-done.33), channel_id=1, source_target_pairs={{0,24},{8,0},{16,8},{24,16},{1,25},{9,1},{17,9},{25,17},{2,26},{10... | collective-permute-start | bytes 884744 | tf_op jit(solution)/shard_map/ppermute | solution.py:855
  (74 other events, 623.4 us)
Sparse Core Ops, SparseCore 0:
  11.1 51.3 all-gather.8
  64.1 59.2 all-gather.6
  171.5 53.2 reduce-scatter.2
  228.6 35.1 reduce-scatter.4
  265.5 30.4 all-gather.10

commit v4 on v3

--- a/solution.py
+++ b/solution.py
@@ -210,8 +210,8 @@
         lower = mm(jnp.concatenate([corner, bottom], -1), scaled[h])
         solved = jnp.concatenate([upper, lower])
         y_ref[h] = solved
-        ms_ref[h, 0] = (keep * (eye - mm(solved[:, :HD], keys[h], TN))).astype(BF16)
-        ms_ref[h, 1] = mm(last * solved[:, HD:], keys[h], TN).astype(BF16)
+        ms_ref[h, 0] = (keep * (eye - mm(solved[:, :HD], keys[h], TN, 1))).astype(BF16)
+        ms_ref[h, 1] = mm(last * solved[:, HD:], keys[h], TN, 1).astype(BF16)
 
 
 def output_kernel(*refs, lengths, sources, n_fsdp):
@@ -483,7 +483,7 @@
     bg_ref[...] = lax.dot_general(logits, xt, (((0,), (1,)), ((), ())), preferred_element_type=F32)[:PAD]
 
 
-def last_kernel(x_ref, gain_ref, part_ref, other_ref, rim_ref, gm_ref, sm_ref, st_ref, bg_ref, cg_ref, grad_ref, small_ref):
+def last_kernel(x_ref, gain_ref, part_ref, other_ref, rim_ref, gm_ref, sm_ref, st_ref, bg_ref, cg_ref, grad_ref, out_ref, small_ref):
     rows, width = x_ref.shape
     heads = cg_ref.shape[0]
     total = part_ref[...] + other_ref[...]
@@ -502,13 +502,14 @@
         small_ref[at : at + 3 * CONV, h * HD : (h + 1) * HD] = cg_ref[h, : 3 * CONV]
     at += 3 * CONV
     small_ref[at : at + 1, :HD] = total[rows + PAD : rows + PAD + 1, :HD]
+    out_ref[...] = small_ref[...].astype(BF16)
 
 
 def mixer_sum_kernel(meta, keep_ref, x_ref, y_ref, late_y_ref, late_x_ref, s0, s1, s2, s3, *outs, n_fsdp):
     width, half = x_ref.shape[1:]
     d_loc = width // n_fsdp
     grouped = len(outs) < n_fsdp
-    small = (s0[...] + s1[...]) + (s2[...] + s3[...])
+    small = (s0[...].astype(F32) + s1[...].astype(F32)) + (s2[...].astype(F32) + s3[...].astype(F32))
     rows, lanes = iota((SMALL_ROWS, 2 * half), 0), iota((SMALL_ROWS, 2 * half), 1)
     stats = jnp.sum(small, -1, keepdims=True)
     high = stats.astype(BF16).astype(F32)
@@ -817,9 +818,10 @@
     input_grad, smalls = call(
         last_kernel,
         "input_back",
-        (sds(rows, width), sds(SMALL_ROWS, width)),
+        (sds(rows, width), sds(SMALL_ROWS, width, dtype=BF16)),
         [VMEM] * 10,
         (tokens, first_gain, in_part, in_other, rim, g_middle, sums, stats, beta_grad, conv_grad),
+        [pltpu.VMEM((SMALL_ROWS, width), F32)],
         gflops=1,
         mbytes=6,
     )

time: 328 us -> 328 us (level)
  transfers between devices with their start and end apart: 53 -> 53, of which waited for: 26 -> 27; matrix products, arithmetic and copies ran while one was open for 6% -> 6% of each run, Pallas kernels for 21% -> 21%
where the time goes in v4:
time: 328 us; the launch traced here: 322 us
  waiting for transfers between devices  104 us (32%)
  Pallas kernels  85.1 us (26%)
  starting transfers between devices  58.3 us (18%)
  blocking collectives  29.7 us (9%)
  local copies, waits for them, and re-layouts  17.2 us (5%)
  between operations  15 us (5%)
  other arithmetic  12.2 us (4%)
    pallas_call x11, Pallas kernels, call(): pl.pallas_call(body, name=name, in_specs=in_specs, out_specs=jax.tree.map...  85.1 us
    ppermute x40, waiting for transfers between devices, swapped(): lax.ppermute(value, axis, [(s, s ^ mask) for s in range(lax.axis_size(axi...  64.1 us
    ppermute x40, starting transfers between devices, swapped(): lax.ppermute(value, axis, [(s, s ^ mask) for s in range(lax.axis_size(axi...  44.6 us
    all_gather x1, blocking collectives, local(): packs = lax.all_gather(pack, 'fsdp', axis=0)  29.7 us
    ppermute x3, waiting for transfers between devices, local(): lax.ppermute(part, 'fsdp', turn)  18.3 us
    reduce_scatter x1, waiting for transfers between devices, local(): lax.psum_scatter(down_grad, 'fsdp', scatter_dimension=1, tiled=True)  13.9 us
    unnamed x115, local copies, waits for them, and re-layouts  9.28 us
  transfers between devices with their start and end apart: 53, of which 27 were waited for; matrix products, arithmetic and copies ran while one was open for 6% of the time, Pallas kernels for 21%

profile of v4, /device:TPU:0, one launch (start us, length us, event | category | flops | bytes accessed | tf_op | source)
XLA Modules:
  0.0 321.8 jit_solution(13905470288771542460)
XLA Ops:
  12.8 29.7 %all-gather = bf16[3200,128]{1,0:T(8,128)(2,1)S(1)} all-gather(bf16[800,128]{1,0:T(8,128)(2,1)S(1)} %pad_maximum_fusion.4), channel_id=2, replica_groups=mesh['fsdp'=4,'ctx'=4,'tp'=2] {'fsdp'}, dimensions={0}, use_global_device_ids=true | all-gather | bytes 1024000 | tf_op jit(solution)/shard_map/all_gather | solution.py:649
  42.6 4.4 %collective-permute-start.7 = (bf16[256,128]{1,0:T(8,128)(2,1)S(1)}, bf16[256,128]{1,0:T(8,128)(2,1)S(1)}, u32[]{:S(2)}, u32[]{:S(2)}) collective-permute-start(bf16[256,128]{1,0:T(8,128)(2,1)S(1)} %dynamic-slice_bitcast_fusion), channel_id=1, source_target_pairs={{0,24},{8,0},{16,8},{24,16},{1,25},{9,1},{17,9},{25,17},{2,26},{10... | collective-permute-start | bytes 196616 | tf_op jit(solution)/shard_map/ppermute | solution.py:615
  49.9 2.4 collective-permute-start
  53.2 6.7 %collective-permute-done.2.refs_8_ = bf16[3,800,128]{2,1,0:T(8,128)(2,1)S(1)} collective-permute-done((bf16[3,800,128]{2,1,0:T(8,128)(2,1)S(1)}, bf16[3,800,128]{2,1,0:T(8,128)(2,1)S(1)}, u32[]{:S(2)}, u32[]{:S(2)}) %collective-permute-start.2) | collective-permute-done | bytes 614432 | tf_op jit(solution)/shard_map/ppermute | solution.py:608
  69.6 4.6 %collective-permute-done.5 = bf16[256,128]{1,0:T(8,128)(2,1)S(1)} collective-permute-done((bf16[256,128]{1,0:T(8,128)(2,1)S(1)}, bf16[256,128]{1,0:T(8,128)(2,1)S(1)}, u32[]{:S(2)}, u32[]{:S(2)}) %collective-permute-start.5) | collective-permute-done | bytes 65568 | tf_op jit(solution)/shard_map/ppermute | solution.py:615
  74.3 3.1 collective-permute-start.10
  78.1 11.7 %delta_terms.1 = (bf16[4,3,1024,128]{3,2,1,0:T(8,128)(2,1)}, bf16[4,3,264,128]{3,2,1,0:T(8,128)(2,1)}, bf16[4,3,256,128]{3,2,1,0:T(8,128)(2,1)}, f32[4,256,256]{...) custom-call(s32[6]{0:T(128)} %pad_add_fusion.refs_0_.meta, ...), custom_call_target="tpu_custom_call" | custom-call | flops 124200001536 | bytes 1000000 | tf_op jit(solution)/shard_map/delta_terms/pallas_call | solution.py:589
  89.8 2.9 collective-permute-start.13
  100.2 3.8 %collective-permute-done.12.refs_10_.refs_5_ = bf16[4,2,128,128]{3,2,1,0:T(8,128)(2,1)S(1)} collective-permute-done((bf16[4,2,128,128]{3,2,1,0:T(8,128)(2,1)}, bf16[4,2,128,128]{3,2,1,0:T(8,128)(2,1)S(1)}, u32[]{:S(2)}, u32[]{:S(2)}) %collective-permute-start.12) | collective-permute-done | bytes 262176 | tf_op jit(solution)/shard_map/ppermute | solution.py:608
  106.7 6.5 %delta_outputs.1 = (bf16[4,1024,128]{2,1,0:T(8,128)(2,1)}, f32[4,256,128]{2,1,0:T(8,128)}, f32[4,256,128]{2,1,0:T(8,128)}, f32[4,128,128]{2,1,0:T(8,128)}, bf16[...) custom-call(s32[6]{0:T(128)} %pad_add_fusion.refs_0_.meta, f32[4,256,256]{2,1,0:T(8,128)} %get-tuple-element.124.refs_1_.y_ref.refs_10_, ...), custom_call_target="tpu_custom_call" | custom-call | flops 67275001856 | bytes 1000000 | tf_op jit(solution)/shard_map/delta_outputs/pallas_call | solution.py:589
  113.2 11.0 %collective-permute-done.16.refs_9_ = bf16[3,256,768]{2,1,0:T(8,128)(2,1)S(1)} collective-permute-done((bf16[3,256,768]{2,1,0:T(8,128)(2,1)S(1)}, bf16[3,256,768]{2,1,0:T(8,128)(2,1)S(1)}, u32[]{:S(2)}, u32[]{:S(2)}) %collective-permute-start.16) | collective-permute-done | bytes 1179680 | tf_op jit(solution)/shard_map/ppermute | solution.py:608
  125.4 2.5 collective-permute-start.17
  128.4 5.8 %collective-permute-done.18.refs_11_ = bf16[3,256,384]{2,1,0:T(8,128)(2,1)S(1)} collective-permute-done((bf16[3,256,384]{2,1,0:T(8,128)(2,1)S(1)}, bf16[3,256,384]{2,1,0:T(8,128)(2,1)S(1)}, u32[]{:S(2)}, u32[]{:S(2)}) %collective-permute-start.18) | collective-permute-done | bytes 589856 | tf_op jit(solution)/shard_map/ppermute | solution.py:608
  135.8 12.3 %mlp.1 = (f32[256,1024]{1,0:T(8,128)}, bf16[1024,256]{1,0:T(8,128)(2,1)}, bf16[1408,256]{1,0:T(8,128)(2,1)}, bf16[4,256,768]{2,1,0:T(8,128)(2,1)}, bf16[256,1024...) custom-call(s32[6]{0:T(128)} %pad_add_fusion.refs_0_.meta, ...), custom_call_target="tpu_custom_call" | custom-call | flops 42090000384 | bytes 1000000 | tf_op jit(solution)/shard_map/mlp/pallas_call | solution.py:589
  151.8 6.0 %mlp_grads.1 = (bf16[1024,384]{1,0:T(8,128)(2,1)}, bf16[1024,384]{1,0:T(8,128)(2,1)}, bf16[1024,384]{1,0:T(8,128)(2,1)}, bf16[1024,384]{1,0:T(8,128)(2,1)}, bf16...) custom-call(bf16[1024,256]{1,0:T(8,128)(2,1)} %get-tuple-element.134.nt_ref, ...), custom_call_target="tpu_custom_call" | custom-call | flops 22424999936 | bytes 1000000 | tf_op jit(solution)/shard_map/mlp_grads/pallas_call | solution.py:589
  157.8 9.7 %middle_back.1 = (bf16[256,1024]{1,0:T(8,128)(2,1)}, f32[256,1024]{1,0:T(8,128)}, bf16[4,1024,128]{2,1,0:T(8,128)(2,1)}, f32[4,256,128]{2,1,0:T(8,128)}, f32[4,2...) custom-call(s32[6]{0:T(128)} %pad_add_fusion.refs_0_.meta, ...), custom_call_target="tpu_custom_call" | custom-call | flops 16560000000 | bytes 1000000 | tf_op jit(solution)/shard_map/middle_back/pallas_call | solution.py:589
  179.2 22.0 %delta_back.1 = (bf16[2,1024,256]{2,1,0:T(8,128)(2,1)}, bf16[2,1024,256]{2,1,0:T(8,128)(2,1)}, bf16[2,1024,256]{2,1,0:T(8,128)(2,1)}, bf16[1024,256]{1,0:T(8,128...) custom-call(s32[6]{0:T(128)} %pad_add_fusion.refs_0_.meta, ...), custom_call_target="tpu_custom_call" | custom-call | flops 455399997440 | bytes 1000000 | tf_op jit(solution)/shard_map/delta_back/pallas_call | solution.py:589
  203.4 6.9 %collective-permute-done.31 = bf16[1024,384]{1,0:T(8,128)(2,1)} collective-permute-done((bf16[1024,384]{1,0:T(8,128)(2,1)}, bf16[1024,384]{1,0:T(8,128)(2,1)}, u32[]{:S(2)}, u32[]{:S(2)}) %collective-permute-start.31) | collective-permute-done | bytes 786464 | tf_op jit(solution)/shard_map/ppermute | solution.py:608
  211.0 13.9 %reduce-scatter.3.cloned.1.call-done = bf16[1408,256]{1,0:T(8,128)(2,1)} async-done(((bf16[1408,1024]{1,0:T(8,128)(2,1)}), bf16[1408,256]{1,0:T(8,128)(2,1)}) %reduce-scatter.3.cloned.1.call-update) | async-done | bytes 720912 | tf_op jit(solution)/shard_map/reduce_scatter | solution.py:785
  224.9 2.4 fusion.3
  236.6 2.4 collective-permute-start.34
  239.2 3.7 %input_back.1 = (f32[256,1024]{1,0:T(8,128)}, bf16[32,1024]{1,0:T(8,128)(2,1)}) custom-call(bf16[256,1024]{1,0:T(8,128)(2,1)} %x_ref.1, f32[1,1024]{1,0:T(1,128)} %bitcast.67, f32[272,1024]{1,0:T(8,128)} %get-tuple-element.170.part_ref, f32[272,1024]{1,0:T(8,128)} %collective-permute-done.25.other_ref, f32[8,1024]{1,0:T(8,128)} %copy-done.52, ...), custom_call_target="tpu_custom_call" | custom-call | flops 1264999936 | bytes 1000000 | tf_op jit(solution)/shard_map/input_back/pallas_call | solution.py:589
  246.5 4.6 %collective-permute-done.34.late_x_ref = bf16[1024,256]{1,0:T(8,128)(2,1)S(1)} collective-permute-done((bf16[1024,256]{1,0:T(8,128)(2,1)S(1)}, bf16[1024,256]{1,0:T(8,128)(2,1)S(1)}, u32[]{:S(2)}, u32[]{:S(2)}) %collective-permute-start.34) | collective-permute-done | bytes 524320 | tf_op jit(solution)/shard_map/ppermute | solution.py:608
  251.9 3.6 %collective-permute-done.33.late_y_ref = bf16[1024,256]{1,0:T(8,128)(2,1)S(1)} collective-permute-done((bf16[1024,256]{1,0:T(8,128)(2,1)S(1)}, bf16[1024,256]{1,0:T(8,128)(2,1)S(1)}, u32[]{:S(2)}, u32[]{:S(2)}) %collective-permute-start.33) | collective-permute-done | bytes 524320 | tf_op jit(solution)/shard_map/ppermute | solution.py:608
  258.1 3.5 %mixer_sum.1 = (bf16[288,512]{1,0:T(8,128)(2,1)}, bf16[288,512]{1,0:T(8,128)(2,1)}, bf16[288,512]{1,0:T(8,128)(2,1)}, bf16[288,512]{1,0:T(8,128)(2,1)}) custom-call(s32[6]{0:T(128)} %pad_add_fusion.refs_0_.meta, bf16[2,1024,256]{2,1,0:T(8,128)(2,1)} %get-tuple-element.188.keep_ref, bf16[2,1024,256]{2,1,0:T(8,128)(2,1)} %copy-done.14, ...), custom_call_target="tpu_custom_call" | custom-call | flops 12074999808 | bytes 1000000 | tf_op jit(solution)/shard_map/mixer_sum/pallas_call | solution.py:589
  271.5 7.5 %collective-permute-done.40.refs_0_ = bf16[288,512]{1,0:T(8,128)(2,1)S(1)} collective-permute-done((bf16[288,512]{1,0:T(8,128)(2,1)S(1)}, bf16[288,512]{1,0:T(8,128)(2,1)S(1)}, u32[]{:S(2)}, u32[]{:S(2)}) %collective-permute-start.40) | collective-permute-done | bytes 294944 | tf_op jit(solution)/shard_map/ppermute | solution.py:857
  279.0 10.8 %collective-permute-done.41.refs_1_ = bf16[288,512]{1,0:T(8,128)(2,1)S(1)} collective-permute-done((bf16[288,512]{1,0:T(8,128)(2,1)S(1)}, bf16[288,512]{1,0:T(8,128)(2,1)S(1)}, u32[]{:S(2)}, u32[]{:S(2)}) %collective-permute-start.41) | collective-permute-done | bytes 294944 | tf_op jit(solution)/shard_map/ppermute | solution.py:857
  290.7 2.8 mixer_total.1
  299.9 4.0 %collective-permute-done.47.p3 = bf16[256,512]{1,0:T(8,128)(2,1)S(1)} collective-permute-done((bf16[256,512]{1,0:T(8,128)(2,1)}, bf16[256,512]{1,0:T(8,128)(2,1)S(1)}, u32[]{:S(2)}, u32[]{:S(2)}) %collective-permute-start.47) | collective-permute-done | bytes 262176 | tf_op jit(solution)/shard_map/ppermute | solution.py:608
  303.9 2.6 collective-permute-done.46.p2
  307.9 2.9 mixer_whole.1
  310.8 4.0 %gate_up_whole.1 = (f32[2,256,1408]{2,1,0:T(8,128)}, f32[1408,256]{1,0:T(8,128)}) custom-call(bf16[4,256,768]{2,1,0:T(8,128)(2,1)} %bitcast.71, bf16[704,256]{1,0:T(8,128)(2,1)} %copy-done.11, bf16[704,256]{1,0:T(8,128)(2,1)} %copy-done.31, bf16[704,256]{1,0:T(8,128)(2,1)} %copy-done.10, bf16[704,256]{1,0:T(8,128)(2,1)} %copy-done.30), custom_call_target="tpu_custom_call" | custom-call | flops 11384999936 | bytes 1000000 | tf_op jit(solution)/shard_map/gate_up_whole/pallas_call | solution.py:589
  (250 shorter events, 86.1 us)
Async XLA Ops:
  7.2 86.2 %all-gather.9.cloned.1.call-start = ((), (), s32[]{:S(2)}) async-start(), calls=%async_computation.5 | async-start | bytes 1966080 | tf_op jit(solution)/shard_map/all_gather | solution.py:656
  11.0 124.8 %all-gather.7.cloned.1.call-start = ((), (), s32[]{:S(2)}) async-start(), calls=%async_computation.2 | async-start | bytes 3604480 | tf_op jit(solution)/shard_map/all_gather | solution.py:658
  42.6 27.0 %collective-permute-start.7 = (bf16[256,128]{1,0:T(8,128)(2,1)S(1)}, bf16[256,128]{1,0:T(8,128)(2,1)S(1)}, u32[]{:S(2)}, u32[]{:S(2)}) collective-permute-start(bf16[256,128]{1,0:T(8,128)(2,1)S(1)} %dynamic-slice_bitcast_fusion), channel_id=1, source_target_pairs={{0,24},{8,0},{16,8},{24,16},{1,25},{9,1},{17,9},{25,17},{2,26},{10... | collective-permute-start | bytes 196616 | tf_op jit(solution)/shard_map/ppermute | solution.py:615
  47.1 22.6 %collective-permute-start.6 = (bf16[256,128]{1,0:T(8,128)(2,1)S(1)}, bf16[256,128]{1,0:T(8,128)(2,1)S(1)}, u32[]{:S(2)}, u32[]{:S(2)}) collective-permute-start(bf16[256,128]{1,0:T(8,128)(2,1)S(1)} %dynamic-slice_bitcast_fusion), channel_id=1, source_target_pairs={{0,16},{8,24},{16,0},{24,8},{1,17},{9,25},{17,1},{25,9},{2,18},{10... | collective-permute-start | bytes 196616 | tf_op jit(solution)/shard_map/ppermute | solution.py:615
  48.4 14.9 %collective-permute-start.1 = (bf16[3,800,128]{2,1,0:T(8,128)(2,1)S(1)}, bf16[3,800,128]{2,1,0:T(8,128)(2,1)S(1)}, u32[]{:S(2)}, u32[]{:S(2)}) collective-permute-start(bf16[3,800,128]{2,1,0:T(8,128)(2,1)S(1)} %pad_maximum_fusion.2), channel_id=1, source_target_pairs={{0,2},{2,0},{4,6},{6,4},{1,3},{3,1},{5,7},{7,5},{8,10},{10,8},{12,... | collective-permute-start | bytes 1843208 | tf_op jit(solution)/shard_map/ppermute | solution.py:608
  49.9 17.8 %collective-permute-start = (bf16[8,1024]{1,0:T(8,128)(2,1)S(1)}, bf16[8,1024]{1,0:T(8,128)(2,1)S(1)}, u32[]{:S(2)}, u32[]{:S(2)}) collective-permute-start(bf16[8,1024]{1,0:T(8,128)(2,1)S(1)} %slice.63), channel_id=1, source_target_pairs={{0,2},{2,4},{4,6},{1,3},{3,5},{5,7},{8,10},{10,12},{12,14},{9,11},... | collective-permute-start | bytes 49160 | tf_op jit(solution)/shard_map/ppermute | solution.py:604
  52.4 172.5 %reduce-scatter.3.cloned.1.call-start = ((), (), s32[]{:S(2)}) async-start(), calls=%async_computation.3 | async-start | bytes 3604480 | tf_op jit(solution)/shard_map/reduce_scatter | solution.py:785
  59.9 14.3 %collective-permute-start.4 = (bf16[3,416,128]{2,1,0:T(8,128)(2,1)S(1)}, bf16[3,416,128]{2,1,0:T(8,128)(2,1)}, u32[]{:S(2)}, u32[]{:S(2)}) collective-permute-start(bf16[3,416,128]{2,1,0:T(8,128)(2,1)S(1)} %slice.89), channel_id=1, source_target_pairs={{0,2},{2,0},{4,6},{6,4},{1,3},{3,1},{5,7},{7,5},{8,10},{10,8},{12,... | collective-permute-start | bytes 958472 | tf_op jit(solution)/shard_map/ppermute | solution.py:608
  74.3 18.4 %collective-permute-start.10 = (bf16[3,256,128]{2,1,0:T(8,128)(2,1)S(1)}, bf16[3,256,128]{2,1,0:T(8,128)(2,1)S(1)}, u32[]{:S(2)}, u32[]{:S(2)}) collective-permute-start(bf16[3,256,128]{2,1,0:T(8,128)(2,1)S(1)} %constant_dynamic-update-slice_fusion.refs_5_), channel_id=1, source_target_pairs={{0,6},{2,4},{4,2},{6,0},{1,7},{3,5},{5,3},{7,1},{8,14},{10,12},{12... | collective-permute-start | bytes 589832 | tf_op jit(solution)/shard_map/ppermute | solution.py:608
  77.4 17.4 %collective-permute-start.9 = (bf16[3,256,128]{2,1,0:T(8,128)(2,1)S(1)}, bf16[3,256,128]{2,1,0:T(8,128)(2,1)}, u32[]{:S(2)}, u32[]{:S(2)}) collective-permute-start(bf16[3,256,128]{2,1,0:T(8,128)(2,1)S(1)} %constant_dynamic-update-slice_fusion.refs_5_), channel_id=1, source_target_pairs={{0,4},{2,6},{4,0},{6,2},{1,5},{3,7},{5,1},{7,3},{8,12},{10,14},{12... | collective-permute-start | bytes 589832 | tf_op jit(solution)/shard_map/ppermute | solution.py:608
  77.4 19.1 %collective-permute-start.8 = (bf16[3,256,128]{2,1,0:T(8,128)(2,1)S(1)}, bf16[3,256,128]{2,1,0:T(8,128)(2,1)}, u32[]{:S(2)}, u32[]{:S(2)}) collective-permute-start(bf16[3,256,128]{2,1,0:T(8,128)(2,1)S(1)} %constant_dynamic-update-slice_fusion.refs_5_), channel_id=1, source_target_pairs={{0,2},{2,0},{4,6},{6,4},{1,3},{3,1},{5,7},{7,5},{8,10},{10,8},{12,... | collective-permute-start | bytes 589832 | tf_op jit(solution)/shard_map/ppermute | solution.py:608
  92.7 13.2 %collective-permute-start.11 = (bf16[4,2,128,128]{3,2,1,0:T(8,128)(2,1)}, bf16[4,2,128,128]{3,2,1,0:T(8,128)(2,1)S(1)}, u32[]{:S(2)}, u32[]{:S(2)}) collective-permute-start(bf16[4,2,128,128]{3,2,1,0:T(8,128)(2,1)} %get-tuple-element.129), channel_id=1, source_target_pairs={{0,2},{2,0},{4,6},{6,4},{1,3},{3,1},{5,7},{7,5},{8,10},{10,8},{12,... | collective-permute-start | bytes 786440 | tf_op jit(solution)/shard_map/ppermute | solution.py:608
  94.8 29.4 %collective-permute-start.16 = (bf16[3,256,768]{2,1,0:T(8,128)(2,1)S(1)}, bf16[3,256,768]{2,1,0:T(8,128)(2,1)S(1)}, u32[]{:S(2)}, u32[]{:S(2)}) collective-permute-start(bf16[3,256,768]{2,1,0:T(8,128)(2,1)S(1)} %pad_maximum_fusion.1), channel_id=1, source_target_pairs={{0,4},{2,6},{4,0},{6,2},{1,5},{3,7},{5,1},{7,3},{8,12},{10,14},{12... | collective-permute-start | bytes 3538952 | tf_op jit(solution)/shard_map/ppermute | solution.py:608
  96.5 27.7 %collective-permute-start.15 = (bf16[3,256,768]{2,1,0:T(8,128)(2,1)S(1)}, bf16[3,256,768]{2,1,0:T(8,128)(2,1)S(1)}, u32[]{:S(2)}, u32[]{:S(2)}) collective-permute-start(bf16[3,256,768]{2,1,0:T(8,128)(2,1)S(1)} %pad_maximum_fusion.1), channel_id=1, source_target_pairs={{0,2},{2,0},{4,6},{6,4},{1,3},{3,1},{5,7},{7,5},{8,10},{10,8},{12,... | collective-permute-start | bytes 3538952 | tf_op jit(solution)/shard_map/ppermute | solution.py:608
  113.1 15.3 %collective-permute-start.14 = (f32[256,1024]{1,0:T(8,128)}, f32[256,1024]{1,0:T(8,128)S(1)}, u32[]{:S(2)}, u32[]{:S(2)}) collective-permute-start(f32[256,1024]{1,0:T(8,128)} %get-tuple-element.130.refs_2_), channel_id=1, source_target_pairs={{0,1},{1,0},{2,3},{3,2},{4,5},{5,4},{6,7},{7,6},{8,9},{9,8},{10,11... | collective-permute-start | bytes 3145736 | tf_op jit(solution)/shard_map/ppermute | solution.py:608
  148.1 25.1 %collective-permute-start.23 = (bf16[1024,384]{1,0:T(8,128)(2,1)}, bf16[1024,384]{1,0:T(8,128)(2,1)S(1)}, u32[]{:S(2)}, u32[]{:S(2)}) collective-permute-start(bf16[1024,384]{1,0:T(8,128)(2,1)} %get-tuple-element.152), channel_id=1, source_target_pairs={{0,4},{2,6},{4,0},{6,2},{1,5},{3,7},{5,1},{7,3},{8,12},{10,14},{12... | collective-permute-start | bytes 2359304 | tf_op jit(solution)/shard_map/ppermute | solution.py:608
  150.5 20.7 %collective-permute-start.24 = (bf16[1024,384]{1,0:T(8,128)(2,1)}, bf16[1024,384]{1,0:T(8,128)(2,1)S(1)}, u32[]{:S(2)}, u32[]{:S(2)}) collective-permute-start(bf16[1024,384]{1,0:T(8,128)(2,1)} %get-tuple-element.154), channel_id=1, source_target_pairs={{0,2},{2,0},{4,6},{6,4},{1,3},{3,1},{5,7},{7,5},{8,10},{10,8},{12,... | collective-permute-start | bytes 2359304 | tf_op jit(solution)/shard_map/ppermute | solution.py:608
  171.2 92.8 %reduce-scatter.5.cloned.1.call-start = ((), (), s32[]{:S(2)}) async-start(), calls=%async_computation.4 | async-start | bytes 1966080 | tf_op jit(solution)/shard_map/reduce_scatter | solution.py:833
  171.2 31.3 %collective-permute-start.29 = (bf16[1024,384]{1,0:T(8,128)(2,1)}, bf16[1024,384]{1,0:T(8,128)(2,1)}, u32[]{:S(2)}, u32[]{:S(2)}) collective-permute-start(bf16[1024,384]{1,0:T(8,128)(2,1)} %get-tuple-element.175), channel_id=1, source_target_pairs={{0,2},{2,0},{4,6},{6,4},{1,3},{3,1},{5,7},{7,5},{8,10},{10,8},{12,... | collective-permute-start | bytes 2359304 | tf_op jit(solution)/shard_map/ppermute | solution.py:608
  173.2 30.2 %collective-permute-start.30 = (bf16[1024,384]{1,0:T(8,128)(2,1)}, bf16[1024,384]{1,0:T(8,128)(2,1)}, u32[]{:S(2)}, u32[]{:S(2)}) collective-permute-start(bf16[1024,384]{1,0:T(8,128)(2,1)} %get-tuple-element.176), channel_id=1, source_target_pairs={{0,4},{2,6},{4,0},{6,2},{1,5},{3,7},{5,1},{7,3},{8,12},{10,14},{12... | collective-permute-start | bytes 2359304 | tf_op jit(solution)/shard_map/ppermute | solution.py:608
  177.2 33.1 %collective-permute-start.31 = (bf16[1024,384]{1,0:T(8,128)(2,1)}, bf16[1024,384]{1,0:T(8,128)(2,1)}, u32[]{:S(2)}, u32[]{:S(2)}) collective-permute-start(bf16[1024,384]{1,0:T(8,128)(2,1)} %add_convert_fusion.1), channel_id=1, source_target_pairs={{0,2},{2,0},{4,6},{6,4},{1,3},{3,1},{5,7},{7,5},{8,10},{10,8},{12,... | collective-permute-start | bytes 2359304 | tf_op jit(solution)/shard_map/ppermute | solution.py:608
  178.4 32.7 %collective-permute-start.32 = (bf16[1024,384]{1,0:T(8,128)(2,1)}, bf16[1024,384]{1,0:T(8,128)(2,1)}, u32[]{:S(2)}, u32[]{:S(2)}) collective-permute-start(bf16[1024,384]{1,0:T(8,128)(2,1)} %add_convert_fusion), channel_id=1, source_target_pairs={{0,4},{2,6},{4,0},{6,2},{1,5},{3,7},{5,1},{7,3},{8,12},{10,14},{12... | collective-permute-start | bytes 2359304 | tf_op jit(solution)/shard_map/ppermute | solution.py:608
  201.2 31.1 %collective-permute-start.26 = (bf16[2,1024,256]{2,1,0:T(8,128)(2,1)}, bf16[2,1024,256]{2,1,0:T(8,128)(2,1)S(1)}, u32[]{:S(2)}, u32[]{:S(2)}) collective-permute-start(bf16[2,1024,256]{2,1,0:T(8,128)(2,1)} %get-tuple-element.171), channel_id=1, source_target_pairs={{0,2},{2,0},{4,6},{6,4},{1,3},{3,1},{5,7},{7,5},{8,10},{10,8},{12,... | collective-permute-start | bytes 3145736 | tf_op jit(solution)/shard_map/ppermute | solution.py:608
  202.6 30.5 %collective-permute-start.27 = (bf16[2,1024,256]{2,1,0:T(8,128)(2,1)}, bf16[2,1024,256]{2,1,0:T(8,128)(2,1)}, u32[]{:S(2)}, u32[]{:S(2)}) collective-permute-start(bf16[2,1024,256]{2,1,0:T(8,128)(2,1)} %get-tuple-element.172), channel_id=1, source_target_pairs={{0,4},{2,6},{4,0},{6,2},{1,5},{3,7},{5,1},{7,3},{8,12},{10,14},{12... | collective-permute-start | bytes 3145736 | tf_op jit(solution)/shard_map/ppermute | solution.py:608
  203.4 25.3 %collective-permute-start.25 = (f32[272,1024]{1,0:T(8,128)}, f32[272,1024]{1,0:T(8,128)}, u32[]{:S(2)}, u32[]{:S(2)}) collective-permute-start(f32[272,1024]{1,0:T(8,128)} %get-tuple-element.170.part_ref), channel_id=1, source_target_pairs={{0,1},{1,0},{2,3},{3,2},{4,5},{5,4},{6,7},{7,6},{8,9},{9,8},{10,11... | collective-permute-start | bytes 3342344 | tf_op jit(solution)/shard_map/ppermute | solution.py:608
  228.6 82.2 %all-gather.11.cloned.1.call-start = ((), (), s32[]{:S(2)}) async-start(), calls=%async_computation.6 | async-start | bytes 1966080 | tf_op jit(solution)/shard_map/all_gather | solution.py:854
  236.6 14.5 %collective-permute-start.34 = (bf16[1024,256]{1,0:T(8,128)(2,1)S(1)}, bf16[1024,256]{1,0:T(8,128)(2,1)S(1)}, u32[]{:S(2)}, u32[]{:S(2)}) collective-permute-start(bf16[1024,256]{1,0:T(8,128)(2,1)S(1)} %fusion.4), channel_id=1, source_target_pairs={{0,2},{2,0},{4,6},{6,4},{1,3},{3,1},{5,7},{7,5},{8,10},{10,8},{12,... | collective-permute-start | bytes 1572872 | tf_op jit(solution)/shard_map/ppermute | solution.py:608
  239.1 16.3 %collective-permute-start.33 = (bf16[1024,256]{1,0:T(8,128)(2,1)S(1)}, bf16[1024,256]{1,0:T(8,128)(2,1)S(1)}, u32[]{:S(2)}, u32[]{:S(2)}) collective-permute-start(bf16[1024,256]{1,0:T(8,128)(2,1)S(1)} %fusion.5), channel_id=1, source_target_pairs={{0,4},{2,6},{4,0},{6,2},{1,5},{3,7},{5,1},{7,3},{8,12},{10,14},{12... | collective-permute-start | bytes 1572872 | tf_op jit(solution)/shard_map/ppermute | solution.py:608
  264.2 25.7 %collective-permute-start.44 = (bf16[704,256]{1,0:T(8,128)(2,1)S(1)}, bf16[704,256]{1,0:T(8,128)(2,1)S(1)}, u32[]{:S(2)}, u32[]{:S(2)}) collective-permute-start(bf16[704,256]{1,0:T(8,128)(2,1)S(1)} %get-tuple-element.223.e0), channel_id=1, source_target_pairs={{0,2},{2,0},{4,6},{6,4},{1,3},{3,1},{5,7},{7,5},{8,10},{10,8},{12,... | collective-permute-start | bytes 1081352 | tf_op jit(solution)/shard_map/ppermute | solution.py:608
  265.7 24.2 %collective-permute-start.43 = (bf16[704,256]{1,0:T(8,128)(2,1)S(1)}, bf16[704,256]{1,0:T(8,128)(2,1)S(1)}, u32[]{:S(2)}, u32[]{:S(2)}) collective-permute-start(bf16[704,256]{1,0:T(8,128)(2,1)S(1)} %get-tuple-element.221.d0), channel_id=1, source_target_pairs={{0,4},{2,6},{4,0},{6,2},{1,5},{3,7},{5,1},{7,3},{8,12},{10,14},{12... | collective-permute-start | bytes 1081352 | tf_op jit(solution)/shard_map/ppermute | solution.py:608
  267.6 22.3 %collective-permute-start.41 = (bf16[288,512]{1,0:T(8,128)(2,1)S(1)}, bf16[288,512]{1,0:T(8,128)(2,1)S(1)}, u32[]{:S(2)}, u32[]{:S(2)}) collective-permute-start(bf16[288,512]{1,0:T(8,128)(2,1)S(1)} %copy-done.34), channel_id=1, source_target_pairs={{0,16},{8,24},{16,0},{24,8},{1,17},{9,25},{17,1},{25,9},{2,18},{10... | collective-permute-start | bytes 884744 | tf_op jit(solution)/shard_map/ppermute | solution.py:857
  269.1 20.7 %collective-permute-start.42 = (bf16[288,512]{1,0:T(8,128)(2,1)S(1)}, bf16[288,512]{1,0:T(8,128)(2,1)S(1)}, u32[]{:S(2)}, u32[]{:S(2)}) collective-permute-start(bf16[288,512]{1,0:T(8,128)(2,1)S(1)} %copy-done.33), channel_id=1, source_target_pairs={{0,24},{8,0},{16,8},{24,16},{1,25},{9,1},{17,9},{25,17},{2,26},{10... | collective-permute-start | bytes 884744 | tf_op jit(solution)/shard_map/ppermute | solution.py:857
  (74 other events, 623.3 us)
Sparse Core Ops, SparseCore 0:
  11.1 51.3 all-gather.8
  64.1 59.2 all-gather.6
  171.3 53.5 reduce-scatter.2
  228.8 35.1 reduce-scatter.4
  265.6 30.4 all-gather.10
